TPU v7x, 512 devices: a whole 4x4x16 slice. The times are simulated.
512 devices in a mesh: seq: 64 (over y_lo, z, core), tensor: 8 (over x, y_hi).
Axes of the slice: x: 4, y: 4 (y_hi: 2, y_lo: 2; y = y_hi * 2 + y_lo), z: 16, core: 2. Of those that a mesh axis runs over, the one named last changes fastest.
Arguments:
- trunk: bfloat16 [2, 4096, 1536], P(None, 'seq', 'tensor'), may hold values from -12 to 12
- w_out: bfloat16 [1536, 1536], P('tensor', 'seq'), may hold values from -1 to 1
- gain_coarse: float32 [1536], replicated, may hold values from 0.1 to 1.9
- w_conv1: bfloat16 [5, 1536, 1536], P(None, 'seq', 'tensor'), may hold values from -0.0625 to 0.0625
- w_up: bfloat16 [1536, 2, 768], P('seq', None, 'tensor'), may hold values from -0.15625 to 0.15625
- skip: bfloat16 [2, 8192, 768], P(None, 'seq', 'tensor'), may hold values from -12 to 12
- gain_fine: float32 [768], replicated, may hold values from 0.1 to 1.9
- w_conv2: bfloat16 [5, 768, 768], P(None, 'seq', 'tensor'), may hold values from -0.09375 to 0.09375
- cotangent: bfloat16 [2, 8192, 768], P(None, 'seq', 'tensor'), may hold values from -6 to 6
Outputs:
- decoded: bfloat16 [2, 8192, 768], P(None, 'seq', 'tensor')
- skip_grad: bfloat16 [2, 8192, 768], P(None, 'seq', 'tensor')
- trunk_grad: bfloat16 [2, 4096, 1536], P(None, 'seq', 'tensor')
All inputs are finite; a program needn't handle non-finite values.
Results may differ from a plain program's by a relative error of at most 0.02.
Values may be sent and summed in bfloat16 or wider, within the bound.
No kernel may reach another device: no remote copies, remote signals or barrier semaphores. Data moves between devices by JAX's collectives and lax.ppermute only.
A program may use at most 64 MiB of HBM per device.

v0:
```python
import jax
import jax.numpy as jnp
from jax import lax
from jax.sharding import PartitionSpec as P

C_COARSE = 1536
C_FINE = 768


EPS = 1e-06


def extended(shard, sides, width):
    for axis, dim in sides:
        size, length = (lax.axis_size(axis), shard.shape[dim])
        up = [(i, (i + 1) % size) for i in range(size - 1)]
        down = [(j, i) for i, j in up]
        last = lax.slice_in_dim(shard, length - width, length, axis=dim)
        leading = lax.slice_in_dim(shard, 0, width, axis=dim)
        before = lax.ppermute(last, axis, up)
        after = lax.ppermute(leading, axis, down)
        shard = jnp.concatenate([before, shard, after], axis=dim)
    return shard


def matmul(left, right):
    return lax.dot_general(
        left, right, (((left.ndim - 1,), (0,)), ((), ())), preferred_element_type=jnp.float32
    )


def matmul_back(left, right):
    return lax.dot_general(
        left,
        right,
        (((left.ndim - 1,), (right.ndim - 1,)), ((), ())),
        preferred_element_type=jnp.float32,
    )


def activate(field, gain):
    scaled = field * lax.rsqrt(jnp.mean(field * field, axis=-1, keepdims=True) + EPS)
    return jax.nn.gelu(scaled * gain)


def widen(field):
    return extended(field, (("seq", 1),), 2)


def spread(field):
    return lax.all_gather(field, "tensor", axis=2, tiled=True)


def conv_rows(total, wide, piece):
    length = wide.shape[1] - 4
    for k in range(5):
        total = total + matmul(wide[:, k : k + length], piece[k])
    return total


def conv_back(wide_grad, piece):
    length = wide_grad.shape[1] - 4
    total = jnp.zeros((wide_grad.shape[0], length, piece.shape[1]), jnp.float32)
    for k in range(5):
        total = total + matmul_back(wide_grad[:, 4 - k : 4 - k + length], piece[k])
    return total


def norm_back(partial_grad, field_full, gain, rank, part):
    field = field_full.astype(jnp.float32)
    start = rank * part
    whole = lax.psum(partial_grad.astype(jnp.bfloat16), "tensor").astype(jnp.float32)

    def apply(value):
        return activate(value, gain)

    _, pull = jax.vjp(apply, field)
    return lax.dynamic_slice_in_dim(pull(whole)[0], start, part, 2)


def per_device(trunk, w_out, gain_coarse, w_conv1, w_up, skip, gain_fine, w_conv2, cotangent):
    rank = lax.axis_index("tensor")
    part_coarse = C_COARSE // lax.axis_size("tensor")
    part_fine = C_FINE // lax.axis_size("tensor")
    seqs = trunk.shape[0]
    slab = trunk.shape[1]
    out_w, up_w, conv2_w = (
        lax.all_gather(w_out, "seq", axis=1, tiled=True),
        lax.all_gather(w_up, "seq", axis=0, tiled=True),
        lax.all_gather(w_conv2, "seq", axis=1, tiled=True),
    )
    partial_proj = matmul(trunk, out_w)
    projected = lax.psum_scatter(
        partial_proj.astype(jnp.bfloat16), "tensor", scatter_dimension=2, tiled=True
    )
    projected_full = lax.all_gather(projected, "tensor", axis=2, tiled=True)
    act_coarse = activate(projected_full.astype(jnp.float32), gain_coarse).astype(jnp.bfloat16)
    coarse_wide = widen(act_coarse)
    empty_coarse = jnp.zeros((seqs, slab, part_coarse), jnp.float32)
    mixed_coarse = conv_rows(
        empty_coarse, coarse_wide, lax.all_gather(w_conv1, "seq", axis=1, tiled=True)
    )
    lifted = (projected.astype(jnp.float32) + mixed_coarse).astype(jnp.bfloat16)
    lifted_full = spread(lifted)
    upper = matmul(lifted_full, up_w).reshape(seqs, 2 * slab, part_fine)
    merged = (upper + skip.astype(jnp.float32)).astype(jnp.bfloat16)
    merged_full = spread(merged)
    act_fine = activate(merged_full.astype(jnp.float32), gain_fine).astype(jnp.bfloat16)
    fine_wide = widen(act_fine)
    empty_fine = jnp.zeros((seqs, 2 * slab, part_fine), jnp.float32)
    mixed_fine = conv_rows(empty_fine, fine_wide, conv2_w)
    decoded = (merged.astype(jnp.float32) + mixed_fine).astype(jnp.bfloat16)
    cot_wide = widen(cotangent)
    back_fine = conv_back(cot_wide, conv2_w)
    skip_grad = (
        cotangent.astype(jnp.float32)
        + norm_back(back_fine, merged_full, gain_fine, rank, part_fine)
    ).astype(jnp.bfloat16)
    folded = skip_grad.reshape(seqs, slab, 2 * part_fine)
    up_partial = matmul_back(folded, up_w.reshape(up_w.shape[0], 2 * part_fine))
    lifted_grad = lax.psum_scatter(
        up_partial.astype(jnp.bfloat16), "tensor", scatter_dimension=2, tiled=True
    )
    grad_wide = widen(lifted_grad)
    back_coarse = conv_back(grad_wide, lax.all_gather(w_conv1, "seq", axis=1, tiled=True))
    projected_grad = (
        lifted_grad.astype(jnp.float32)
        + norm_back(back_coarse, projected_full, gain_coarse, rank, part_coarse)
    ).astype(jnp.bfloat16)
    grad_full = spread(projected_grad)
    trunk_grad = matmul_back(grad_full, out_w).astype(jnp.bfloat16)
    return (decoded, skip_grad, trunk_grad)


def solution(mesh):
    in_specs = (
        P(None, "seq", "tensor"),
        P("tensor", "seq"),
        P(),
        P(None, "seq", "tensor"),
        P("seq", None, "tensor"),
        P(None, "seq", "tensor"),
        P(),
        P(None, "seq", "tensor"),
        P(None, "seq", "tensor"),
    )
    out_specs = (P(None, "seq", "tensor"), P(None, "seq", "tensor"), P(None, "seq", "tensor"))
    return jax.shard_map(
        per_device, mesh=mesh, in_specs=in_specs, out_specs=out_specs, check_vma=False
    )
```

profile of v0, /device:TPU:32, one launch (start us, length us, event | category | flops | bytes accessed | tf_op | source)
XLA Modules:
  0.0 605.8 jit_solution(13952073995251404903)
XLA Ops:
  8.1 69.1 %all_gather.25 = bf16[192,1536]{0,1:T(8,128)(2,1)S(1)} all-gather(bf16[192,24]{0,1:T(8,128)(2,1)} %param.10), channel_id=1, replica_groups=mesh['seq'=64,'tensor'=8] {'seq'}, dimensions={1}, use_global_device_ids=true | all-gather | bytes 599040 | tf_op jit(solution)/shard_map/all_gather | solution.py:88
  77.5 0.6 copy.66
  78.1 1.1 reshape.66
  79.9 0.7 fusion.111
  80.6 5.0 collective-permute-start.4
  85.6 1.9 collective-permute-start.5
  87.5 0.7 copy.58
  88.3 0.6 copy.46
  88.9 65.4 %all_gather.31 = bf16[5,768,96]{2,0,1:T(8,128)(2,1)S(1)} all-gather(bf16[5,12,96]{2,0,1:T(8,128)(2,1)S(1)} %copy.52), channel_id=1, replica_groups=mesh['seq'=64,'tensor'=8] {'seq'}, dimensions={1}, use_global_device_ids=true | all-gather | bytes 748800 | tf_op jit(solution)/shard_map/all_gather | solution.py:90
  154.3 1.4 fusion.107
  155.8 0.9 copy.76
  157.0 0.9 copy.75
  157.9 0.9 copy.79
  158.8 0.9 copy.78
  159.7 0.6 constant_dynamic-update-slice_fusion.1
  160.6 62.1 %all_gather.29 = bf16[1536,2,96]{2,0,1:T(8,128)(2,1)S(1)} all-gather(bf16[24,2,96]{2,0,1:T(8,128)(2,1)} %copy.46), channel_id=1, replica_groups=mesh['seq'=64,'tensor'=8] {'seq'}, dimensions={0}, use_global_device_ids=true | all-gather | bytes 599040 | tf_op jit(solution)/shard_map/all_gather | solution.py:89
  223.0 1.4 constant_dynamic-update-slice_fusion
  224.4 1.3 fusion.60
  225.7 1.3 fusion.69
  227.1 1.3 fusion.4
  228.3 1.9 fusion.5
  230.4 0.9 reshape.67
  231.3 37.2 %all_gather.26 = bf16[2,64,1536]{1,0,2:T(2,128)(2,1)S(1)} all-gather(bf16[2,64,192]{1,0,2:T(2,128)(2,1)S(1)} %bitcast.93), channel_id=1, replica_groups=mesh['seq'=64,'tensor'=8] {'tensor'}, dimensions={2}, use_global_device_ids=true | all-gather | bytes 442368 | tf_op jit(solution)/shard_map/all_gather | solution.py:96
  268.4 0.7 copy.67
  269.2 0.6 copy.39
  269.9 1.0 convert_element_type.67
  270.9 0.5 copy-done.13
  271.4 1.1 multiply_convert_fusion.1
  272.6 1.9 collective-permute-start
  274.5 3.6 collective-permute-start.1
  278.2 1.4 fusion.43
  279.6 1.4 fusion.41
  281.0 1.4 fusion.45
  282.5 1.4 fusion.6
  283.9 1.4 fusion.9
  285.5 35.9 %all_gather.28 = bf16[2,64,1536]{1,0,2:T(2,128)(2,1)S(1)} all-gather(bf16[2,64,192]{1,0,2:T(2,128)(2,1)S(1)} %copy.45), channel_id=1, replica_groups=mesh['seq'=64,'tensor'=8] {'tensor'}, dimensions={2}, use_global_device_ids=true | all-gather | bytes 442368 | tf_op jit(solution)/shard_map/all_gather | solution.py:51
  322.0 0.6 copy-done.7
  322.6 34.9 %all_gather.30 = bf16[2,128,768]{1,0,2:T(2,128)(2,1)S(1)} all-gather(bf16[2,128,96]{1,0,2:T(2,128)(2,1)S(1)} %copy.50), channel_id=1, replica_groups=mesh['seq'=64,'tensor'=8] {'tensor'}, dimensions={2}, use_global_device_ids=true | all-gather | bytes 442368 | tf_op jit(solution)/shard_map/all_gather | solution.py:51
  358.2 0.6 fusion.90
  358.8 1.9 multiply_reduce_fusion.1
  360.7 0.7 multiply_multiply_fusion.7
  361.4 1.0 fusion.75
  363.4 0.6 copy.68
  363.9 1.1 reshape.68
  365.2 1.9 collective-permute-start.2
  367.4 1.6 copy.62
  368.9 3.6 collective-permute-start.3
  372.6 1.2 fusion.56
  373.8 1.2 fusion.10
  375.0 69.0 %reduce-scatter.9.cloned.1.call-done = bf16[192,128]{1,0:T(8,128)(2,1)} async-done(((bf16[1536,128]{1,0:T(8,128)(2,1)}), bf16[192,128]{1,0:T(8,128)(2,1)}) %reduce-scatter.9.cloned.1.call-update) | async-done | bytes 49168
  444.0 0.9 reshape.69
  445.0 1.9 collective-permute-start.6
  447.0 2.6 collective-permute-start.7
  449.5 1.5 fusion.42
  451.1 1.5 fusion.40
  452.6 1.6 fusion.44
  454.2 1.6 fusion
  455.9 2.3 fusion.2
  458.5 0.9 fusion.13
  459.4 99.1 %all-reduce.5.cloned.1.call-done = bf16[2,64,1536]{2,1,0:T(8,128)(2,1)} async-done(((bf16[2,64,1536]{2,1,0:T(8,128)(2,1)}), bf16[2,64,1536]{2,1,0:T(8,128)(2,1)}) %all-reduce.5.cloned.1.call-update) | async-done | bytes 393232 | tf_op jit(solution)/shard_map/psum | solution.py:72
  558.5 1.8 multiply_reduce_fusion
  560.3 1.1 fusion.77
  561.6 36.0 %all_gather.32 = bf16[2,64,1536]{1,0,2:T(2,128)(2,1)S(1)} all-gather(bf16[2,64,192]{1,0,2:T(2,128)(2,1)S(1)} %copy.60), channel_id=1, replica_groups=mesh['seq'=64,'tensor'=8] {'tensor'}, dimensions={2}, use_global_device_ids=true | all-gather | bytes 442368 | tf_op jit(solution)/shard_map/all_gather | solution.py:51
  597.6 1.1 convolution_convert_fusion.2
  (83 shorter events, 5.4 us)
Async XLA Ops:
  8.0 69.1 %copy-start = (bf16[2,64,192]{2,1,0:T(8,128)(2,1)S(1)}, bf16[2,64,192]{2,1,0:T(8,128)(2,1)}, u32[]{:S(2)}) copy-start(bf16[2,64,192]{2,1,0:T(8,128)(2,1)} %param.9) | copy-start | bytes 147460
  8.0 71.9 %copy-start.1 = (bf16[2,128,96]{1,2,0:T(8,128)(2,1)S(1)}, bf16[2,128,96]{1,2,0:T(8,128)(2,1)}, u32[]{:S(2)}) copy-start(bf16[2,128,96]{1,2,0:T(8,128)(2,1)} %param.17) | copy-start | bytes 147460
  8.0 80.3 %copy-start.15 = (bf16[24,2,96]{2,1,0:T(2,128)(2,1)S(1)}, bf16[24,2,96]{2,1,0:T(2,128)(2,1)}, u32[]{:S(2)}) copy-start(bf16[24,2,96]{2,1,0:T(2,128)(2,1)} %param.13) | copy-start | bytes 27652
  8.0 80.9 %copy-start.12 = (bf16[5,12,96]{2,1,0:T(8,128)(2,1)S(1)}, bf16[5,12,96]{2,1,0:T(8,128)(2,1)}, u32[]{:S(2)}) copy-start(bf16[5,12,96]{2,1,0:T(8,128)(2,1)} %param.16) | copy-start | bytes 34564
  8.0 222.3 %reduce-scatter.7.cloned.1.call-start = ((), (), s32[]{:S(2)}) async-start(), calls=%async_computation.5 | async-start | bytes 442368
  79.3 198.9 %all-gather.2.cloned.1.call-start = ((), (), s32[]{:S(2)}) async-start(), calls=%async_computation.2 | async-start | bytes 3993600 | tf_op jit(solution)/shard_map/all_gather | solution.py:101
  79.8 278.9 %all-reduce.3.cloned.1.call-start = ((), (), s32[]{:S(2)}) async-start(), calls=%async_computation.3 | async-start | bytes 786432 | tf_op jit(solution)/shard_map/psum | solution.py:72
  80.6 142.4 %collective-permute-start.4 = (bf16[2,2,96]{1,2,0:T(8,128)(2,1)}, bf16[2,2,96]{1,2,0:T(8,128)(2,1)}, u32[]{:S(2)}, u32[]{:S(2)}) collective-permute-start(bf16[2,2,96]{1,2,0:T(8,128)(2,1)} %get-tuple-element.28), channel_id=1, source_target_pairs={{8,0},{16,8},{24,16},{32,24},{40,32},{48,40},{56,48},{64,56},{72,6... | collective-permute-start | bytes 2312 | tf_op jit(solution)/shard_map/ppermute | solution.py:21
  85.6 138.8 %collective-permute-start.5 = (bf16[2,2,96]{1,2,0:T(8,128)(2,1)}, bf16[2,2,96]{1,2,0:T(8,128)(2,1)}, u32[]{:S(2)}, u32[]{:S(2)}) collective-permute-start(bf16[2,2,96]{1,2,0:T(8,128)(2,1)} %get-tuple-element.29), channel_id=1, source_target_pairs={{0,8},{8,16},{16,24},{24,32},{32,40},{40,48},{48,56},{56,64},{64,7... | collective-permute-start | bytes 2312 | tf_op jit(solution)/shard_map/ppermute | solution.py:20
  159.7 67.3 %copy-start.4 = (bf16[1,768,96]{1,2,0:T(8,128)(2,1)S(1)}, bf16[1,768,96]{1,2,0:T(8,128)(2,1)}, u32[]{:S(2)}) copy-start(bf16[1,768,96]{1,2,0:T(8,128)(2,1)} %copy.75) | copy-start | bytes 442372
  160.4 68.0 %copy-start.2 = (bf16[1,768,96]{1,2,0:T(8,128)(2,1)S(1)}, bf16[1,768,96]{1,2,0:T(8,128)(2,1)}, u32[]{:S(2)}) copy-start(bf16[1,768,96]{1,2,0:T(8,128)(2,1)} %copy.78) | copy-start | bytes 442372
  230.3 213.7 %reduce-scatter.9.cloned.1.call-start = ((), (), s32[]{:S(2)}) async-start(), calls=%async_computation.6 | async-start | bytes 442368
  269.9 4.6 copy-start.16
  270.9 0.5 copy-start.13
  271.4 12.5 %copy-start.9 = (bf16[2,64,192]{2,1,0:T(8,128)(2,1)S(1)}, bf16[2,64,192]{2,1,0:T(8,128)(2,1)}, u32[]{:S(2)}) copy-start(bf16[2,64,192]{2,1,0:T(8,128)(2,1)} %copy.67) | copy-start | bytes 147460
  272.6 7.0 %collective-permute-start = (bf16[2,2,1536]{2,1,0:T(2,128)(2,1)S(1)}, bf16[2,2,1536]{2,1,0:T(2,128)(2,1)S(1)}, u32[]{:S(2)}, u32[]{:S(2)}) collective-permute-start(bf16[2,2,1536]{2,1,0:T(2,128)(2,1)S(1)} %get-tuple-element.24), channel_id=1, source_target_pairs={{0,8},{8,16},{16,24},{24,32},{32,40},{40,48},{48,56},{56,64},{64,7... | collective-permute-start | bytes 36872 | tf_op jit(solution)/shard_map/ppermute | solution.py:20
  274.5 6.5 %collective-permute-start.1 = (bf16[2,2,1536]{2,1,0:T(2,128)(2,1)S(1)}, bf16[2,2,1536]{2,1,0:T(2,128)(2,1)S(1)}, u32[]{:S(2)}, u32[]{:S(2)}) collective-permute-start(bf16[2,2,1536]{2,1,0:T(2,128)(2,1)S(1)} %get-tuple-element.25), channel_id=1, source_target_pairs={{8,0},{16,8},{24,16},{32,24},{40,32},{48,40},{56,48},{64,56},{72,6... | collective-permute-start | bytes 36872 | tf_op jit(solution)/shard_map/ppermute | solution.py:21
  282.5 39.5 %copy-start.10 = (bf16[2,128,96]{1,2,0:T(8,128)(2,1)S(1)}, bf16[2,128,96]{1,2,0:T(8,128)(2,1)}, u32[]{:S(2)}) copy-start(bf16[2,128,96]{1,2,0:T(8,128)(2,1)} %param.14) | copy-start | bytes 147460
  322.0 0.6 copy-start.7
  358.2 0.6 copy-start.18
  362.5 0.6 copy-start.5
  365.1 193.4 %all-reduce.5.cloned.1.call-start = ((), (), s32[]{:S(2)}) async-start(), calls=%async_computation.4 | async-start | bytes 786432 | tf_op jit(solution)/shard_map/psum | solution.py:72
  365.2 7.4 %collective-permute-start.2 = (bf16[2,2,768]{2,1,0:T(2,128)(2,1)S(1)}, bf16[2,2,768]{2,1,0:T(2,128)(2,1)S(1)}, u32[]{:S(2)}, u32[]{:S(2)}) collective-permute-start(bf16[2,2,768]{2,1,0:T(2,128)(2,1)S(1)} %get-tuple-element.22), channel_id=1, source_target_pairs={{0,8},{8,16},{16,24},{24,32},{32,40},{40,48},{48,56},{56,64},{64,7... | collective-permute-start | bytes 18440 | tf_op jit(solution)/shard_map/ppermute | solution.py:20
  368.9 89.3 %collective-permute-start.3 = (bf16[2,2,768]{2,1,0:T(2,128)(2,1)S(1)}, bf16[2,2,768]{2,1,0:T(2,128)(2,1)S(1)}, u32[]{:S(2)}, u32[]{:S(2)}) collective-permute-start(bf16[2,2,768]{2,1,0:T(2,128)(2,1)S(1)} %get-tuple-element.23), channel_id=1, source_target_pairs={{8,0},{16,8},{24,16},{32,24},{40,32},{48,40},{56,48},{64,56},{72,6... | collective-permute-start | bytes 18440 | tf_op jit(solution)/shard_map/ppermute | solution.py:21
  445.0 6.1 collective-permute-start.6
  447.0 5.7 collective-permute-start.7
  452.6 5.6 copy-start.6
  454.2 4.3 copy-start.3
  454.2 4.3 copy-start.8
  454.2 104.3 %copy-start.11 = (f32[1536]{0:T(1024)S(1)}, f32[1536]{0:T(1024)}, u32[]{:S(2)}) copy-start(f32[1536]{0:T(1024)} %param.11) | copy-start | bytes 18436
  454.2 104.3 %copy-start.14 = (f32[2,64]{1,0:T(2,128)S(1)}, f32[2,64]{1,0:T(2,128)}, u32[]{:S(2)}) copy-start(f32[2,64]{1,0:T(2,128)} %copy-done.13) | copy-start | bytes 1540
  455.8 104.5 %copy-start.17 = (f32[2,64]{1,0:T(2,128)S(1)}, f32[2,64]{1,0:T(2,128)}, u32[]{:S(2)}) copy-start(f32[2,64]{1,0:T(2,128)} %copy-done.16) | copy-start | bytes 1540
Sparse Core Ops, SparseCore 0:
  79.4 80.6 reduce-scatter.6
  230.4 92.9 all-reduce.2
  365.2 78.7 reduce-scatter.8
  458.3 100.1 all-reduce.4
Sparse Core Ops, SparseCore 1:
  81.8 117.8 all-gather.1
where the time goes:
time: 607 us; the launch traced here: 606 us
  blocking collectives  341 us (56%)
  waiting for transfers between devices  169 us (28%)
  matrix products  27.6 us (5%)
  starting transfers between devices  22.8 us (4%)
  local copies, waits for them, and re-layouts  20.7 us (3%)
  between operations  15.9 us (3%)
  other arithmetic  9.67 us (2%)
    all_gather x3, blocking collectives, spread(): return lax.all_gather(field, 'tensor', axis=2, tiled=True)  107 us
    psum x2, waiting for transfers between devices, norm_back(): lax.psum(partial_grad.astype(jnp.bfloat16), 'tensor').astype(jnp.float32)  99.1 us
    unnamed x7, waiting for transfers between devices  69.6 us
    all_gather x1, blocking collectives, per_device(): lax.all_gather(w_out, 'seq', axis=1, tiled=True)  69.1 us
    all_gather x1, blocking collectives, per_device(): lax.all_gather(w_conv2, 'seq', axis=1, tiled=True)  65.4 us
    all_gather x1, blocking collectives, per_device(): lax.all_gather(w_up, 'seq', axis=0, tiled=True)  62.1 us
    all_gather x1, blocking collectives, per_device(): projected_full = lax.all_gather(projected, 'tensor', axis=2, tiled=True)  37.2 us
    dot_general x12, matrix products, matmul_back(): lax.dot_general(left, right, (((left.ndim - 1,), (right.ndim - 1,)), ((),...  15.9 us
  transfers between devices with their start and end apart: 13, of which 2 were waited for; matrix products, arithmetic and copies ran while one was open for 7% of the time, Pallas kernels for 0%

commit v1 on v0

v1 whole, which is shorter than its diff:
```python
import jax
import jax.numpy as jnp
from jax import lax
from jax.sharding import PartitionSpec as P

C_COARSE = 1536
C_FINE = 768
EPS = 1e-06
BF16 = jnp.bfloat16
F32 = jnp.float32
NT = 8
ZS = 16
Y_PAIRS = [[y * 32 + i for y in range(2)] for i in range(32)]
Z_CORES = [[y * 32 + i for i in range(32)] for y in range(2)]


def dot(left, right):
    return lax.dot_general(
        left, right, (((left.ndim - 1,), (0,)), ((), ())), preferred_element_type=F32
    )


def dot_t(left, right):
    return lax.dot_general(
        left,
        right,
        (((left.ndim - 1,), (right.ndim - 1,)), ((), ())),
        preferred_element_type=F32,
    )


def exchange(blocks):
    return lax.all_to_all(blocks, "tensor", 0, 0)


def share(piece):
    return exchange(jnp.broadcast_to(piece[None], (NT,) + piece.shape))


def neighbours(shard, width):
    size, length = lax.axis_size("seq"), shard.shape[1]
    up = [(i, i + 1) for i in range(size - 1)]
    down = [(j, i) for i, j in up]
    before = lax.ppermute(shard[:, length - width :], "seq", up)
    after = lax.ppermute(shard[:, :width], "seq", down)
    return jnp.concatenate([before, shard, after], axis=1)


def lanes(blocks):
    moved = jnp.moveaxis(blocks, 0, 2)
    return moved.reshape(moved.shape[:2] + (-1,))


def split(full):
    return jnp.moveaxis(full.reshape(full.shape[:2] + (NT, -1)), 2, 0)


def per_device(trunk, w_out, gain_coarse, w_conv1, w_up, skip, gain_fine, w_conv2, cotangent):
    rank = lax.axis_index("tensor")
    place = lax.axis_index("seq")
    part_coarse, part_fine = C_COARSE // NT, C_FINE // NT
    seqs, slab = trunk.shape[0], trunk.shape[1]

    turned = [
        ((8 * a + b) * NT + t, (8 * t + b) * NT + a)
        for a in range(8)
        for b in range(8)
        for t in range(8)
    ]
    up_shard = w_up.reshape(24, 192)
    up_turned = lax.ppermute(up_shard, ("seq", "tensor"), turned)
    conv1_shard = jnp.transpose(w_conv1, (1, 0, 2)).reshape(24, 960)
    conv2_flat = jnp.transpose(w_conv2, (1, 0, 2)).reshape(12, 480)
    conv2_shard = jnp.concatenate([conv2_flat[:, :240], conv2_flat[:, 240:]], axis=0)
    packed = jnp.concatenate(
        [w_out.T, conv1_shard, up_shard, up_turned, conv2_shard, jnp.zeros((24, 80), BF16)],
        axis=1,
    )
    paired = lax.all_gather(packed, "seq", axis=0, axis_index_groups=Y_PAIRS)
    gathered = lax.all_gather(
        paired[:, :, 192:], "seq", axis=1, tiled=True, axis_index_groups=Z_CORES
    )
    out_t = lax.all_gather(
        paired[:, :, :192], "seq", axis=1, tiled=True, axis_index_groups=Z_CORES
    ).reshape(C_COARSE, part_coarse)
    flat = gathered.reshape(C_COARSE, -1)
    conv1_w = flat[:, :960]
    up_w = flat[:, 960:1152]
    up_turned_w = flat[:, 1152:1344].reshape(NT, part_coarse, 192)
    conv2_w = (
        gathered[:, :, 1344:1584]
        .reshape(2, 32, 2, 12, 240)
        .transpose(0, 1, 3, 2, 4)
        .reshape(C_FINE, 480)
    )

    trunk_ext = neighbours(trunk, 4)
    skip_ext = neighbours(skip, 4)
    cot_ext = neighbours(cotangent, 6)
    fine_rows = 2 * slab + 8
    index = place * 2 * slab - 4 + lax.broadcasted_iota(jnp.int32, (1, fine_rows, 1), 1)
    inside = (index >= 0) & (index < 2 * slab * lax.axis_size("seq"))

    partial = dot_t(trunk_ext, out_t).astype(BF16)
    projected = jnp.sum(exchange(split(partial)).astype(F32), axis=0).astype(BF16)
    projected_full = lanes(share(projected)).astype(F32)
    scale_coarse = lax.rsqrt(
        jnp.mean(projected_full * projected_full, axis=-1, keepdims=True) + EPS
    )
    act_coarse = jax.nn.gelu(projected_full * scale_coarse * gain_coarse).astype(BF16)
    cot_full = lanes(share(cot_ext[:, 2 : 2 + fine_rows]))

    taps = dot(act_coarse, conv1_w)
    rows = slab + 4
    mixed = sum(
        taps[:, k : k + rows, k * part_coarse : (k + 1) * part_coarse] for k in range(5)
    )
    lifted = (projected[:, 2 : 2 + rows].astype(F32) + mixed).astype(BF16)

    stacked = jnp.concatenate([cot_ext[:, 4 - k : 4 - k + fine_rows] for k in range(5)], axis=2)
    back_partial = split(dot_t(stacked, conv2_w).astype(BF16))
    first = exchange(
        jnp.concatenate(
            [
                jnp.broadcast_to(lifted[None], (NT,) + lifted.shape),
                back_partial.reshape(NT, seqs, rows, 2 * part_fine),
            ],
            axis=1,
        )
    )
    lifted_full = lanes(first[:, :seqs])
    back_piece = jnp.sum(first[:, seqs:].astype(F32), axis=0).astype(BF16)
    upper = dot(lifted_full, up_w).reshape(seqs, fine_rows, part_fine)
    merged = jnp.where(inside, upper + skip_ext.astype(F32), 0.0).astype(BF16)
    second = share(
        jnp.concatenate([merged, back_piece.reshape(seqs, fine_rows, part_fine)], axis=0)
    )
    merged_full = lanes(second[:, :seqs]).astype(F32)
    back_fine = lanes(second[:, seqs:]).astype(F32)

    def activate(value):
        scaled = value * lax.rsqrt(jnp.mean(value * value, axis=-1, keepdims=True) + EPS)
        return jax.nn.gelu(scaled * gain_fine)

    act_fine, pull = jax.vjp(activate, merged_full)
    skip_grad_full = jnp.where(
        inside, cot_full.astype(F32) + pull(back_fine)[0], 0.0
    ).astype(BF16)
    folded = skip_grad_full.reshape(seqs, rows, 2, NT, part_fine)
    lifted_grad = sum(
        dot_t(folded[:, :, :, t].reshape(seqs, rows, 2 * part_fine), up_turned_w[t])
        for t in range(NT)
    ).astype(BF16)
    stacked_grad = jnp.concatenate(
        [lifted_grad[:, 4 - k : 4 - k + slab] for k in range(5)], axis=2
    )
    third = exchange(split(dot_t(stacked_grad, conv1_w).astype(BF16)))
    back_coarse = jnp.sum(third.astype(F32), axis=0)

    own = projected[:, 4 : 4 + slab].astype(F32)
    own_gain = lax.dynamic_slice_in_dim(gain_coarse, rank * part_coarse, part_coarse, 0)
    scale = scale_coarse[:, 4 : 4 + slab]
    _, pull_gelu = jax.vjp(jax.nn.gelu, own * scale * own_gain)
    inner = pull_gelu(back_coarse)[0] * own_gain
    share_sum = jnp.sum(inner * own, axis=-1, keepdims=True)
    high = share_sum.astype(BF16)
    low = (share_sum - high.astype(F32)).astype(BF16)
    direct = (lifted_grad[:, 2 : 2 + slab].astype(F32) + scale * inner).astype(BF16)
    fourth = share(
        jnp.concatenate([direct, high, low, jnp.zeros((seqs, slab, 62), BF16)], axis=2)
    )
    total = jnp.sum(fourth[..., 192:194].astype(F32), axis=(0, 3))[..., None]
    factor = scale * scale * scale * total * (1.0 / C_COARSE)
    projected_grad = (
        lanes(fourth[..., :192]).astype(F32) - projected_full[:, 4 : 4 + slab] * factor
    ).astype(BF16)
    trunk_grad = dot(projected_grad, out_t).astype(BF16)

    fine_taps = dot(act_fine.astype(BF16), conv2_w)
    fine_mixed = sum(
        fine_taps[:, 2 + k : 2 + k + 2 * slab, k * part_fine : (k + 1) * part_fine]
        for k in range(5)
    )
    keep = slice(4, 4 + 2 * slab)
    decoded = (merged[:, keep].astype(F32) + fine_mixed).astype(BF16)
    skip_grad = lax.dynamic_slice_in_dim(
        skip_grad_full[:, keep], rank * part_fine, part_fine, 2
    )
    return (decoded, skip_grad, trunk_grad)


def solution(mesh):
    in_specs = (
        P(None, "seq", "tensor"),
        P("tensor", "seq"),
        P(),
        P(None, "seq", "tensor"),
        P("seq", None, "tensor"),
        P(None, "seq", "tensor"),
        P(),
        P(None, "seq", "tensor"),
        P(None, "seq", "tensor"),
    )
    out_specs = (P(None, "seq", "tensor"), P(None, "seq", "tensor"), P(None, "seq", "tensor"))
    return jax.shard_map(
        per_device, mesh=mesh, in_specs=in_specs, out_specs=out_specs, check_vma=False
    )
```

time: 607 us -> 254 us (0.42)
  blocking collectives: 341 us -> 55.8 us
  waiting for transfers between devices: 169 us -> 68.5 us
  starting transfers between devices: 22.8 us -> 48 us
  local copies, waits for them, and re-layouts: 20.7 us -> 36.6 us
  matrix products: 27.6 us -> 18.4 us
    all_gather x7 -> x2, blocking collectives: 341 us -> 55.8 us  [the longest x1 45.6 us: per_device(): lax.all_gather(paired[:, :, :192], 'seq', axis=1, tiled=True, axis_index_...]
    psum x2 -> x0, waiting for transfers between devices: 99.1 us -> none  [norm_back(): lax.psum(partial_grad.astype(jnp.bfloat16), 'tensor').astype(jnp.float32)]
    unnamed x7 -> x1, waiting for transfers between devices: 69.6 us -> 0.02 us
    all_to_all x0 -> x7, waiting for transfers between devices: none -> 67.1 us  [exchange(): return lax.all_to_all(blocks, 'tensor', 0, 0)]
    all_to_all x0 -> x7, starting transfers between devices: none -> 30.6 us  [exchange(): return lax.all_to_all(blocks, 'tensor', 0, 0)]
    unnamed x56 -> x32, local copies, waits for them, and re-layouts: 15.2 us -> 3.67 us
    dot_general x24 -> x15, matrix products: 27.6 us -> 18.4 us  [the longest x11 12.6 us: dot_t(): lax.dot_general(left, right, (((left.ndim - 1,), (right.ndim - 1,)), ((),...]
    convert_element_type x3 -> x14, local copies, waits for them, and re-layouts: 0.27 us -> 6.84 us  [the longest x2 1.66 us: per_device(): merged_full = lanes(second[:, :seqs]).astype(F32)]
  transfers between devices with their start and end apart: 13 -> 15, of which waited for: 2 -> 8; matrix products, arithmetic and copies ran while one was open for 7% -> 7% of each run, Pallas kernels for 0% -> 0%
where the time goes in v1:
time: 254 us; the launch traced here: 252 us
  waiting for transfers between devices  68.5 us (27%)
  blocking collectives  55.8 us (22%)
  starting transfers between devices  48 us (19%)
  local copies, waits for them, and re-layouts  36.6 us (14%)
  matrix products  18.4 us (7%)
  between operations  14.8 us (6%)
  other arithmetic  10 us (4%)
    all_to_all x7, waiting for transfers between devices, exchange(): return lax.all_to_all(blocks, 'tensor', 0, 0)  67.1 us
    all_gather x1, blocking collectives, per_device(): lax.all_gather(paired[:, :, :192], 'seq', axis=1, tiled=True, axis_index_...  45.6 us
    all_to_all x7, starting transfers between devices, exchange(): return lax.all_to_all(blocks, 'tensor', 0, 0)  30.6 us
    dot_general x11, matrix products, dot_t(): lax.dot_general(left, right, (((left.ndim - 1,), (right.ndim - 1,)), ((),...  12.6 us
    all_gather x1, blocking collectives, per_device(): paired = lax.all_gather(packed, 'seq', axis=0, axis_index_groups=Y_PAIRS)  10.2 us
    ppermute x3, starting transfers between devices, neighbours(): after = lax.ppermute(shard[:, :width], 'seq', down)  10 us
    ppermute x3, starting transfers between devices, neighbours(): before = lax.ppermute(shard[:, length - width:], 'seq', up)  6.64 us
    dot_general x4, matrix products, dot(): lax.dot_general(left, right, (((left.ndim - 1,), (0,)), ((), ())), prefer...  5.85 us
  transfers between devices with their start and end apart: 15, of which 8 were waited for; matrix products, arithmetic and copies ran while one was open for 7% of the time, Pallas kernels for 0%

profile of v1, /device:TPU:32, one launch (start us, length us, event | category | flops | bytes accessed | tf_op | source)
XLA Modules:
  0.0 252.2 jit_solution(4612936945657712477)
XLA Ops:
  7.2 0.8 reshape.193
  8.7 0.7 copy.178
  9.6 0.9 copy.177
  10.6 0.8 concatenate.32
  11.4 10.2 %all-gather = bf16[48,1856]{1,0:T(8,128)(2,1)S(1)} all-gather(bf16[24,1856]{1,0:T(8,128)(2,1)S(1)} %concatenate.32), channel_id=2, replica_groups={{0,256},{8,264},{16,272},{24,280},{32,288},{40,296},{48,304},{56,312},{..., dimensions={0}, use_global_device_ids=true | all-gather | bytes 267264 | tf_op jit(solution)/shard_map/all_gather | solution.py:79
  21.6 0.8 slice.267
  22.4 1.9 collective-permute-start
  24.3 3.6 %collective-permute-start.1 = (bf16[2,4,192]{2,1,0:T(4,128)(2,1)S(1)}, bf16[2,4,192]{2,1,0:T(4,128)(2,1)S(1)}, u32[]{:S(2)}, u32[]{:S(2)}) collective-permute-start(bf16[2,4,192]{2,1,0:T(4,128)(2,1)S(1)} %get-tuple-element.54), channel_id=1, source_target_pairs={{8,0},{16,8},{24,16},{32,24},{40,32},{48,40},{56,48},{64,56},{72,6... | collective-permute-start | bytes 9224 | tf_op jit(solution)/shard_map/ppermute | solution.py:45
  28.0 45.6 %all_gather.14 = bf16[2,768,192]{2,1,0:T(8,128)(2,1)S(1)} all-gather(bf16[2,24,192]{2,1,0:T(8,128)(2,1)S(1)} %slice.265), channel_id=1, replica_groups={{0,8,16,24,32,40,48,56,64,72,80,88,96,104,112,120,128,136,144,152,160,1..., dimensions={1}, use_global_device_ids=true | all-gather | bytes 608256 | tf_op jit(solution)/shard_map/all_gather | solution.py:83
  73.6 0.9 copy-done.3
  75.4 0.9 copy.254
  76.3 7.4 %all-to-all-start = ((bf16[8,2,72,192]{3,2,1,0:T(8,128)(2,1)}), bf16[8,2,72,192]{3,2,1,0:T(8,128)(2,1)S(1)}, u32[]{:S(2)}, u32[]{:S(2)}) async-start(bf16[8,2,72,192]{3,2,1,0:T(8,128)(2,1)} %bitcast.146), calls=%async_computation | async-start | bytes 1179648 | tf_op jit(solution)/shard_map/all_to_all | solution.py:33
  83.8 11.7 %all-to-all-done = bf16[8,2,72,192]{3,2,1,0:T(8,128)(2,1)S(1)} async-done(((bf16[8,2,72,192]{3,2,1,0:T(8,128)(2,1)}), bf16[8,2,72,192]{3,2,1,0:T(8,128)(2,1)S(1)}, u32[]{:S(2)}, u32[]{:S(2)}) %all-to-all-start) | async-done | bytes 442400 | tf_op jit(solution)/shard_map/all_to_all | solution.py:33
  95.6 0.9 broadcast_in_dim.81
  96.5 3.7 %all-to-all-start.1 = ((bf16[8,2,72,192]{3,2,1,0:T(8,128)(2,1)}), bf16[8,2,72,192]{3,2,1,0:T(8,128)(2,1)S(1)}, u32[]{:S(2)}, u32[]{:S(2)}) async-start(bf16[8,2,72,192]{3,2,1,0:T(8,128)(2,1)} %broadcast_in_dim.81), calls=%async_computation.1 | async-start | bytes 1179648 | tf_op jit(solution)/shard_map/all_to_all | solution.py:33
  100.2 1.9 collective-permute-start.3
  102.2 3.6 %collective-permute-start.4 = (bf16[2,6,96]{2,1,0:T(8,128)(2,1)S(1)}, bf16[2,6,96]{2,1,0:T(8,128)(2,1)S(1)}, u32[]{:S(2)}, u32[]{:S(2)}) collective-permute-start(bf16[2,6,96]{2,1,0:T(8,128)(2,1)S(1)} %get-tuple-element.56), channel_id=1, source_target_pairs={{8,0},{16,8},{24,16},{32,24},{40,32},{48,40},{56,48},{64,56},{72,6... | collective-permute-start | bytes 6920 | tf_op jit(solution)/shard_map/ppermute | solution.py:45
  105.8 1.3 collective-permute-done.4
  107.4 3.9 %all-to-all-done.1 = bf16[8,2,72,192]{3,2,1,0:T(8,128)(2,1)S(1)} async-done(((bf16[8,2,72,192]{3,2,1,0:T(8,128)(2,1)}), bf16[8,2,72,192]{3,2,1,0:T(8,128)(2,1)S(1)}, u32[]{:S(2)}, u32[]{:S(2)}) %all-to-all-start.1) | async-done | bytes 442400 | tf_op jit(solution)/shard_map/all_to_all | solution.py:33
  112.8 2.8 %fusion = f32[2,72,960]{2,1,0:T(8,128)S(1)} fusion(bf16[1536,1664]{1,0:T(8,128)(2,1)} %bitcast.158, f32[2,72,1536]{2,1,0:T(8,128)S(1)} %reshape.206, f32[1536]{0:T(1024)S(1)} %copy-done.13, f32[2,72]{1,0:T(2,128)S(1)} %get-tuple-element.62), kind=kOutput, calls=%fused_computation.3 | convolution fusion | flops 427106304 | bytes 4590144 | tf_op jit(solution)/shard_map/dot_general | solution.py:18
  115.8 1.6 slice.281
  117.4 0.8 copy.186
  121.1 1.5 copy.190
  122.6 3.7 %all-to-all-start.2 = ((bf16[8,4,68,192]{3,1,2,0:T(4,128)(2,1)}), bf16[8,4,68,192]{3,1,2,0:T(4,128)(2,1)S(1)}, u32[]{:S(2)}, u32[]{:S(2)}) async-start(bf16[8,4,68,192]{3,1,2,0:T(4,128)(2,1)} %copy.190), calls=%async_computation.2 | async-start | bytes 2228224 | tf_op jit(solution)/shard_map/all_to_all | solution.py:33
  126.5 2.8 %collective-permute-start.5 = (bf16[2,4,96]{2,1,0:T(4,128)(2,1)S(1)}, bf16[2,4,96]{2,1,0:T(4,128)(2,1)S(1)}, u32[]{:S(2)}, u32[]{:S(2)}) collective-permute-start(bf16[2,4,96]{2,1,0:T(4,128)(2,1)S(1)} %get-tuple-element.51), channel_id=1, source_target_pairs={{0,8},{8,16},{16,24},{24,32},{32,40},{40,48},{48,56},{56,64},{64,7... | collective-permute-start | bytes 4616 | tf_op jit(solution)/shard_map/ppermute | solution.py:44
  129.3 2.8 %collective-permute-start.6 = (bf16[2,4,96]{2,1,0:T(4,128)(2,1)S(1)}, bf16[2,4,96]{2,1,0:T(4,128)(2,1)S(1)}, u32[]{:S(2)}, u32[]{:S(2)}) collective-permute-start(bf16[2,4,96]{2,1,0:T(4,128)(2,1)S(1)} %get-tuple-element.52), channel_id=1, source_target_pairs={{8,0},{16,8},{24,16},{32,24},{40,32},{48,40},{56,48},{64,56},{72,6... | collective-permute-start | bytes 4616 | tf_op jit(solution)/shard_map/ppermute | solution.py:45
  132.1 13.6 %all-to-all-done.2 = bf16[8,4,68,192]{3,1,2,0:T(4,128)(2,1)S(1)} async-done(((bf16[8,4,68,192]{3,1,2,0:T(4,128)(2,1)}), bf16[8,4,68,192]{3,1,2,0:T(4,128)(2,1)S(1)}, u32[]{:S(2)}, u32[]{:S(2)}) %all-to-all-start.2) | async-done | bytes 835616 | tf_op jit(solution)/shard_map/all_to_all | solution.py:33
  145.7 0.9 broadcast_in_dim.86
  146.5 4.7 %all-to-all-start.4 = ((bf16[8,2,136,96]{3,2,1,0:T(8,128)(2,1)}), bf16[8,2,136,96]{3,2,1,0:T(8,128)(2,1)S(1)}, u32[]{:S(2)}, u32[]{:S(2)}) async-start(bf16[8,2,136,96]{3,2,1,0:T(8,128)(2,1)} %broadcast_in_dim.86), calls=%async_computation.4 | async-start | bytes 1114112 | tf_op jit(solution)/shard_map/all_to_all | solution.py:33
  151.2 1.0 slice_bitcast_fusion.5
  152.9 1.7 fusion.44
  155.0 7.7 %all-to-all-done.4 = bf16[8,2,136,96]{3,2,1,0:T(8,128)(2,1)S(1)} async-done(((bf16[8,2,136,96]{3,2,1,0:T(8,128)(2,1)}), bf16[8,2,136,96]{3,2,1,0:T(8,128)(2,1)S(1)}, u32[]{:S(2)}, u32[]{:S(2)}) %all-to-all-start.4) | async-done | bytes 417824 | tf_op jit(solution)/shard_map/all_to_all | solution.py:33
  162.7 1.2 broadcast_in_dim.84
  163.9 3.7 %all-to-all-start.3 = ((bf16[8,4,136,96]{3,2,1,0:T(8,128)(2,1)}), bf16[8,4,136,96]{3,2,1,0:T(8,128)(2,1)S(1)}, u32[]{:S(2)}, u32[]{:S(2)}) async-start(bf16[8,4,136,96]{3,2,1,0:T(8,128)(2,1)} %broadcast_in_dim.84), calls=%async_computation.3 | async-start | bytes 2228224 | tf_op jit(solution)/shard_map/all_to_all | solution.py:33
  168.8 1.0 slice.299
  169.9 14.2 %all-to-all-done.3 = bf16[8,4,136,96]{3,2,1,0:T(8,128)(2,1)S(1)} async-done(((bf16[8,4,136,96]{3,2,1,0:T(8,128)(2,1)}), bf16[8,4,136,96]{3,2,1,0:T(8,128)(2,1)S(1)}, u32[]{:S(2)}, u32[]{:S(2)}) %all-to-all-start.3) | async-done | bytes 835616 | tf_op jit(solution)/shard_map/all_to_all | solution.py:33
  184.4 2.1 fusion.11
  186.5 0.8 reduce_sum.91
  187.3 0.8 add.186
  188.9 1.3 reshape.209
  190.2 1.2 reshape.208
  191.5 1.0 fusion.95
  192.4 1.5 fusion.22
  193.9 3.8 %slice_reduce_fusion.1 = (bf16[2,68,2,96]{3,2,1,0:T(2,128)(2,1)S(1)}, bf16[2,68,2,96]{3,2,1,0:T(2,128)(2,1)S(1)}, bf16[2,68,2,96]{3,2,1,0:T(2,128)(2,1)S(1)}, bf...) fusion(bf16[2,68,2,8,96]{4,3,2,1,0:T(8,128)(2,1)S(1)} %fusion.22), kind=kLoop, calls=%fused_computation.104 | loop fusion | bytes 835584 | tf_op jit(solution)/shard_map/slice | solution.py:151
  197.8 1.1 fusion.76
  199.7 1.1 convolution_add_fusion.6
  200.8 1.1 convolution_add_fusion.5
  201.9 1.1 convolution_add_fusion.4
  203.0 1.1 convolution_add_fusion.3
  204.1 1.1 convolution_add_fusion.2
  205.2 1.1 convolution_add_fusion.1
  206.3 1.1 fusion.2
  207.6 3.1 %convolution_convert_fusion.1 = bf16[2,64,1536]{2,1,0:T(8,128)(2,1)S(1)} fusion(bf16[2,64,960]{2,1,0:T(8,128)(2,1)S(1)} %concatenate.38, bf16[1536,1664]{1,0:T(8,128)(2,1)} %bitcast.168), kind=kOutput, calls=%fused_computation.2 | convolution fusion | flops 377683968 | bytes 3784704 | tf_op jit(solution)/shard_map/dot_general | solution.py:24
  211.1 0.9 copy.256
  212.0 4.0 %all-to-all-start.5 = ((bf16[8,2,64,192]{3,2,1,0:T(8,128)(2,1)}), bf16[8,2,64,192]{3,2,1,0:T(8,128)(2,1)S(1)}, u32[]{:S(2)}, u32[]{:S(2)}) async-start(bf16[8,2,64,192]{3,2,1,0:T(8,128)(2,1)} %bitcast.148), calls=%async_computation.5 | async-start | bytes 1048576 | tf_op jit(solution)/shard_map/all_to_all | solution.py:33
  216.9 1.2 fusion.73
  218.2 0.7 copy.218
  219.5 6.9 %all-to-all-done.5 = bf16[8,2,64,192]{3,2,1,0:T(8,128)(2,1)S(1)} async-done(((bf16[8,2,64,192]{3,2,1,0:T(8,128)(2,1)}), bf16[8,2,64,192]{3,2,1,0:T(8,128)(2,1)S(1)}, u32[]{:S(2)}, u32[]{:S(2)}) %all-to-all-start.5) | async-done | bytes 393248 | tf_op jit(solution)/shard_map/all_to_all | solution.py:33
  227.2 0.8 broadcast_in_dim.93
  228.0 3.5 %all-to-all-start.6 = ((bf16[8,2,64,256]{3,2,1,0:T(8,128)(2,1)}), bf16[8,2,64,256]{3,2,1,0:T(8,128)(2,1)S(1)}, u32[]{:S(2)}, u32[]{:S(2)}) async-start(bf16[8,2,64,256]{3,2,1,0:T(8,128)(2,1)} %broadcast_in_dim.93), calls=%async_computation.6 | async-start | bytes 1048576 | tf_op jit(solution)/shard_map/all_to_all | solution.py:33
  232.1 0.7 copy.217
  232.8 9.1 %all-to-all-done.6 = bf16[8,2,64,256]{3,2,1,0:T(8,128)(2,1)S(1)} async-done(((bf16[8,2,64,256]{3,2,1,0:T(8,128)(2,1)}), bf16[8,2,64,256]{3,2,1,0:T(8,128)(2,1)S(1)}, u32[]{:S(2)}, u32[]{:S(2)}) %all-to-all-start.6) | async-done | bytes 524320 | tf_op jit(solution)/shard_map/all_to_all | solution.py:33
  243.3 0.8 copy-done.4
  244.4 1.0 convolution_convert_fusion.3
  (124 shorter events, 16.3 us)
Async XLA Ops:
  7.2 15.2 %copy-start.9 = (bf16[2,64,192]{2,1,0:T(8,128)(2,1)S(1)}, bf16[2,64,192]{2,1,0:T(8,128)(2,1)}, u32[]{:S(2)}) copy-start(bf16[2,64,192]{2,1,0:T(8,128)(2,1)} %param.9) | copy-start | bytes 147460
  7.2 105.6 %all-gather.3.cloned.1.call-start = ((), (), s32[]{:S(2)}) async-start(), calls=%async_computation.7 | async-start | bytes 5271552 | tf_op jit(solution)/shard_map/all_gather | solution.py:80
  8.0 2.5 %collective-permute-start.2 = (bf16[24,192]{1,0:T(8,128)(2,1)S(1)}, bf16[24,192]{1,0:T(8,128)(2,1)S(1)}, u32[]{:S(2)}, u32[]{:S(2)}) collective-permute-start(bf16[24,192]{1,0:T(8,128)(2,1)S(1)} %reshape.193), channel_id=1, source_target_pairs={{0,0},{1,64},{2,128},{3,192},{4,256},{5,320},{6,384},{7,448},{8,8}... | collective-permute-start | bytes 27656 | tf_op jit(solution)/shard_map/ppermute | solution.py:71
  22.4 51.2 %collective-permute-start = (bf16[2,4,192]{2,1,0:T(4,128)(2,1)S(1)}, bf16[2,4,192]{2,1,0:T(4,128)(2,1)S(1)}, u32[]{:S(2)}, u32[]{:S(2)}) collective-permute-start(bf16[2,4,192]{2,1,0:T(4,128)(2,1)S(1)} %get-tuple-element.53), channel_id=1, source_target_pairs={{0,8},{8,16},{16,24},{24,32},{32,40},{40,48},{48,56},{56,64},{64,7... | collective-permute-start | bytes 9224 | tf_op jit(solution)/shard_map/ppermute | solution.py:44
  24.3 49.3 %collective-permute-start.1 = (bf16[2,4,192]{2,1,0:T(4,128)(2,1)S(1)}, bf16[2,4,192]{2,1,0:T(4,128)(2,1)S(1)}, u32[]{:S(2)}, u32[]{:S(2)}) collective-permute-start(bf16[2,4,192]{2,1,0:T(4,128)(2,1)S(1)} %get-tuple-element.54), channel_id=1, source_target_pairs={{8,0},{16,8},{24,16},{32,24},{40,32},{48,40},{56,48},{64,56},{72,6... | collective-permute-start | bytes 9224 | tf_op jit(solution)/shard_map/ppermute | solution.py:45
  73.6 0.9 copy-start.3
  75.4 8.3 %copy-start.10 = (bf16[2,128,96]{1,2,0:T(8,128)(2,1)S(1)}, bf16[2,128,96]{1,2,0:T(8,128)(2,1)}, u32[]{:S(2)}) copy-start(bf16[2,128,96]{1,2,0:T(8,128)(2,1)} %param.17) | copy-start | bytes 147460
  76.3 19.2 %all-to-all-start = ((bf16[8,2,72,192]{3,2,1,0:T(8,128)(2,1)}), bf16[8,2,72,192]{3,2,1,0:T(8,128)(2,1)S(1)}, u32[]{:S(2)}, u32[]{:S(2)}) async-start(bf16[8,2,72,192]{3,2,1,0:T(8,128)(2,1)} %bitcast.146), calls=%async_computation | async-start | bytes 1179648 | tf_op jit(solution)/shard_map/all_to_all | solution.py:33
  96.5 14.8 %all-to-all-start.1 = ((bf16[8,2,72,192]{3,2,1,0:T(8,128)(2,1)}), bf16[8,2,72,192]{3,2,1,0:T(8,128)(2,1)S(1)}, u32[]{:S(2)}, u32[]{:S(2)}) async-start(bf16[8,2,72,192]{3,2,1,0:T(8,128)(2,1)} %broadcast_in_dim.81), calls=%async_computation.1 | async-start | bytes 1179648 | tf_op jit(solution)/shard_map/all_to_all | solution.py:33
  100.2 5.6 %collective-permute-start.3 = (bf16[2,6,96]{2,1,0:T(8,128)(2,1)S(1)}, bf16[2,6,96]{2,1,0:T(8,128)(2,1)S(1)}, u32[]{:S(2)}, u32[]{:S(2)}) collective-permute-start(bf16[2,6,96]{2,1,0:T(8,128)(2,1)S(1)} %get-tuple-element.55), channel_id=1, source_target_pairs={{0,8},{8,16},{16,24},{24,32},{32,40},{40,48},{48,56},{56,64},{64,7... | collective-permute-start | bytes 6920 | tf_op jit(solution)/shard_map/ppermute | solution.py:44
  102.2 5.0 %collective-permute-start.4 = (bf16[2,6,96]{2,1,0:T(8,128)(2,1)S(1)}, bf16[2,6,96]{2,1,0:T(8,128)(2,1)S(1)}, u32[]{:S(2)}, u32[]{:S(2)}) collective-permute-start(bf16[2,6,96]{2,1,0:T(8,128)(2,1)S(1)} %get-tuple-element.56), channel_id=1, source_target_pairs={{8,0},{16,8},{24,16},{32,24},{40,32},{48,40},{56,48},{64,56},{72,6... | collective-permute-start | bytes 6920 | tf_op jit(solution)/shard_map/ppermute | solution.py:45
  112.1 0.7 copy-start.13
  112.5 3.1 %copy-start.6 = (f32[2,72,1536]{2,1,0:T(8,128)}, f32[2,72,1536]{2,1,0:T(8,128)S(1)}, u32[]{:S(2)}) copy-start(f32[2,72,1536]{2,1,0:T(8,128)S(1)} %reshape.206) | copy-start | bytes 2654212
  119.2 1.1 copy-start.1
  122.6 3.7 %copy-start.11 = (bf16[2,128,96]{1,2,0:T(8,128)(2,1)S(1)}, bf16[2,128,96]{1,2,0:T(8,128)(2,1)}, u32[]{:S(2)}) copy-start(bf16[2,128,96]{1,2,0:T(8,128)(2,1)} %param.14) | copy-start | bytes 147460
  122.6 23.0 %all-to-all-start.2 = ((bf16[8,4,68,192]{3,1,2,0:T(4,128)(2,1)}), bf16[8,4,68,192]{3,1,2,0:T(4,128)(2,1)S(1)}, u32[]{:S(2)}, u32[]{:S(2)}) async-start(bf16[8,4,68,192]{3,1,2,0:T(4,128)(2,1)} %copy.190), calls=%async_computation.2 | async-start | bytes 2228224 | tf_op jit(solution)/shard_map/all_to_all | solution.py:33
  126.5 28.3 %collective-permute-start.5 = (bf16[2,4,96]{2,1,0:T(4,128)(2,1)S(1)}, bf16[2,4,96]{2,1,0:T(4,128)(2,1)S(1)}, u32[]{:S(2)}, u32[]{:S(2)}) collective-permute-start(bf16[2,4,96]{2,1,0:T(4,128)(2,1)S(1)} %get-tuple-element.51), channel_id=1, source_target_pairs={{0,8},{8,16},{16,24},{24,32},{32,40},{40,48},{48,56},{56,64},{64,7... | collective-permute-start | bytes 4616 | tf_op jit(solution)/shard_map/ppermute | solution.py:44
  129.3 25.5 %collective-permute-start.6 = (bf16[2,4,96]{2,1,0:T(4,128)(2,1)S(1)}, bf16[2,4,96]{2,1,0:T(4,128)(2,1)S(1)}, u32[]{:S(2)}, u32[]{:S(2)}) collective-permute-start(bf16[2,4,96]{2,1,0:T(4,128)(2,1)S(1)} %get-tuple-element.52), channel_id=1, source_target_pairs={{8,0},{16,8},{24,16},{32,24},{40,32},{48,40},{56,48},{64,56},{72,6... | collective-permute-start | bytes 4616 | tf_op jit(solution)/shard_map/ppermute | solution.py:45
  146.5 16.1 %all-to-all-start.4 = ((bf16[8,2,136,96]{3,2,1,0:T(8,128)(2,1)}), bf16[8,2,136,96]{3,2,1,0:T(8,128)(2,1)S(1)}, u32[]{:S(2)}, u32[]{:S(2)}) async-start(bf16[8,2,136,96]{3,2,1,0:T(8,128)(2,1)} %broadcast_in_dim.86), calls=%async_computation.4 | async-start | bytes 1114112 | tf_op jit(solution)/shard_map/all_to_all | solution.py:33
  163.9 3.8 %copy-start.12 = (f32[768]{0:T(1024)S(1)}, f32[768]{0:T(1024)}, u32[]{:S(2)}) copy-start(f32[768]{0:T(1024)} %param.15) | copy-start | bytes 9220
  163.9 20.2 %all-to-all-start.3 = ((bf16[8,4,136,96]{3,2,1,0:T(8,128)(2,1)}), bf16[8,4,136,96]{3,2,1,0:T(8,128)(2,1)S(1)}, u32[]{:S(2)}, u32[]{:S(2)}) async-start(bf16[8,4,136,96]{3,2,1,0:T(8,128)(2,1)} %broadcast_in_dim.84), calls=%async_computation.3 | async-start | bytes 2228224 | tf_op jit(solution)/shard_map/all_to_all | solution.py:33
  211.0 4.9 %copy-start = (f32[2,136,768]{2,1,0:T(8,128)S(1)}, f32[2,136,768]{2,1,0:T(8,128)}, u32[]{:S(2)}) copy-start(f32[2,136,768]{2,1,0:T(8,128)} %reshape.209) | copy-start | bytes 2506756
  212.0 4.1 %copy-start.5 = (f32[2,136,768]{2,1,0:T(8,128)S(1)}, f32[2,136,768]{2,1,0:T(8,128)}, u32[]{:S(2)}) copy-start(f32[2,136,768]{2,1,0:T(8,128)} %reshape.208) | copy-start | bytes 2506756
  212.0 14.4 %all-to-all-start.5 = ((bf16[8,2,64,192]{3,2,1,0:T(8,128)(2,1)}), bf16[8,2,64,192]{3,2,1,0:T(8,128)(2,1)S(1)}, u32[]{:S(2)}, u32[]{:S(2)}) async-start(bf16[8,2,64,192]{3,2,1,0:T(8,128)(2,1)} %bitcast.148), calls=%async_computation.5 | async-start | bytes 1048576 | tf_op jit(solution)/shard_map/all_to_all | solution.py:33
  216.8 2.1 copy-start.8
  226.7 4.8 %copy-start.2 = (bf16[768,480]{1,0:T(8,128)(2,1)S(1)}, bf16[768,480]{1,0:T(8,128)(2,1)}, u32[]{:S(2)}) copy-start(bf16[768,480]{1,0:T(8,128)(2,1)} %copy-done.1) | copy-start | bytes 2211844
  228.0 13.9 %all-to-all-start.6 = ((bf16[8,2,64,256]{3,2,1,0:T(8,128)(2,1)}), bf16[8,2,64,256]{3,2,1,0:T(8,128)(2,1)S(1)}, u32[]{:S(2)}, u32[]{:S(2)}) async-start(bf16[8,2,64,256]{3,2,1,0:T(8,128)(2,1)} %broadcast_in_dim.93), calls=%async_computation.6 | async-start | bytes 1048576 | tf_op jit(solution)/shard_map/all_to_all | solution.py:33
  243.0 1.1 copy-start.4
  243.0 1.4 copy-start.7
Sparse Core Ops, SparseCore 0:
  22.5 86.4 all-gather.2

commit v2 on v1

--- a/solution.py
+++ b/solution.py
@@ -1,6 +1,7 @@
 import jax
 import jax.numpy as jnp
 from jax import lax
+from jax.experimental.layout import Layout, with_layout_constraint
 from jax.sharding import PartitionSpec as P
 
 C_COARSE = 1536
@@ -9,7 +10,6 @@
 BF16 = jnp.bfloat16
 F32 = jnp.float32
 NT = 8
-ZS = 16
 Y_PAIRS = [[y * 32 + i for y in range(2)] for i in range(32)]
 Z_CORES = [[y * 32 + i for i in range(32)] for y in range(2)]
 
@@ -68,27 +68,37 @@
         for t in range(8)
     ]
     up_shard = w_up.reshape(24, 192)
-    up_turned = lax.ppermute(up_shard, ("seq", "tensor"), turned)
+    out_shard = w_out.T
+    both_turned = lax.ppermute(
+        jnp.concatenate([out_shard, up_shard], axis=1), ("seq", "tensor"), turned
+    )
     conv1_shard = jnp.transpose(w_conv1, (1, 0, 2)).reshape(24, 960)
     conv2_flat = jnp.transpose(w_conv2, (1, 0, 2)).reshape(12, 480)
     conv2_shard = jnp.concatenate([conv2_flat[:, :240], conv2_flat[:, 240:]], axis=0)
     packed = jnp.concatenate(
-        [w_out.T, conv1_shard, up_shard, up_turned, conv2_shard, jnp.zeros((24, 80), BF16)],
+        [
+            both_turned[:, :192],
+            conv1_shard,
+            up_shard,
+            both_turned[:, 192:],
+            out_shard,
+            conv2_shard,
+            jnp.zeros((24, 16), BF16),
+        ],
         axis=1,
     )
     paired = lax.all_gather(packed, "seq", axis=0, axis_index_groups=Y_PAIRS)
     gathered = lax.all_gather(
         paired[:, :, 192:], "seq", axis=1, tiled=True, axis_index_groups=Z_CORES
     )
-    out_t = lax.all_gather(
-        paired[:, :, :192], "seq", axis=1, tiled=True, axis_index_groups=Z_CORES
-    ).reshape(C_COARSE, part_coarse)
+    gathered = with_layout_constraint(gathered, Layout(major_to_minor=(0, 1, 2)))
     flat = gathered.reshape(C_COARSE, -1)
     conv1_w = flat[:, :960]
     up_w = flat[:, 960:1152]
     up_turned_w = flat[:, 1152:1344].reshape(NT, part_coarse, 192)
+    out_t = flat[:, 1344:1536]
     conv2_w = (
-        gathered[:, :, 1344:1584]
+        gathered[:, :, 1536:1776]
         .reshape(2, 32, 2, 12, 240)
         .transpose(0, 1, 3, 2, 4)
         .reshape(C_FINE, 480)
@@ -96,19 +106,29 @@
 
     trunk_ext = neighbours(trunk, 4)
     skip_ext = neighbours(skip, 4)
-    cot_ext = neighbours(cotangent, 6)
+    cot_ext = neighbours(cotangent, 8)
     fine_rows = 2 * slab + 8
     index = place * 2 * slab - 4 + lax.broadcasted_iota(jnp.int32, (1, fine_rows, 1), 1)
     inside = (index >= 0) & (index < 2 * slab * lax.axis_size("seq"))
 
-    partial = dot_t(trunk_ext, out_t).astype(BF16)
-    projected = jnp.sum(exchange(split(partial)).astype(F32), axis=0).astype(BF16)
+    both = share(
+        jnp.concatenate([trunk_ext, cot_ext.reshape(seqs, slab + 8, 2 * part_fine)], axis=0)
+    )
+    trunk_blocks = both[:, :seqs]
+    cot_blocks = both[:, seqs:].reshape(NT, seqs, 2 * slab + 16, part_fine)
+    cot_blocks = cot_blocks[:, :, 4 : 4 + fine_rows]
+    out_turned = lax.all_gather(
+        paired[:, :, :192], "seq", axis=1, tiled=True, axis_index_groups=Z_CORES
+    ).reshape(NT, part_coarse, 192)
+    projected = lax.dot_general(
+        trunk_blocks, out_turned, (((0, 3), (0, 2)), ((), ())), preferred_element_type=F32
+    ).astype(BF16)
     projected_full = lanes(share(projected)).astype(F32)
     scale_coarse = lax.rsqrt(
         jnp.mean(projected_full * projected_full, axis=-1, keepdims=True) + EPS
     )
     act_coarse = jax.nn.gelu(projected_full * scale_coarse * gain_coarse).astype(BF16)
-    cot_full = lanes(share(cot_ext[:, 2 : 2 + fine_rows]))
+    cot_full = lanes(cot_blocks)
 
     taps = dot(act_coarse, conv1_w)
     rows = slab + 4
@@ -117,7 +137,7 @@
     )
     lifted = (projected[:, 2 : 2 + rows].astype(F32) + mixed).astype(BF16)
 
-    stacked = jnp.concatenate([cot_ext[:, 4 - k : 4 - k + fine_rows] for k in range(5)], axis=2)
+    stacked = jnp.concatenate([cot_ext[:, 6 - k : 6 - k + fine_rows] for k in range(5)], axis=2)
     back_partial = split(dot_t(stacked, conv2_w).astype(BF16))
     first = exchange(
         jnp.concatenate(
@@ -147,9 +167,10 @@
         inside, cot_full.astype(F32) + pull(back_fine)[0], 0.0
     ).astype(BF16)
     folded = skip_grad_full.reshape(seqs, rows, 2, NT, part_fine)
-    lifted_grad = sum(
-        dot_t(folded[:, :, :, t].reshape(seqs, rows, 2 * part_fine), up_turned_w[t])
-        for t in range(NT)
+    lifted_grad = lax.dot_general(
+        folded, up_turned_w.reshape(NT, part_coarse, 2, part_fine),
+        (((2, 3, 4), (2, 0, 3)), ((), ())),
+        preferred_element_type=F32,
     ).astype(BF16)
     stacked_grad = jnp.concatenate(
         [lifted_grad[:, 4 - k : 4 - k + slab] for k in range(5)], axis=2
@@ -202,6 +223,7 @@
         P(None, "seq", "tensor"),
     )
     out_specs = (P(None, "seq", "tensor"), P(None, "seq", "tensor"), P(None, "seq", "tensor"))
+
     return jax.shard_map(
         per_device, mesh=mesh, in_specs=in_specs, out_specs=out_specs, check_vma=False
     )

time: 254 us -> 234 us (0.921)
  the two profiles are of different devices: /device:TPU:32 before, /device:TPU:8 now
where the time goes in v2:
time: 234 us; the launch traced here: 233 us
  starting transfers between devices  64.7 us (28%)
  waiting for transfers between devices  46.2 us (20%)
  local copies, waits for them, and re-layouts  39.9 us (17%)
  blocking collectives  36.1 us (15%)
  other arithmetic  18.2 us (8%)
  between operations  14.7 us (6%)
  matrix products  12.8 us (5%)
    all_to_all x6, waiting for transfers between devices, exchange(): return lax.all_to_all(blocks, 'tensor', 0, 0)  39.7 us
    all_to_all x6, starting transfers between devices, exchange(): return lax.all_to_all(blocks, 'tensor', 0, 0)  32.7 us
    all_gather x1, blocking collectives, per_device(): lax.all_gather(paired[:, :, :192], 'seq', axis=1, tiled=True, axis_index_...  30.9 us
    ppermute x3, starting transfers between devices, neighbours(): after = lax.ppermute(shard[:, :width], 'seq', down)  20.9 us
    dot_general x4, matrix products, dot(): lax.dot_general(left, right, (((left.ndim - 1,), (0,)), ((), ())), prefer...  8.45 us
    ppermute x3, starting transfers between devices, neighbours(): before = lax.ppermute(shard[:, length - width:], 'seq', up)  6.25 us
    all_gather x1, blocking collectives, per_device(): paired = lax.all_gather(packed, 'seq', axis=0, axis_index_groups=Y_PAIRS)  5.29 us
    ppermute x3, waiting for transfers between devices, neighbours(): before = lax.ppermute(shard[:, length - width:], 'seq', up)  5.05 us
  transfers between devices with their start and end apart: 14, of which 7 were waited for; matrix products, arithmetic and copies ran while one was open for 13% of the time, Pallas kernels for 0%

profile of v2, /device:TPU:8, one launch (start us, length us, event | category | flops | bytes accessed | tf_op | source)
XLA Modules:
  0.0 232.6 jit_solution(10196816001869931320)
XLA Ops:
  7.2 0.8 reshape.179
  8.0 0.8 pad_maximum_fusion.4
  8.8 4.8 %collective-permute-start.4 = (bf16[24,384]{1,0:T(8,128)(2,1)S(1)}, bf16[24,384]{1,0:T(8,128)(2,1)S(1)}, u32[]{:S(2)}, u32[]{:S(2)}) collective-permute-start(bf16[24,384]{1,0:T(8,128)(2,1)S(1)} %pad_maximum_fusion.4), channel_id=1, source_target_pairs={{0,0},{1,64},{2,128},{3,192},{4,256},{5,320},{6,384},{7,448},{8,8}... | collective-permute-start | bytes 55304 | tf_op jit(solution)/shard_map/ppermute | solution.py:72
  13.6 0.7 copy.200
  14.5 0.9 copy.199
  15.5 1.3 collective-permute-done.4
  16.9 0.8 concatenate.41
  17.8 5.3 %all-gather = bf16[48,1984]{1,0:T(8,128)(2,1)S(1)} all-gather(bf16[24,1984]{1,0:T(8,128)(2,1)S(1)} %concatenate.41), channel_id=2, replica_groups={{0,256},{8,264},{16,272},{24,280},{32,288},{40,296},{48,304},{56,312},{..., dimensions={0}, use_global_device_ids=true | all-gather | bytes 285696 | tf_op jit(solution)/shard_map/all_gather | solution.py:90
  23.0 0.8 slice.217
  24.0 13.2 %collective-permute-start.3 = (bf16[2,8,96]{2,1,0:T(8,128)(2,1)S(1)}, bf16[2,8,96]{2,1,0:T(8,128)(2,1)S(1)}, u32[]{:S(2)}, u32[]{:S(2)}) collective-permute-start(bf16[2,8,96]{2,1,0:T(8,128)(2,1)S(1)} %get-tuple-element.55), channel_id=1, source_target_pairs={{8,0},{16,8},{24,16},{32,24},{40,32},{48,40},{56,48},{64,56},{72,6... | collective-permute-start | bytes 9224 | tf_op jit(solution)/shard_map/ppermute | solution.py:45
  37.2 1.9 collective-permute-start.2
  39.2 5.8 %collective-permute-start.1 = (bf16[2,4,192]{2,1,0:T(4,128)(2,1)S(1)}, bf16[2,4,192]{2,1,0:T(4,128)(2,1)S(1)}, u32[]{:S(2)}, u32[]{:S(2)}) collective-permute-start(bf16[2,4,192]{2,1,0:T(4,128)(2,1)S(1)} %get-tuple-element.53), channel_id=1, source_target_pairs={{8,0},{16,8},{24,16},{32,24},{40,32},{48,40},{56,48},{64,56},{72,6... | collective-permute-start | bytes 9224 | tf_op jit(solution)/shard_map/ppermute | solution.py:45
  45.0 1.9 collective-permute-start
  47.0 5.0 %collective-permute-done = bf16[2,4,192]{2,1,0:T(4,128)(2,1)S(1)} collective-permute-done((bf16[2,4,192]{2,1,0:T(4,128)(2,1)S(1)}, bf16[2,4,192]{2,1,0:T(4,128)(2,1)S(1)}, u32[]{:S(2)}, u32[]{:S(2)}) %collective-permute-start) | collective-permute-done | bytes 3104 | tf_op jit(solution)/shard_map/ppermute | solution.py:44
  52.1 1.1 broadcast_in_dim.80
  53.3 9.5 %all-to-all-start = ((bf16[8,4,72,192]{3,2,1,0:T(8,128)(2,1)}), bf16[8,4,72,192]{3,2,1,0:T(8,128)(2,1)S(1)}, u32[]{:S(2)}, u32[]{:S(2)}) async-start(bf16[8,4,72,192]{3,2,1,0:T(8,128)(2,1)} %broadcast_in_dim.80), calls=%async_computation | async-start | bytes 2359296 | tf_op jit(solution)/shard_map/all_to_all | solution.py:33
  62.8 30.9 %all_gather.14 = bf16[2,768,192]{2,1,0:T(8,128)(2,1)S(1)} all-gather(bf16[2,24,192]{2,1,0:T(8,128)(2,1)S(1)} %slice.215), channel_id=1, replica_groups={{0,8,16,24,32,40,48,56,64,72,80,88,96,104,112,120,128,136,144,152,160,1..., dimensions={1}, use_global_device_ids=true | all-gather | bytes 608256 | tf_op jit(solution)/shard_map/all_gather | solution.py:120
  94.1 0.9 broadcast_in_dim.82
  95.0 7.3 %all-to-all-start.1 = ((bf16[8,2,72,192]{3,2,1,0:T(8,128)(2,1)}), bf16[8,2,72,192]{3,2,1,0:T(8,128)(2,1)S(1)}, u32[]{:S(2)}, u32[]{:S(2)}) async-start(bf16[8,2,72,192]{3,2,1,0:T(8,128)(2,1)} %broadcast_in_dim.82), calls=%async_computation.1 | async-start | bytes 1179648 | tf_op jit(solution)/shard_map/all_to_all | solution.py:33
  102.3 0.9 concatenate.42
  103.2 10.8 %all-to-all-done.1 = bf16[8,2,72,192]{3,2,1,0:T(8,128)(2,1)S(1)} async-done(((bf16[8,2,72,192]{3,2,1,0:T(8,128)(2,1)}), bf16[8,2,72,192]{3,2,1,0:T(8,128)(2,1)S(1)}, u32[]{:S(2)}, u32[]{:S(2)}) %all-to-all-start.1) | async-done | bytes 442400 | tf_op jit(solution)/shard_map/all_to_all | solution.py:33
  114.2 0.7 copy.201
  114.9 1.3 reshape.193
  116.5 1.1 slice-done
  117.6 0.8 copy.203
  118.4 0.6 copy.204
  121.7 3.1 %fusion = f32[2,72,960]{2,1,0:T(8,128)S(1)} fusion(bf16[1536,1792]{1,0:T(8,128)(2,1)} %bitcast.123, f32[2,72,1536]{2,1,0:T(8,128)} %reshape.193, f32[1536]{0:T(1024)S(1)} %copy-done.14, f32[2,72]{1,0:T(2,128)S(1)} %get-tuple-element.63), kind=kOutput, calls=%fused_computation.2 | convolution fusion | flops 427106304 | bytes 4590144 | tf_op jit(solution)/shard_map/dot_general | solution.py:18
  125.2 1.5 copy.207
  126.7 3.8 %all-to-all-start.2 = ((bf16[8,4,68,192]{3,1,2,0:T(4,128)(2,1)}), bf16[8,4,68,192]{3,1,2,0:T(4,128)(2,1)S(1)}, u32[]{:S(2)}, u32[]{:S(2)}) async-start(bf16[8,4,68,192]{3,1,2,0:T(4,128)(2,1)} %copy.207), calls=%async_computation.2 | async-start | bytes 2228224 | tf_op jit(solution)/shard_map/all_to_all | solution.py:33
  130.7 1.9 collective-permute-start.6
  132.6 2.4 %collective-permute-start.5 = (bf16[2,4,96]{2,1,0:T(4,128)(2,1)S(1)}, bf16[2,4,96]{2,1,0:T(4,128)(2,1)S(1)}, u32[]{:S(2)}, u32[]{:S(2)}) collective-permute-start(bf16[2,4,96]{2,1,0:T(4,128)(2,1)S(1)} %get-tuple-element.50), channel_id=1, source_target_pairs={{0,8},{8,16},{16,24},{24,32},{32,40},{40,48},{48,56},{56,64},{64,7... | collective-permute-start | bytes 4616 | tf_op jit(solution)/shard_map/ppermute | solution.py:44
  135.0 11.6 %all-to-all-done.2 = bf16[8,4,68,192]{3,1,2,0:T(4,128)(2,1)S(1)} async-done(((bf16[8,4,68,192]{3,1,2,0:T(4,128)(2,1)}), bf16[8,4,68,192]{3,1,2,0:T(4,128)(2,1)S(1)}, u32[]{:S(2)}, u32[]{:S(2)}) %all-to-all-start.2) | async-done | bytes 835616 | tf_op jit(solution)/shard_map/all_to_all | solution.py:33
  146.6 1.0 slice_bitcast_fusion.7
  148.3 1.7 fusion.43
  150.4 1.2 broadcast_in_dim.85
  151.5 4.3 %all-to-all-start.3 = ((bf16[8,4,136,96]{3,2,1,0:T(8,128)(2,1)}), bf16[8,4,136,96]{3,2,1,0:T(8,128)(2,1)S(1)}, u32[]{:S(2)}, u32[]{:S(2)}) async-start(bf16[8,4,136,96]{3,2,1,0:T(8,128)(2,1)} %broadcast_in_dim.85), calls=%async_computation.3 | async-start | bytes 2228224 | tf_op jit(solution)/shard_map/all_to_all | solution.py:33
  156.3 0.9 slice.242
  157.2 1.5 reshape.191
  159.2 1.3 reshape.194
  160.5 2.1 slice.249
  162.6 2.1 slice.251
  164.7 3.1 %reshape.211 = bf16[8,192,2,96]{3,2,1,0:T(2,128)(2,1)} reshape(bf16[1536,192]{1,0:T(8,128)(2,1)} %slice.251) | data formatting | bytes 1179648 | tf_op jit(solution)/shard_map/reshape;reshape | solution.py:171
  167.8 4.1 %all-to-all-done.3 = bf16[8,4,136,96]{3,2,1,0:T(8,128)(2,1)S(1)} async-done(((bf16[8,4,136,96]{3,2,1,0:T(8,128)(2,1)}), bf16[8,4,136,96]{3,2,1,0:T(8,128)(2,1)S(1)}, u32[]{:S(2)}, u32[]{:S(2)}) %all-to-all-start.3) | async-done | bytes 835616 | tf_op jit(solution)/shard_map/all_to_all | solution.py:33
  171.9 1.0 multiply_reduce_fusion
  173.0 1.9 copy_convert_fusion
  174.9 4.4 %fusion.12 = (f32[2,136]{1,0:T(2,128)S(1)}, bf16[2,136,8,96]{3,2,1,0:T(8,128)(2,1)}) fusion(f32[8,96]{1,0:T(8,128)S(1)} %mul.394, f32[2,136]{1,0:T(2,128)S(1)} %get-tuple-element.61, bf16[8,2,136,96]{3,2,1,0:T(8,128)(2,1)S(1)} %get-tuple-element.29, bf16[8,2,136,96]{3,2,1,0:T(8,128)(2,1)S(1)} %get-tuple-element.28), kind=kLoop, calls=%fused_computation.29 | loop fusion | flops 5848816 | bytes 1258624 | tf_op jit(solution)/shard_map/transpose(jvp())/reduce_sum | solution.py:162
  179.3 2.3 convert_element_type.200
  181.9 3.0 %fusion.23 = bf16[2,68,2,8,96]{4,3,2,1,0:T(8,128)(2,1)S(1)} fusion(f32[2,68,2,8,96]{4,3,2,1,0:T(8,128)S(1)} %bitcast.118, f32[2,68,2,8,96]{4,3,2,1,0:T(8,128)} %bitcast.120, f32[2,68,2,8,96]{4,3,2,1,0:T(8,128)S(1)} %bitcast.119, f32[2,68,2]{2,1,0:T(8,128)S(1)} %get-tuple-element.44, f32[8,96]{1,0:T(8,128)S(1)} %mul.394, ...), kind=kLoop, calls=%fused_computation.40 | loop fusion | flops 6057984 | bytes 2929928 | tf_op jit(solution)/shard_map/convert_element_type | solution.py:168
  185.6 3.1 %convolution_convert_fusion = bf16[2,64,1536]{2,1,0:T(8,128)(2,1)S(1)} fusion(bf16[2,64,960]{2,1,0:T(8,128)(2,1)S(1)} %concatenate.46, bf16[1536,1792]{1,0:T(8,128)(2,1)} %bitcast.126), kind=kOutput, calls=%fused_computation.1 | convolution fusion | flops 377683968 | bytes 3784704 | tf_op jit(solution)/shard_map/dot_general | solution.py:24
  189.1 0.9 copy.266
  190.0 4.2 %all-to-all-start.4 = ((bf16[8,2,64,192]{3,2,1,0:T(8,128)(2,1)}), bf16[8,2,64,192]{3,2,1,0:T(8,128)(2,1)}, u32[]{:S(2)}, u32[]{:S(2)}) async-start(bf16[8,2,64,192]{3,2,1,0:T(8,128)(2,1)} %bitcast.117), calls=%async_computation.4 | async-start | bytes 1048576 | tf_op jit(solution)/shard_map/all_to_all | solution.py:33
  194.2 1.3 fusion.44
  195.9 0.9 copy-done
  197.1 1.6 fusion.40
  198.7 6.1 %all-to-all-done.4 = bf16[8,2,64,192]{3,2,1,0:T(8,128)(2,1)} async-done(((bf16[8,2,64,192]{3,2,1,0:T(8,128)(2,1)}), bf16[8,2,64,192]{3,2,1,0:T(8,128)(2,1)}, u32[]{:S(2)}, u32[]{:S(2)}) %all-to-all-start.4) | async-done | bytes 393248 | tf_op jit(solution)/shard_map/all_to_all | solution.py:33
  204.9 1.1 convert_reduce_fusion
  206.7 0.9 broadcast_in_dim.93
  207.6 3.5 %all-to-all-start.5 = ((bf16[8,2,64,256]{3,2,1,0:T(8,128)(2,1)}), bf16[8,2,64,256]{3,2,1,0:T(8,128)(2,1)S(1)}, u32[]{:S(2)}, u32[]{:S(2)}) async-start(bf16[8,2,64,256]{3,2,1,0:T(8,128)(2,1)} %broadcast_in_dim.93), calls=%async_computation.5 | async-start | bytes 1048576 | tf_op jit(solution)/shard_map/all_to_all | solution.py:33
  211.5 0.7 copy.228
  212.4 1.2 fusion.75
  213.7 0.7 copy.229
  214.4 7.1 %all-to-all-done.5 = bf16[8,2,64,256]{3,2,1,0:T(8,128)(2,1)S(1)} async-done(((bf16[8,2,64,256]{3,2,1,0:T(8,128)(2,1)}), bf16[8,2,64,256]{3,2,1,0:T(8,128)(2,1)S(1)}, u32[]{:S(2)}, u32[]{:S(2)}) %all-to-all-start.5) | async-done | bytes 524320 | tf_op jit(solution)/shard_map/all_to_all | solution.py:33
  221.6 0.6 copy.226
  223.4 2.4 %convolution_convert_fusion.2 = bf16[2,64,192]{2,1,0:T(8,128)(2,1)} fusion(bf16[1536,1792]{1,0:T(8,128)(2,1)} %bitcast.127, f32[2,64,1536]{2,1,0:T(8,128)S(1)} %reshape.200, f32[2,72,1536]{2,1,0:T(8,128)S(1)} %copy-done.8, f32[2,64]{1,0:T(2,128)S(1)} %fusion.80), kind=kOutput, calls=%fused_computation.20 | convolution fusion | flops 76111872 | bytes 2409472 | tf_op jit(solution)/shard_map/dot_general | solution.py:18
  (112 shorter events, 11.3 us)
Async XLA Ops:
  7.2 16.7 %copy-start.11 = (bf16[2,128,96]{1,2,0:T(8,128)(2,1)S(1)}, bf16[2,128,96]{1,2,0:T(8,128)(2,1)}, u32[]{:S(2)}) copy-start(bf16[2,128,96]{1,2,0:T(8,128)(2,1)} %param.17) | copy-start | bytes 147460
  7.2 32.0 %copy-start.10 = (bf16[2,64,192]{2,1,0:T(8,128)(2,1)S(1)}, bf16[2,64,192]{2,1,0:T(8,128)(2,1)}, u32[]{:S(2)}) copy-start(bf16[2,64,192]{2,1,0:T(8,128)(2,1)} %param.9) | copy-start | bytes 147460
  7.2 109.3 %all-gather.3.cloned.1.call-start = ((), (), s32[]{:S(2)}) async-start(), calls=%async_computation.6 | async-start | bytes 5677056 | tf_op jit(solution)/shard_map/all_gather | solution.py:91
  8.8 8.0 %collective-permute-start.4 = (bf16[24,384]{1,0:T(8,128)(2,1)S(1)}, bf16[24,384]{1,0:T(8,128)(2,1)S(1)}, u32[]{:S(2)}, u32[]{:S(2)}) collective-permute-start(bf16[24,384]{1,0:T(8,128)(2,1)S(1)} %pad_maximum_fusion.4), channel_id=1, source_target_pairs={{0,0},{1,64},{2,128},{3,192},{4,256},{5,320},{6,384},{7,448},{8,8}... | collective-permute-start | bytes 55304 | tf_op jit(solution)/shard_map/ppermute | solution.py:72
  24.0 22.9 %collective-permute-start.3 = (bf16[2,8,96]{2,1,0:T(8,128)(2,1)S(1)}, bf16[2,8,96]{2,1,0:T(8,128)(2,1)S(1)}, u32[]{:S(2)}, u32[]{:S(2)}) collective-permute-start(bf16[2,8,96]{2,1,0:T(8,128)(2,1)S(1)} %get-tuple-element.55), channel_id=1, source_target_pairs={{8,0},{16,8},{24,16},{32,24},{40,32},{48,40},{56,48},{64,56},{72,6... | collective-permute-start | bytes 9224 | tf_op jit(solution)/shard_map/ppermute | solution.py:45
  37.2 9.7 %collective-permute-start.2 = (bf16[2,8,96]{2,1,0:T(8,128)(2,1)S(1)}, bf16[2,8,96]{2,1,0:T(8,128)(2,1)S(1)}, u32[]{:S(2)}, u32[]{:S(2)}) collective-permute-start(bf16[2,8,96]{2,1,0:T(8,128)(2,1)S(1)} %get-tuple-element.54), channel_id=1, source_target_pairs={{0,8},{8,16},{16,24},{24,32},{32,40},{40,48},{48,56},{56,64},{64,7... | collective-permute-start | bytes 9224 | tf_op jit(solution)/shard_map/ppermute | solution.py:44
  39.2 7.8 %collective-permute-start.1 = (bf16[2,4,192]{2,1,0:T(4,128)(2,1)S(1)}, bf16[2,4,192]{2,1,0:T(4,128)(2,1)S(1)}, u32[]{:S(2)}, u32[]{:S(2)}) collective-permute-start(bf16[2,4,192]{2,1,0:T(4,128)(2,1)S(1)} %get-tuple-element.53), channel_id=1, source_target_pairs={{8,0},{16,8},{24,16},{32,24},{40,32},{48,40},{56,48},{64,56},{72,6... | collective-permute-start | bytes 9224 | tf_op jit(solution)/shard_map/ppermute | solution.py:45
  45.0 7.1 %collective-permute-start = (bf16[2,4,192]{2,1,0:T(4,128)(2,1)S(1)}, bf16[2,4,192]{2,1,0:T(4,128)(2,1)S(1)}, u32[]{:S(2)}, u32[]{:S(2)}) collective-permute-start(bf16[2,4,192]{2,1,0:T(4,128)(2,1)S(1)} %get-tuple-element.52), channel_id=1, source_target_pairs={{0,8},{8,16},{16,24},{24,32},{32,40},{40,48},{48,56},{56,64},{64,7... | collective-permute-start | bytes 9224 | tf_op jit(solution)/shard_map/ppermute | solution.py:44
  53.3 40.4 %all-to-all-start = ((bf16[8,4,72,192]{3,2,1,0:T(8,128)(2,1)}), bf16[8,4,72,192]{3,2,1,0:T(8,128)(2,1)S(1)}, u32[]{:S(2)}, u32[]{:S(2)}) async-start(bf16[8,4,72,192]{3,2,1,0:T(8,128)(2,1)} %broadcast_in_dim.80), calls=%async_computation | async-start | bytes 2359296 | tf_op jit(solution)/shard_map/all_to_all | solution.py:33
  94.1 0.9 copy-start.4
  95.0 19.1 %all-to-all-start.1 = ((bf16[8,2,72,192]{3,2,1,0:T(8,128)(2,1)}), bf16[8,2,72,192]{3,2,1,0:T(8,128)(2,1)S(1)}, u32[]{:S(2)}, u32[]{:S(2)}) async-start(bf16[8,2,72,192]{3,2,1,0:T(8,128)(2,1)} %broadcast_in_dim.82), calls=%async_computation.1 | async-start | bytes 1179648 | tf_op jit(solution)/shard_map/all_to_all | solution.py:33
  116.5 1.1 slice-start
  119.0 1.0 copy-start.7
  121.0 0.7 copy-start.14
  121.7 3.1 %copy-start.5 = (bf16[2,72,192]{2,1,0:T(8,128)(2,1)S(1)}, bf16[2,72,192]{2,1,0:T(8,128)(2,1)}, u32[]{:S(2)}) copy-start(bf16[2,72,192]{2,1,0:T(8,128)(2,1)} %copy-done.4) | copy-start | bytes 165892
  126.7 3.8 %copy-start.12 = (bf16[2,128,96]{1,2,0:T(8,128)(2,1)S(1)}, bf16[2,128,96]{1,2,0:T(8,128)(2,1)}, u32[]{:S(2)}) copy-start(bf16[2,128,96]{1,2,0:T(8,128)(2,1)} %param.14) | copy-start | bytes 147460
  126.7 19.9 %all-to-all-start.2 = ((bf16[8,4,68,192]{3,1,2,0:T(4,128)(2,1)}), bf16[8,4,68,192]{3,1,2,0:T(4,128)(2,1)S(1)}, u32[]{:S(2)}, u32[]{:S(2)}) async-start(bf16[8,4,68,192]{3,1,2,0:T(4,128)(2,1)} %copy.207), calls=%async_computation.2 | async-start | bytes 2228224 | tf_op jit(solution)/shard_map/all_to_all | solution.py:33
  130.7 19.5 %collective-permute-start.6 = (bf16[2,4,96]{2,1,0:T(4,128)(2,1)S(1)}, bf16[2,4,96]{2,1,0:T(4,128)(2,1)S(1)}, u32[]{:S(2)}, u32[]{:S(2)}) collective-permute-start(bf16[2,4,96]{2,1,0:T(4,128)(2,1)S(1)} %get-tuple-element.51), channel_id=1, source_target_pairs={{8,0},{16,8},{24,16},{32,24},{40,32},{48,40},{56,48},{64,56},{72,6... | collective-permute-start | bytes 4616 | tf_op jit(solution)/shard_map/ppermute | solution.py:45
  132.6 17.6 %collective-permute-start.5 = (bf16[2,4,96]{2,1,0:T(4,128)(2,1)S(1)}, bf16[2,4,96]{2,1,0:T(4,128)(2,1)S(1)}, u32[]{:S(2)}, u32[]{:S(2)}) collective-permute-start(bf16[2,4,96]{2,1,0:T(4,128)(2,1)S(1)} %get-tuple-element.50), channel_id=1, source_target_pairs={{0,8},{8,16},{16,24},{24,32},{32,40},{40,48},{48,56},{56,64},{64,7... | collective-permute-start | bytes 4616 | tf_op jit(solution)/shard_map/ppermute | solution.py:44
  151.5 4.4 %copy-start.13 = (f32[768]{0:T(1024)S(1)}, f32[768]{0:T(1024)}, u32[]{:S(2)}) copy-start(f32[768]{0:T(1024)} %param.15) | copy-start | bytes 9220
  151.5 20.3 %all-to-all-start.3 = ((bf16[8,4,136,96]{3,2,1,0:T(8,128)(2,1)}), bf16[8,4,136,96]{3,2,1,0:T(8,128)(2,1)S(1)}, u32[]{:S(2)}, u32[]{:S(2)}) async-start(bf16[8,4,136,96]{3,2,1,0:T(8,128)(2,1)} %broadcast_in_dim.85), calls=%async_computation.3 | async-start | bytes 2228224 | tf_op jit(solution)/shard_map/all_to_all | solution.py:33
  181.9 3.1 %copy-start.9 = (bf16[8,192,2,96]{3,2,1,0:T(2,128)(2,1)S(1)}, bf16[8,192,2,96]{3,2,1,0:T(2,128)(2,1)}, u32[]{:S(2)}) copy-start(bf16[8,192,2,96]{3,2,1,0:T(2,128)(2,1)} %reshape.211) | copy-start | bytes 1769476
  189.1 5.1 %copy-start.6 = (bf16[2,136,768]{2,1,0:T(8,128)(2,1)S(1)}, bf16[2,136,768]{2,1,0:T(8,128)(2,1)}, u32[]{:S(2)}) copy-start(bf16[2,136,768]{2,1,0:T(8,128)(2,1)} %convert_element_type.200) | copy-start | bytes 1253380
  190.0 14.9 %all-to-all-start.4 = ((bf16[8,2,64,192]{3,2,1,0:T(8,128)(2,1)}), bf16[8,2,64,192]{3,2,1,0:T(8,128)(2,1)}, u32[]{:S(2)}, u32[]{:S(2)}) async-start(bf16[8,2,64,192]{3,2,1,0:T(8,128)(2,1)} %bitcast.117), calls=%async_computation.4 | async-start | bytes 1048576 | tf_op jit(solution)/shard_map/all_to_all | solution.py:33
  194.2 1.3 copy-start.1
  195.5 1.2 copy-start
  206.2 4.9 %copy-start.3 = (f32[2,136,480]{2,1,0:T(8,128)S(1)}, f32[2,136,480]{2,1,0:T(8,128)}, u32[]{:S(2)}) copy-start(f32[2,136,480]{2,1,0:T(8,128)} %fusion.44) | copy-start | bytes 1566724
  207.6 13.9 %all-to-all-start.5 = ((bf16[8,2,64,256]{3,2,1,0:T(8,128)(2,1)}), bf16[8,2,64,256]{3,2,1,0:T(8,128)(2,1)S(1)}, u32[]{:S(2)}, u32[]{:S(2)}) async-start(bf16[8,2,64,256]{3,2,1,0:T(8,128)(2,1)} %broadcast_in_dim.93), calls=%async_computation.5 | async-start | bytes 1048576 | tf_op jit(solution)/shard_map/all_to_all | solution.py:33
  211.1 1.2 copy-start.2
  222.2 1.2 copy-start.8
Sparse Core Ops, SparseCore 0:
  24.0 87.0 all-gather.2

commit v3 on v2

--- a/solution.py
+++ b/solution.py
@@ -1,12 +1,17 @@
+import math
+
 import jax
 import jax.numpy as jnp
 from jax import lax
+from jax.experimental import pallas as pl
 from jax.experimental.layout import Layout, with_layout_constraint
+from jax.experimental.pallas import tpu as pltpu
 from jax.sharding import PartitionSpec as P
 
 C_COARSE = 1536
 C_FINE = 768
 EPS = 1e-06
+SQRT_2_PI = math.sqrt(2.0 / math.pi)
 BF16 = jnp.bfloat16
 F32 = jnp.float32
 NT = 8
@@ -53,6 +58,86 @@
 
 def split(full):
     return jnp.moveaxis(full.reshape(full.shape[:2] + (NT, -1)), 2, 0)
+
+
+def fine_adjoint(shared_ref, cot_ref, gain_ref, inside_ref, up_ref, conv_ref, back_ref, grad_ref, lifted_ref, norm_ref, rows_ref, taps_ref):
+    slab, rows = back_ref.shape[2], rows_ref.shape[1]
+    for p in range(2):
+        square = jnp.zeros(shared_ref.shape[2:], F32)
+        for t in range(NT):
+            value = shared_ref[t, p].astype(F32)
+            square = square + value * value
+        mean = jnp.sum(square, axis=-1, keepdims=True) * (1.0 / C_FINE)
+        scale = lax.rsqrt(mean + EPS)
+        weighted = jnp.zeros(shared_ref.shape[2:], F32)
+        for t in range(NT):
+            value = shared_ref[t, p].astype(F32)
+            gain = gain_ref[t]
+            inner = slope(value * scale * gain) * shared_ref[t, 2 + p].astype(F32) * gain
+            weighted = weighted + inner * value
+            norm_ref[t] = inner * scale
+        total = jnp.sum(weighted, axis=-1, keepdims=True)
+        factor = scale * scale * scale * total * (1.0 / C_FINE)
+        keep = inside_ref[p] > 0.0
+        lifted = jnp.zeros((shared_ref.shape[2], up_ref.shape[2]), F32)
+        for t in range(NT):
+            value = shared_ref[t, p].astype(F32)
+            grad = cot_ref[t, p].astype(F32) + (norm_ref[t] - value * factor)
+            grad = jnp.where(keep, grad, 0.0).astype(BF16)
+            grad_ref[t, p] = grad
+            lifted = lifted + dot_t(grad, up_ref[p, t])
+        if p == 0:
+            first = lifted
+        else:
+            lifted = (first + lifted).astype(BF16).astype(F32)
+    for s in range(2):
+        rows_ref[s] = lifted[s * rows : (s + 1) * rows]
+        lifted_ref[s] = rows_ref[s, 2 : 2 + slab, :192].astype(BF16)
+        for k in range(5):
+            taps_ref[s * slab : (s + 1) * slab, k * 128 : (k + 1) * 128] = rows_ref[
+                s, 4 - k : 4 - k + slab, :128
+            ].astype(BF16)
+        for k in (0, 2, 4):
+            tail = rows_ref[s, 4 - k : 4 - k + slab, 128:256]
+            if k < 4:
+                tail = tail + pltpu.roll(rows_ref[s, 3 - k : 3 - k + slab, 128:256], 64, 1)
+            taps_ref[s * slab : (s + 1) * slab, 640 + k * 64 : 768 + k * 64] = tail.astype(BF16)
+    for t in range(NT):
+        back = dot_t(taps_ref[...], conv_ref[192 * t : 192 * (t + 1), :]).astype(BF16)
+        for s in range(2):
+            back_ref[t, s] = back[s * slab : (s + 1) * slab]
+
+
+def slope(value):
+    square = value * value
+    bend = jnp.tanh(SQRT_2_PI * (value + 0.044715 * (square * value)))
+    half = 0.5 * (1.0 + bend)
+    return half + 0.5 * value * (1.0 - bend * bend) * (
+        SQRT_2_PI * (1.0 + (3 * 0.044715) * square)
+    )
+
+
+def run_fine_adjoint(shared, cot, gain, inside, up_phases, flat, slab):
+    whole = pl.BlockSpec(memory_space=pltpu.VMEM)
+    rows = shared.shape[2] // 2
+    return pl.pallas_call(
+        fine_adjoint,
+        grid=(1,),
+        in_specs=[whole] * 5 + [pl.BlockSpec((C_COARSE, 1024), lambda i: (0, 0))],
+        out_specs=[whole] * 3,
+        out_shape=[
+            jax.ShapeDtypeStruct((NT, 2, slab, 192), BF16),
+            jax.ShapeDtypeStruct(cot.shape, BF16),
+            jax.ShapeDtypeStruct((2, slab, 192), BF16),
+        ],
+        scratch_shapes=[
+            pltpu.VMEM((NT,) + shared.shape[2:], F32),
+            pltpu.VMEM((2, rows, 256), F32),
+            pltpu.VMEM((2 * slab, 1024), BF16),
+        ],
+        compiler_params=pltpu.CompilerParams(vmem_limit_bytes=40 * 2**20),
+        name="fine_adjoint",
+    )(shared, cot, gain, inside, up_phases, flat)
 
 
 def per_device(trunk, w_out, gain_coarse, w_conv1, w_up, skip, gain_fine, w_conv2, cotangent):
@@ -72,18 +157,23 @@
     both_turned = lax.ppermute(
         jnp.concatenate([out_shard, up_shard], axis=1), ("seq", "tensor"), turned
     )
-    conv1_shard = jnp.transpose(w_conv1, (1, 0, 2)).reshape(24, 960)
+    conv1_turned = jnp.transpose(w_conv1, (1, 0, 2))
+    conv1_shard = jnp.concatenate(
+        [conv1_turned[:, :, :128].reshape(24, 640), conv1_turned[:, :, 128:].reshape(24, 320)],
+        axis=1,
+    )
     conv2_flat = jnp.transpose(w_conv2, (1, 0, 2)).reshape(12, 480)
     conv2_shard = jnp.concatenate([conv2_flat[:, :240], conv2_flat[:, 240:]], axis=0)
     packed = jnp.concatenate(
         [
             both_turned[:, :192],
             conv1_shard,
+            jnp.zeros((24, 64), BF16),
             up_shard,
             both_turned[:, 192:],
             out_shard,
             conv2_shard,
-            jnp.zeros((24, 16), BF16),
+            jnp.zeros((24, 80), BF16),
         ],
         axis=1,
     )
@@ -94,11 +184,11 @@
     gathered = with_layout_constraint(gathered, Layout(major_to_minor=(0, 1, 2)))
     flat = gathered.reshape(C_COARSE, -1)
     conv1_w = flat[:, :960]
-    up_w = flat[:, 960:1152]
-    up_turned_w = flat[:, 1152:1344].reshape(NT, part_coarse, 192)
-    out_t = flat[:, 1344:1536]
+    up_w = flat[:, 1024:1216]
+    up_turned_w = flat[:, 1216:1408].reshape(NT, part_coarse, 192)
+    out_t = flat[:, 1408:1600]
     conv2_w = (
-        gathered[:, :, 1536:1776]
+        gathered[:, :, 1600:1840]
         .reshape(2, 32, 2, 12, 240)
         .transpose(0, 1, 3, 2, 4)
         .reshape(C_FINE, 480)
@@ -108,8 +198,10 @@
     skip_ext = neighbours(skip, 4)
     cot_ext = neighbours(cotangent, 8)
     fine_rows = 2 * slab + 8
-    index = place * 2 * slab - 4 + lax.broadcasted_iota(jnp.int32, (1, fine_rows, 1), 1)
-    inside = (index >= 0) & (index < 2 * slab * lax.axis_size("seq"))
+    index = place * slab - 2 + lax.broadcasted_iota(jnp.int32, (1, slab + 4, 1), 1)
+    inside = (index >= 0) & (index < slab * lax.axis_size("seq"))
+    inside_rows = jnp.broadcast_to(inside, (2, 2, slab + 4, 1)).astype(F32)
+    skip_phases = jnp.moveaxis(skip_ext.reshape(seqs, slab + 4, 2, part_fine), 2, 0)
 
     both = share(
         jnp.concatenate([trunk_ext, cot_ext.reshape(seqs, slab + 8, 2 * part_fine)], axis=0)
@@ -128,13 +220,12 @@
         jnp.mean(projected_full * projected_full, axis=-1, keepdims=True) + EPS
     )
     act_coarse = jax.nn.gelu(projected_full * scale_coarse * gain_coarse).astype(BF16)
-    cot_full = lanes(cot_blocks)
 
     taps = dot(act_coarse, conv1_w)
     rows = slab + 4
-    mixed = sum(
-        taps[:, k : k + rows, k * part_coarse : (k + 1) * part_coarse] for k in range(5)
-    )
+    wide = sum(taps[:, k : k + rows, k * 128 : (k + 1) * 128] for k in range(5))
+    tail = sum(taps[:, k : k + rows, 640 + k * 64 : 704 + k * 64] for k in range(5))
+    mixed = jnp.concatenate([wide, tail], axis=2)
     lifted = (projected[:, 2 : 2 + rows].astype(F32) + mixed).astype(BF16)
 
     stacked = jnp.concatenate([cot_ext[:, 6 - k : 6 - k + fine_rows] for k in range(5)], axis=2)
@@ -150,32 +241,33 @@
     )
     lifted_full = lanes(first[:, :seqs])
     back_piece = jnp.sum(first[:, seqs:].astype(F32), axis=0).astype(BF16)
-    upper = dot(lifted_full, up_w).reshape(seqs, fine_rows, part_fine)
-    merged = jnp.where(inside, upper + skip_ext.astype(F32), 0.0).astype(BF16)
+    upper = dot(lifted_full, up_w)
+    upper = jnp.stack([upper[..., :part_fine], upper[..., part_fine:]])
+    merged = jnp.where(inside, upper + skip_phases.astype(F32), 0.0).astype(BF16)
+    back_piece = jnp.stack([back_piece[..., :part_fine], back_piece[..., part_fine:]])
     second = share(
-        jnp.concatenate([merged, back_piece.reshape(seqs, fine_rows, part_fine)], axis=0)
-    )
-    merged_full = lanes(second[:, :seqs]).astype(F32)
-    back_fine = lanes(second[:, seqs:]).astype(F32)
-
-    def activate(value):
-        scaled = value * lax.rsqrt(jnp.mean(value * value, axis=-1, keepdims=True) + EPS)
-        return jax.nn.gelu(scaled * gain_fine)
-
-    act_fine, pull = jax.vjp(activate, merged_full)
-    skip_grad_full = jnp.where(
-        inside, cot_full.astype(F32) + pull(back_fine)[0], 0.0
-    ).astype(BF16)
-    folded = skip_grad_full.reshape(seqs, rows, 2, NT, part_fine)
-    lifted_grad = lax.dot_general(
-        folded, up_turned_w.reshape(NT, part_coarse, 2, part_fine),
-        (((2, 3, 4), (2, 0, 3)), ((), ())),
-        preferred_element_type=F32,
-    ).astype(BF16)
-    stacked_grad = jnp.concatenate(
-        [lifted_grad[:, 4 - k : 4 - k + slab] for k in range(5)], axis=2
-    )
-    third = exchange(split(dot_t(stacked_grad, conv1_w).astype(BF16)))
+        jnp.concatenate([merged, back_piece], axis=0).reshape(4, seqs * rows, part_fine)
+    )
+
+    cot_phases = (
+        cot_blocks.reshape(NT, seqs, rows, 2, part_fine)
+        .transpose(0, 3, 1, 2, 4)
+        .reshape(NT, 2, seqs * rows, part_fine)
+    )
+    up_phases = jnp.pad(
+        up_turned_w.reshape(NT, part_coarse, 2, part_fine).transpose(2, 0, 1, 3),
+        ((0, 0), (0, 0), (0, 64), (0, 0)),
+    )
+    back_blocks, grad_blocks, lifted_grad = run_fine_adjoint(
+        second,
+        cot_phases,
+        gain_fine.reshape(NT, 1, part_fine),
+        inside_rows.reshape(2, seqs * rows, 1),
+        up_phases,
+        flat,
+        slab,
+    )
+    third = exchange(back_blocks)
     back_coarse = jnp.sum(third.astype(F32), axis=0)
 
     own = projected[:, 4 : 4 + slab].astype(F32)
@@ -186,7 +278,7 @@
     share_sum = jnp.sum(inner * own, axis=-1, keepdims=True)
     high = share_sum.astype(BF16)
     low = (share_sum - high.astype(F32)).astype(BF16)
-    direct = (lifted_grad[:, 2 : 2 + slab].astype(F32) + scale * inner).astype(BF16)
+    direct = (lifted_grad.astype(F32) + scale * inner).astype(BF16)
     fourth = share(
         jnp.concatenate([direct, high, low, jnp.zeros((seqs, slab, 62), BF16)], axis=2)
     )
@@ -197,16 +289,29 @@
     ).astype(BF16)
     trunk_grad = dot(projected_grad, out_t).astype(BF16)
 
-    fine_taps = dot(act_fine.astype(BF16), conv2_w)
+    merged_full = (
+        second[:, :2]
+        .reshape(NT, 2, seqs, rows, part_fine)
+        .transpose(2, 3, 1, 0, 4)
+        .reshape(seqs, fine_rows, C_FINE)
+        .astype(F32)
+    )
+    scaled = merged_full * lax.rsqrt(
+        jnp.mean(merged_full * merged_full, axis=-1, keepdims=True) + EPS
+    )
+    act_fine = jax.nn.gelu(scaled * gain_fine).astype(BF16)
+    fine_taps = dot(act_fine, conv2_w)
     fine_mixed = sum(
         fine_taps[:, 2 + k : 2 + k + 2 * slab, k * part_fine : (k + 1) * part_fine]
         for k in range(5)
     )
-    keep = slice(4, 4 + 2 * slab)
-    decoded = (merged[:, keep].astype(F32) + fine_mixed).astype(BF16)
-    skip_grad = lax.dynamic_slice_in_dim(
-        skip_grad_full[:, keep], rank * part_fine, part_fine, 2
-    )
+
+    def natural(phases):
+        moved = jnp.moveaxis(phases.reshape(2, seqs, rows, part_fine)[:, :, 2 : 2 + slab], 0, 2)
+        return moved.reshape(seqs, 2 * slab, part_fine)
+
+    decoded = (natural(merged).astype(F32) + fine_mixed).astype(BF16)
+    skip_grad = natural(lax.dynamic_index_in_dim(grad_blocks, rank, 0, keepdims=False))
     return (decoded, skip_grad, trunk_grad)
 
 

time: 234 us -> 223 us (0.953)
  the two profiles are of different devices: /device:TPU:8 before, /device:TPU:32 now
where the time goes in v3:
time: 223 us; the launch traced here: 221 us
  starting transfers between devices  54.8 us (25%)
  blocking collectives  49.8 us (22%)
  waiting for transfers between devices  48.3 us (22%)
  local copies, waits for them, and re-layouts  34.2 us (15%)
  between operations  14.8 us (7%)
  matrix products  7.76 us (3%)
  other arithmetic  7.65 us (3%)
  Pallas kernels  3.96 us (2%)
    all_to_all x6, waiting for transfers between devices, exchange(): return lax.all_to_all(blocks, 'tensor', 0, 0)  46 us
    all_gather x1, blocking collectives, per_device(): lax.all_gather(paired[:, :, :192], 'seq', axis=1, tiled=True, axis_index_...  40.1 us
    all_to_all x6, starting transfers between devices, exchange(): return lax.all_to_all(blocks, 'tensor', 0, 0)  37.2 us
    ppermute x3, starting transfers between devices, neighbours(): after = lax.ppermute(shard[:, :width], 'seq', down)  10.8 us
    all_gather x1, blocking collectives, per_device(): paired = lax.all_gather(packed, 'seq', axis=0, axis_index_groups=Y_PAIRS)  9.71 us
    dot_general x4, matrix products, dot(): lax.dot_general(left, right, (((left.ndim - 1,), (0,)), ((), ())), prefer...  6.93 us
    unnamed x28, local copies, waits for them, and re-layouts  6.08 us
    ppermute x3, starting transfers between devices, neighbours(): before = lax.ppermute(shard[:, length - width:], 'seq', up)  6.05 us
  transfers between devices with their start and end apart: 14, of which 7 were waited for; matrix products, arithmetic and copies ran while one was open for 9% of the time, Pallas kernels for 0%

profile of v3, /device:TPU:32, one launch (start us, length us, event | category | flops | bytes accessed | tf_op | source)
XLA Modules:
  0.0 221.2 jit_solution(1263628668923887834)
XLA Ops:
  7.2 0.8 reshape.166
  8.0 0.8 pad_maximum_fusion.3
  8.8 0.7 collective-permute-start.4
  9.5 0.7 copy.220
  10.4 0.8 copy_bitcast_fusion.2
  11.1 0.8 slice.232
  12.1 0.8 concatenate.48
  13.0 9.7 %all-gather = bf16[48,2112]{1,0:T(8,128)(2,1)S(1)} all-gather(bf16[24,2112]{1,0:T(8,128)(2,1)S(1)} %concatenate.48), channel_id=2, replica_groups={{0,256},{8,264},{16,272},{24,280},{32,288},{40,296},{48,304},{56,312},{..., dimensions={0}, use_global_device_ids=true | all-gather | bytes 304128 | tf_op jit(solution)/shard_map/all_gather | solution.py:180
  22.7 0.8 slice.238
  23.7 1.9 collective-permute-start.2
  25.6 3.6 %collective-permute-start.3 = (bf16[2,8,96]{2,1,0:T(8,128)(2,1)S(1)}, bf16[2,8,96]{2,1,0:T(8,128)(2,1)S(1)}, u32[]{:S(2)}, u32[]{:S(2)}) collective-permute-start(bf16[2,8,96]{2,1,0:T(8,128)(2,1)S(1)} %get-tuple-element.48), channel_id=1, source_target_pairs={{8,0},{16,8},{24,16},{32,24},{40,32},{48,40},{56,48},{64,56},{72,6... | collective-permute-start | bytes 9224 | tf_op jit(solution)/shard_map/ppermute | solution.py:50
  29.3 2.2 collective-permute-start
  31.5 3.4 %collective-permute-start.1 = (bf16[2,4,192]{2,1,0:T(4,128)(2,1)S(1)}, bf16[2,4,192]{2,1,0:T(4,128)(2,1)S(1)}, u32[]{:S(2)}, u32[]{:S(2)}) collective-permute-start(bf16[2,4,192]{2,1,0:T(4,128)(2,1)S(1)} %get-tuple-element.46), channel_id=1, source_target_pairs={{8,0},{16,8},{24,16},{32,24},{40,32},{48,40},{56,48},{64,56},{72,6... | collective-permute-start | bytes 9224 | tf_op jit(solution)/shard_map/ppermute | solution.py:50
  35.0 1.1 collective-permute-done.1
  36.2 1.1 broadcast_in_dim.39
  37.3 14.8 %all-to-all-start = ((bf16[8,4,72,192]{3,2,1,0:T(8,128)(2,1)}), bf16[8,4,72,192]{3,2,1,0:T(8,128)(2,1)S(1)}, u32[]{:S(2)}, u32[]{:S(2)}) async-start(bf16[8,4,72,192]{3,2,1,0:T(8,128)(2,1)} %broadcast_in_dim.39), calls=%async_computation | async-start | bytes 2359296 | tf_op jit(solution)/shard_map/all_to_all | solution.py:38
  52.1 40.1 %all_gather.14 = bf16[2,768,192]{2,1,0:T(8,128)(2,1)S(1)} all-gather(bf16[2,24,192]{2,1,0:T(8,128)(2,1)S(1)} %slice.236), channel_id=1, replica_groups={{0,8,16,24,32,40,48,56,64,72,80,88,96,104,112,120,128,136,144,152,160,1..., dimensions={1}, use_global_device_ids=true | all-gather | bytes 608256 | tf_op jit(solution)/shard_map/all_gather | solution.py:212
  92.5 0.9 broadcast_in_dim.75
  93.4 6.9 %all-to-all-start.1 = ((bf16[8,2,72,192]{3,2,1,0:T(8,128)(2,1)}), bf16[8,2,72,192]{3,2,1,0:T(8,128)(2,1)S(1)}, u32[]{:S(2)}, u32[]{:S(2)}) async-start(bf16[8,2,72,192]{3,2,1,0:T(8,128)(2,1)} %broadcast_in_dim.75), calls=%async_computation.1 | async-start | bytes 1179648 | tf_op jit(solution)/shard_map/all_to_all | solution.py:38
  100.6 11.6 %all-to-all-done.1 = bf16[8,2,72,192]{3,2,1,0:T(8,128)(2,1)S(1)} async-done(((bf16[8,2,72,192]{3,2,1,0:T(8,128)(2,1)}), bf16[8,2,72,192]{3,2,1,0:T(8,128)(2,1)S(1)}, u32[]{:S(2)}, u32[]{:S(2)}) %all-to-all-start.1) | async-done | bytes 442400 | tf_op jit(solution)/shard_map/all_to_all | solution.py:38
  112.3 0.7 copy.221
  113.0 1.3 reshape.183
  114.6 3.1 %fusion = f32[2,72,960]{2,1,0:T(8,128)S(1)} fusion(bf16[1536,1920]{1,0:T(8,128)(2,1)} %bitcast.106, f32[2,72,1536]{2,1,0:T(8,128)} %reshape.183, f32[1536]{0:T(1024)S(1)} %copy-done.11, f32[2,72]{1,0:T(2,128)S(1)} %get-tuple-element.54), kind=kOutput, calls=%fused_computation.1 | convolution fusion | flops 427106304 | bytes 4590144 | tf_op jit(solution)/shard_map/dot_general | solution.py:23
  117.6 0.7 slice_add_fusion.4
  118.4 0.7 slice_add_fusion.8
  119.1 1.6 slice.255
  120.7 0.8 copy.223
  121.5 0.6 copy.224
  122.1 0.4 reshape.173
  122.5 0.4 convolution_convert_fusion
  123.0 0.6 reshape.174
  123.7 0.4 reshape.175
  124.8 1.4 copy.227
  126.3 3.8 %all-to-all-start.2 = ((bf16[8,4,68,192]{3,1,2,0:T(4,128)(2,1)}), bf16[8,4,68,192]{3,1,2,0:T(4,128)(2,1)S(1)}, u32[]{:S(2)}, u32[]{:S(2)}) async-start(bf16[8,4,68,192]{3,1,2,0:T(4,128)(2,1)} %copy.227), calls=%async_computation.2 | async-start | bytes 2228224 | tf_op jit(solution)/shard_map/all_to_all | solution.py:38
  130.2 1.9 collective-permute-start.5
  132.2 3.8 %collective-permute-start.6 = (bf16[2,4,96]{2,1,0:T(4,128)(2,1)S(1)}, bf16[2,4,96]{2,1,0:T(4,128)(2,1)S(1)}, u32[]{:S(2)}, u32[]{:S(2)}) collective-permute-start(bf16[2,4,96]{2,1,0:T(4,128)(2,1)S(1)} %get-tuple-element.44), channel_id=1, source_target_pairs={{8,0},{16,8},{24,16},{32,24},{40,32},{48,40},{56,48},{64,56},{72,6... | collective-permute-start | bytes 4616 | tf_op jit(solution)/shard_map/ppermute | solution.py:50
  136.0 1.1 collective-permute-done.6
  137.1 9.6 %all-to-all-done.2 = bf16[8,4,68,192]{3,1,2,0:T(4,128)(2,1)S(1)} async-done(((bf16[8,4,68,192]{3,1,2,0:T(4,128)(2,1)}), bf16[8,4,68,192]{3,1,2,0:T(4,128)(2,1)S(1)}, u32[]{:S(2)}, u32[]{:S(2)}) %all-to-all-start.2) | async-done | bytes 835616 | tf_op jit(solution)/shard_map/all_to_all | solution.py:38
  146.8 1.0 slice_reduce_fusion
  147.9 0.5 reshape.176
  148.4 1.4 fusion.21
  150.6 1.2 broadcast_in_dim.79
  151.8 4.0 %all-to-all-start.3 = ((bf16[8,4,136,96]{3,2,1,0:T(8,128)(2,1)}), bf16[8,4,136,96]{3,2,1,0:T(8,128)(2,1)S(1)}, u32[]{:S(2)}, u32[]{:S(2)}) async-start(bf16[8,4,136,96]{3,2,1,0:T(8,128)(2,1)} %broadcast_in_dim.79), calls=%async_computation.3 | async-start | bytes 2228224 | tf_op jit(solution)/shard_map/all_to_all | solution.py:38
  157.1 2.5 %slice.274 = bf16[1536,192]{1,0:T(8,128)(2,1)} slice(bf16[1536,1920]{1,0:T(8,128)(2,1)} %bitcast.108), slice={[0:1536], [1216:1408]} | slice | bytes 1179648 | tf_op jit(solution)/shard_map/slice | solution.py:188
  159.6 2.4 %reshape.196 = bf16[8,192,2,96]{3,2,1,0:T(2,128)(2,1)S(1)} reshape(bf16[1536,192]{1,0:T(8,128)(2,1)} %slice.274) | data formatting | bytes 1179648 | tf_op jit(solution)/shard_map/reshape;reshape | solution.py:258
  162.4 0.8 copy.234
  163.2 8.6 %all-to-all-done.3.shared_ref = bf16[8,4,136,96]{3,2,1,0:T(8,128)(2,1)S(1)} async-done(((bf16[8,4,136,96]{3,2,1,0:T(8,128)(2,1)}), bf16[8,4,136,96]{3,2,1,0:T(8,128)(2,1)S(1)}, u32[]{:S(2)}, u32[]{:S(2)}) %all-to-all-start.3) | async-done | bytes 835616 | tf_op jit(solution)/shard_map/all_to_all | solution.py:38
  171.9 2.7 %copy-done = bf16[2,768,1920]{2,1,0:T(8,128)(2,1)S(1)} copy-done((bf16[2,768,1920]{2,1,0:T(8,128)(2,1)S(1)}, bf16[2,768,1920]{2,1,0:T(8,128)(2,1)}, u32[]{:S(2)}) %copy-start) | copy-done | bytes 5898264
  174.5 4.0 %fine_adjoint.1 = (bf16[8,2,64,192]{3,2,1,0:T(8,128)(2,1)}, bf16[8,2,136,96]{3,2,1,0:T(8,128)(2,1)S(1)}, bf16[2,64,192]{2,1,0:T(8,128)(2,1)S(1)}) custom-call(bf16[8,4,136,96]{3,2,1,0:T(8,128)(2,1)S(1)} %all-to-all-done.3.shared_ref, bf16[8,2,136,96]{3,2,1,0:T(8,128)(2,1)S(1)} %copy.248.cot_ref, f32[8,1,96]{2,1,0:T(1,128)S(1)} %reshape.180.gain_ref, ...), custom_call_target="tpu_custom_call" | custom-call | tf_op jit(solution)/shard_map/fine_adjoint/pallas_call | solution.py:123
  178.5 4.2 %all-to-all-start.4 = ((bf16[8,2,64,192]{3,2,1,0:T(8,128)(2,1)}), bf16[8,2,64,192]{3,2,1,0:T(8,128)(2,1)}, u32[]{:S(2)}, u32[]{:S(2)}) async-start(bf16[8,2,64,192]{3,2,1,0:T(8,128)(2,1)} %get-tuple-element.8), calls=%async_computation.4 | async-start | bytes 1048576 | tf_op jit(solution)/shard_map/all_to_all | solution.py:38
  183.2 0.6 multiply_reduce_fusion
  183.9 0.7 copy.256
  184.6 0.5 fusion.10
  185.3 0.4 convert_element_type.167
  185.7 7.7 %all-to-all-done.4 = bf16[8,2,64,192]{3,2,1,0:T(8,128)(2,1)} async-done(((bf16[8,2,64,192]{3,2,1,0:T(8,128)(2,1)}), bf16[8,2,64,192]{3,2,1,0:T(8,128)(2,1)}, u32[]{:S(2)}, u32[]{:S(2)}) %all-to-all-start.4) | async-done | bytes 393248 | tf_op jit(solution)/shard_map/all_to_all | solution.py:38
  193.4 1.1 convert_reduce_fusion
  195.3 0.9 broadcast_in_dim.84
  196.2 3.5 %all-to-all-start.5 = ((bf16[8,2,64,256]{3,2,1,0:T(8,128)(2,1)}), bf16[8,2,64,256]{3,2,1,0:T(8,128)(2,1)S(1)}, u32[]{:S(2)}, u32[]{:S(2)}) async-start(bf16[8,2,64,256]{3,2,1,0:T(8,128)(2,1)} %broadcast_in_dim.84), calls=%async_computation.5 | async-start | bytes 1048576 | tf_op jit(solution)/shard_map/all_to_all | solution.py:38
  200.1 0.5 copy-done.4
  200.8 0.7 copy.255
  201.5 8.5 %all-to-all-done.5 = bf16[8,2,64,256]{3,2,1,0:T(8,128)(2,1)S(1)} async-done(((bf16[8,2,64,256]{3,2,1,0:T(8,128)(2,1)}), bf16[8,2,64,256]{3,2,1,0:T(8,128)(2,1)S(1)}, u32[]{:S(2)}, u32[]{:S(2)}) %all-to-all-start.5) | async-done | bytes 524320 | tf_op jit(solution)/shard_map/all_to_all | solution.py:38
  210.5 0.6 copy.253
  211.4 0.8 copy-done.3
  212.3 2.1 convolution_convert_fusion.1
  (109 shorter events, 7.9 us)
Async XLA Ops:
  7.2 16.3 %copy-start.8 = (bf16[2,128,96]{1,2,0:T(8,128)(2,1)S(1)}, bf16[2,128,96]{1,2,0:T(8,128)(2,1)}, u32[]{:S(2)}) copy-start(bf16[2,128,96]{1,2,0:T(8,128)(2,1)} %param.17) | copy-start | bytes 147460
  7.2 22.1 %copy-start.7 = (bf16[2,64,192]{2,1,0:T(8,128)(2,1)S(1)}, bf16[2,64,192]{2,1,0:T(8,128)(2,1)}, u32[]{:S(2)}) copy-start(bf16[2,64,192]{2,1,0:T(8,128)(2,1)} %param.9) | copy-start | bytes 147460
  7.2 107.4 %all-gather.3.cloned.1.call-start = ((), (), s32[]{:S(2)}) async-start(), calls=%async_computation.6 | async-start | bytes 6082560 | tf_op jit(solution)/shard_map/all_gather | solution.py:181
  8.8 3.2 %collective-permute-start.4 = (bf16[24,384]{1,0:T(8,128)(2,1)S(1)}, bf16[24,384]{1,0:T(8,128)(2,1)S(1)}, u32[]{:S(2)}, u32[]{:S(2)}) collective-permute-start(bf16[24,384]{1,0:T(8,128)(2,1)S(1)} %pad_maximum_fusion.3), channel_id=1, source_target_pairs={{0,0},{1,64},{2,128},{3,192},{4,256},{5,320},{6,384},{7,448},{8,8}... | collective-permute-start | bytes 55304 | tf_op jit(solution)/shard_map/ppermute | solution.py:157
  23.7 11.2 %collective-permute-start.2 = (bf16[2,8,96]{2,1,0:T(8,128)(2,1)S(1)}, bf16[2,8,96]{2,1,0:T(8,128)(2,1)S(1)}, u32[]{:S(2)}, u32[]{:S(2)}) collective-permute-start(bf16[2,8,96]{2,1,0:T(8,128)(2,1)S(1)} %get-tuple-element.47), channel_id=1, source_target_pairs={{0,8},{8,16},{16,24},{24,32},{32,40},{40,48},{48,56},{56,64},{64,7... | collective-permute-start | bytes 9224 | tf_op jit(solution)/shard_map/ppermute | solution.py:49
  25.6 9.3 %collective-permute-start.3 = (bf16[2,8,96]{2,1,0:T(8,128)(2,1)S(1)}, bf16[2,8,96]{2,1,0:T(8,128)(2,1)S(1)}, u32[]{:S(2)}, u32[]{:S(2)}) collective-permute-start(bf16[2,8,96]{2,1,0:T(8,128)(2,1)S(1)} %get-tuple-element.48), channel_id=1, source_target_pairs={{8,0},{16,8},{24,16},{32,24},{40,32},{48,40},{56,48},{64,56},{72,6... | collective-permute-start | bytes 9224 | tf_op jit(solution)/shard_map/ppermute | solution.py:50
  29.3 5.7 %collective-permute-start = (bf16[2,4,192]{2,1,0:T(4,128)(2,1)S(1)}, bf16[2,4,192]{2,1,0:T(4,128)(2,1)S(1)}, u32[]{:S(2)}, u32[]{:S(2)}) collective-permute-start(bf16[2,4,192]{2,1,0:T(4,128)(2,1)S(1)} %get-tuple-element.45), channel_id=1, source_target_pairs={{0,8},{8,16},{16,24},{24,32},{32,40},{40,48},{48,56},{56,64},{64,7... | collective-permute-start | bytes 9224 | tf_op jit(solution)/shard_map/ppermute | solution.py:49
  31.5 4.7 %collective-permute-start.1 = (bf16[2,4,192]{2,1,0:T(4,128)(2,1)S(1)}, bf16[2,4,192]{2,1,0:T(4,128)(2,1)S(1)}, u32[]{:S(2)}, u32[]{:S(2)}) collective-permute-start(bf16[2,4,192]{2,1,0:T(4,128)(2,1)S(1)} %get-tuple-element.46), channel_id=1, source_target_pairs={{8,0},{16,8},{24,16},{32,24},{40,32},{48,40},{56,48},{64,56},{72,6... | collective-permute-start | bytes 9224 | tf_op jit(solution)/shard_map/ppermute | solution.py:50
  37.3 54.8 %all-to-all-start = ((bf16[8,4,72,192]{3,2,1,0:T(8,128)(2,1)}), bf16[8,4,72,192]{3,2,1,0:T(8,128)(2,1)S(1)}, u32[]{:S(2)}, u32[]{:S(2)}) async-start(bf16[8,4,72,192]{3,2,1,0:T(8,128)(2,1)} %broadcast_in_dim.39), calls=%async_computation | async-start | bytes 2359296 | tf_op jit(solution)/shard_map/all_to_all | solution.py:38
  93.4 18.8 %all-to-all-start.1 = ((bf16[8,2,72,192]{3,2,1,0:T(8,128)(2,1)}), bf16[8,2,72,192]{3,2,1,0:T(8,128)(2,1)S(1)}, u32[]{:S(2)}, u32[]{:S(2)}) async-start(bf16[8,2,72,192]{3,2,1,0:T(8,128)(2,1)} %broadcast_in_dim.75), calls=%async_computation.1 | async-start | bytes 1179648 | tf_op jit(solution)/shard_map/all_to_all | solution.py:38
  113.0 1.6 copy-start.11
  122.5 1.1 copy-start.1
  123.6 0.9 copy-start.5
  123.6 0.9 copy-start.6
  126.3 3.8 %copy-start.9 = (bf16[2,128,96]{1,2,0:T(8,128)(2,1)S(1)}, bf16[2,128,96]{1,2,0:T(8,128)(2,1)}, u32[]{:S(2)}) copy-start(bf16[2,128,96]{1,2,0:T(8,128)(2,1)} %param.14) | copy-start | bytes 147460
  126.3 20.5 %all-to-all-start.2 = ((bf16[8,4,68,192]{3,1,2,0:T(4,128)(2,1)}), bf16[8,4,68,192]{3,1,2,0:T(4,128)(2,1)S(1)}, u32[]{:S(2)}, u32[]{:S(2)}) async-start(bf16[8,4,68,192]{3,1,2,0:T(4,128)(2,1)} %copy.227), calls=%async_computation.2 | async-start | bytes 2228224 | tf_op jit(solution)/shard_map/all_to_all | solution.py:38
  130.2 5.8 %collective-permute-start.5 = (bf16[2,4,96]{2,1,0:T(4,128)(2,1)S(1)}, bf16[2,4,96]{2,1,0:T(4,128)(2,1)S(1)}, u32[]{:S(2)}, u32[]{:S(2)}) collective-permute-start(bf16[2,4,96]{2,1,0:T(4,128)(2,1)S(1)} %get-tuple-element.43), channel_id=1, source_target_pairs={{0,8},{8,16},{16,24},{24,32},{32,40},{40,48},{48,56},{56,64},{64,7... | collective-permute-start | bytes 4616 | tf_op jit(solution)/shard_map/ppermute | solution.py:49
  132.2 4.9 %collective-permute-start.6 = (bf16[2,4,96]{2,1,0:T(4,128)(2,1)S(1)}, bf16[2,4,96]{2,1,0:T(4,128)(2,1)S(1)}, u32[]{:S(2)}, u32[]{:S(2)}) collective-permute-start(bf16[2,4,96]{2,1,0:T(4,128)(2,1)S(1)} %get-tuple-element.44), channel_id=1, source_target_pairs={{8,0},{16,8},{24,16},{32,24},{40,32},{48,40},{56,48},{64,56},{72,6... | collective-permute-start | bytes 4616 | tf_op jit(solution)/shard_map/ppermute | solution.py:50
  151.8 4.0 %copy-start.10 = (f32[768]{0:T(1024)S(1)}, f32[768]{0:T(1024)}, u32[]{:S(2)}) copy-start(f32[768]{0:T(1024)} %param.15) | copy-start | bytes 9220
  151.8 20.0 %all-to-all-start.3 = ((bf16[8,4,136,96]{3,2,1,0:T(8,128)(2,1)}), bf16[8,4,136,96]{3,2,1,0:T(8,128)(2,1)S(1)}, u32[]{:S(2)}, u32[]{:S(2)}) async-start(bf16[8,4,136,96]{3,2,1,0:T(8,128)(2,1)} %broadcast_in_dim.79), calls=%async_computation.3 | async-start | bytes 2228224 | tf_op jit(solution)/shard_map/all_to_all | solution.py:38
  171.9 2.7 %copy-start = (bf16[2,768,1920]{2,1,0:T(8,128)(2,1)S(1)}, bf16[2,768,1920]{2,1,0:T(8,128)(2,1)}, u32[]{:S(2)}) copy-start(bf16[2,768,1920]{2,1,0:T(8,128)(2,1)} %all-gather.3.cloned.1.call-done) | copy-start | bytes 17694724
  178.5 14.9 %all-to-all-start.4 = ((bf16[8,2,64,192]{3,2,1,0:T(8,128)(2,1)}), bf16[8,2,64,192]{3,2,1,0:T(8,128)(2,1)}, u32[]{:S(2)}, u32[]{:S(2)}) async-start(bf16[8,2,64,192]{3,2,1,0:T(8,128)(2,1)} %get-tuple-element.8), calls=%async_computation.4 | async-start | bytes 1048576 | tf_op jit(solution)/shard_map/all_to_all | solution.py:38
  194.8 4.8 %copy-start.2 = (bf16[768,480]{1,0:T(8,128)(2,1)S(1)}, bf16[768,480]{1,0:T(8,128)(2,1)}, u32[]{:S(2)}) copy-start(bf16[768,480]{1,0:T(8,128)(2,1)} %copy-done.1) | copy-start | bytes 2211844
  196.2 13.9 %all-to-all-start.5 = ((bf16[8,2,64,256]{3,2,1,0:T(8,128)(2,1)}), bf16[8,2,64,256]{3,2,1,0:T(8,128)(2,1)S(1)}, u32[]{:S(2)}, u32[]{:S(2)}) async-start(bf16[8,2,64,256]{3,2,1,0:T(8,128)(2,1)} %broadcast_in_dim.84), calls=%async_computation.5 | async-start | bytes 1048576 | tf_op jit(solution)/shard_map/all_to_all | solution.py:38
  199.7 0.9 copy-start.4
  211.1 1.2 copy-start.3
Sparse Core Ops, SparseCore 0:
  23.6 87.6 all-gather.2

commit v4 on v3

--- a/solution.py
+++ b/solution.py
@@ -54,10 +54,6 @@
 def lanes(blocks):
     moved = jnp.moveaxis(blocks, 0, 2)
     return moved.reshape(moved.shape[:2] + (-1,))
-
-
-def split(full):
-    return jnp.moveaxis(full.reshape(full.shape[:2] + (NT, -1)), 2, 0)
 
 
 def fine_adjoint(shared_ref, cot_ref, gain_ref, inside_ref, up_ref, conv_ref, back_ref, grad_ref, lifted_ref, norm_ref, rows_ref, taps_ref):
@@ -140,6 +136,24 @@
     )(shared, cot, gain, inside, up_phases, flat)
 
 
+def fine_back(stacked_ref, weight_ref, back_ref):
+    total = jnp.zeros(back_ref.shape, F32)
+    for t in range(NT):
+        total = total + dot_t(stacked_ref[t], weight_ref[t])
+    back_ref[...] = total.astype(BF16)
+
+
+def run_fine_back(stacked, weight):
+    whole = pl.BlockSpec(memory_space=pltpu.VMEM)
+    return pl.pallas_call(
+        fine_back,
+        in_specs=[whole] * 2,
+        out_specs=whole,
+        out_shape=jax.ShapeDtypeStruct((stacked.shape[1], weight.shape[1]), BF16),
+        name="fine_back",
+    )(stacked, weight)
+
+
 def per_device(trunk, w_out, gain_coarse, w_conv1, w_up, skip, gain_fine, w_conv2, cotangent):
     rank = lax.axis_index("tensor")
     place = lax.axis_index("seq")
@@ -154,26 +168,27 @@
     ]
     up_shard = w_up.reshape(24, 192)
     out_shard = w_out.T
+    conv2_flat = jnp.transpose(w_conv2, (1, 0, 2)).reshape(12, 480)
+    conv2_shard = jnp.concatenate([conv2_flat[:, :240], conv2_flat[:, 240:]], axis=0)
     both_turned = lax.ppermute(
-        jnp.concatenate([out_shard, up_shard], axis=1), ("seq", "tensor"), turned
+        jnp.concatenate([out_shard, up_shard, conv2_shard], axis=1), ("seq", "tensor"), turned
     )
     conv1_turned = jnp.transpose(w_conv1, (1, 0, 2))
     conv1_shard = jnp.concatenate(
         [conv1_turned[:, :, :128].reshape(24, 640), conv1_turned[:, :, 128:].reshape(24, 320)],
         axis=1,
     )
-    conv2_flat = jnp.transpose(w_conv2, (1, 0, 2)).reshape(12, 480)
-    conv2_shard = jnp.concatenate([conv2_flat[:, :240], conv2_flat[:, 240:]], axis=0)
     packed = jnp.concatenate(
         [
             both_turned[:, :192],
             conv1_shard,
             jnp.zeros((24, 64), BF16),
             up_shard,
-            both_turned[:, 192:],
+            both_turned[:, 192:384],
             out_shard,
             conv2_shard,
-            jnp.zeros((24, 80), BF16),
+            both_turned[:, 384:],
+            jnp.zeros((24, 96), BF16),
         ],
         axis=1,
     )
@@ -194,6 +209,13 @@
         .reshape(C_FINE, 480)
     )
 
+    conv2_turned_w = (
+        gathered[:, :, 1840:2080]
+        .reshape(NT, 8, 2, 12, 240)
+        .transpose(0, 1, 3, 2, 4)
+        .reshape(NT, part_fine, 480)
+    )
+
     trunk_ext = neighbours(trunk, 4)
     skip_ext = neighbours(skip, 4)
     cot_ext = neighbours(cotangent, 8)
@@ -207,8 +229,20 @@
         jnp.concatenate([trunk_ext, cot_ext.reshape(seqs, slab + 8, 2 * part_fine)], axis=0)
     )
     trunk_blocks = both[:, :seqs]
-    cot_blocks = both[:, seqs:].reshape(NT, seqs, 2 * slab + 16, part_fine)
-    cot_blocks = cot_blocks[:, :, 4 : 4 + fine_rows]
+    rows = slab + 4
+    cot_planes = jnp.moveaxis(
+        both[:, seqs:].reshape(NT, seqs, slab + 8, 2, part_fine), 3, 1
+    )
+    cot_phases = cot_planes[:, :, :, 2 : 2 + rows].reshape(NT, 2, seqs * rows, part_fine)
+
+    def tap(p, k):
+        offset = p - k + 2
+        q, start = offset % 2, 2 + offset // 2
+        return cot_planes[:, q, :, start : start + rows]
+
+    stacked = jnp.stack(
+        [jnp.concatenate([tap(p, k) for k in range(5)], axis=-1) for p in range(2)], axis=1
+    ).reshape(NT, 2 * seqs * rows, 5 * part_fine)
     out_turned = lax.all_gather(
         paired[:, :, :192], "seq", axis=1, tiled=True, axis_index_groups=Z_CORES
     ).reshape(NT, part_coarse, 192)
@@ -222,38 +256,20 @@
     act_coarse = jax.nn.gelu(projected_full * scale_coarse * gain_coarse).astype(BF16)
 
     taps = dot(act_coarse, conv1_w)
-    rows = slab + 4
     wide = sum(taps[:, k : k + rows, k * 128 : (k + 1) * 128] for k in range(5))
     tail = sum(taps[:, k : k + rows, 640 + k * 64 : 704 + k * 64] for k in range(5))
     mixed = jnp.concatenate([wide, tail], axis=2)
     lifted = (projected[:, 2 : 2 + rows].astype(F32) + mixed).astype(BF16)
 
-    stacked = jnp.concatenate([cot_ext[:, 6 - k : 6 - k + fine_rows] for k in range(5)], axis=2)
-    back_partial = split(dot_t(stacked, conv2_w).astype(BF16))
-    first = exchange(
-        jnp.concatenate(
-            [
-                jnp.broadcast_to(lifted[None], (NT,) + lifted.shape),
-                back_partial.reshape(NT, seqs, rows, 2 * part_fine),
-            ],
-            axis=1,
-        )
-    )
-    lifted_full = lanes(first[:, :seqs])
-    back_piece = jnp.sum(first[:, seqs:].astype(F32), axis=0).astype(BF16)
+    lifted_full = lanes(share(lifted))
+    back_piece = run_fine_back(stacked, conv2_turned_w).reshape(2, seqs, rows, part_fine)
     upper = dot(lifted_full, up_w)
     upper = jnp.stack([upper[..., :part_fine], upper[..., part_fine:]])
     merged = jnp.where(inside, upper + skip_phases.astype(F32), 0.0).astype(BF16)
-    back_piece = jnp.stack([back_piece[..., :part_fine], back_piece[..., part_fine:]])
     second = share(
         jnp.concatenate([merged, back_piece], axis=0).reshape(4, seqs * rows, part_fine)
     )
 
-    cot_phases = (
-        cot_blocks.reshape(NT, seqs, rows, 2, part_fine)
-        .transpose(0, 3, 1, 2, 4)
-        .reshape(NT, 2, seqs * rows, part_fine)
-    )
     up_phases = jnp.pad(
         up_turned_w.reshape(NT, part_coarse, 2, part_fine).transpose(2, 0, 1, 3),
         ((0, 0), (0, 0), (0, 64), (0, 0)),

time: 223 us -> 228 us (1.022)
  the two profiles are of different devices: /device:TPU:32 before, /device:TPU:8 now
where the time goes in v4:
time: 228 us; the launch traced here: 227 us
  starting transfers between devices  69.6 us (31%)
  local copies, waits for them, and re-layouts  51.6 us (23%)
  blocking collectives  36.2 us (16%)
  waiting for transfers between devices  33.4 us (15%)
  between operations  14.7 us (6%)
  matrix products  7.61 us (3%)
  Pallas kernels  7.19 us (3%)
  other arithmetic  6.23 us (3%)
    all_to_all x6, starting transfers between devices, exchange(): return lax.all_to_all(blocks, 'tensor', 0, 0)  37.6 us
    all_gather x1, blocking collectives, per_device(): lax.all_gather(paired[:, :, :192], 'seq', axis=1, tiled=True, axis_index_...  30.7 us
    all_to_all x6, waiting for transfers between devices, exchange(): return lax.all_to_all(blocks, 'tensor', 0, 0)  22.3 us
    ppermute x3, starting transfers between devices, neighbours(): after = lax.ppermute(shard[:, :width], 'seq', down)  20.9 us
    ppermute x3, waiting for transfers between devices, neighbours(): before = lax.ppermute(shard[:, length - width:], 'seq', up)  9.4 us
    dot_general x4, matrix products, dot(): lax.dot_general(left, right, (((left.ndim - 1,), (0,)), ((), ())), prefer...  7.21 us
    ppermute x3, starting transfers between devices, neighbours(): before = lax.ppermute(shard[:, length - width:], 'seq', up)  6.25 us
    concatenate x2, local copies, waits for them, and re-layouts, per_device(): jnp.concatenate([tap(p, k) for k in range(5)], axis=-1)  5.96 us
  transfers between devices with their start and end apart: 14, of which 7 were waited for; matrix products, arithmetic and copies ran while one was open for 19% of the time, Pallas kernels for 1%

profile of v4, /device:TPU:8, one launch (start us, length us, event | category | flops | bytes accessed | tf_op | source)
XLA Modules:
  0.0 226.5 jit_solution(5159492432403350596)
XLA Ops:
  7.2 0.7 copy.474
  8.1 0.8 reshape.165
  8.9 0.8 maximum_maximum_fusion.1
  9.7 4.8 %collective-permute-start.4 = (bf16[24,624]{1,0:T(8,128)(2,1)S(1)}, bf16[24,624]{1,0:T(8,128)(2,1)S(1)}, u32[]{:S(2)}, u32[]{:S(2)}) collective-permute-start(bf16[24,624]{1,0:T(8,128)(2,1)S(1)} %maximum_maximum_fusion.1), channel_id=1, source_target_pairs={{0,0},{1,64},{2,128},{3,192},{4,256},{5,320},{6,384},{7,448},{8,8}... | collective-permute-start | bytes 89864 | tf_op jit(solution)/shard_map/ppermute | solution.py:173
  14.5 0.8 copy_bitcast_fusion.7
  15.3 0.8 slice.232
  16.2 1.7 collective-permute-done.4
  18.0 0.8 concatenate.46
  18.8 5.5 %all-gather = bf16[48,2368]{1,0:T(8,128)(2,1)S(1)} all-gather(bf16[24,2368]{1,0:T(8,128)(2,1)S(1)} %concatenate.46), channel_id=2, replica_groups={{0,256},{8,264},{16,272},{24,280},{32,288},{40,296},{48,304},{56,312},{..., dimensions={0}, use_global_device_ids=true | all-gather | bytes 340992 | tf_op jit(solution)/shard_map/all_gather | solution.py:195
  24.3 0.8 slice.237
  25.3 13.2 %collective-permute-start.3 = (bf16[2,8,96]{1,2,0:T(8,128)(2,1)S(1)}, bf16[2,8,96]{1,2,0:T(8,128)(2,1)S(1)}, u32[]{:S(2)}, u32[]{:S(2)}) collective-permute-start(bf16[2,8,96]{1,2,0:T(8,128)(2,1)S(1)} %get-tuple-element.65), channel_id=1, source_target_pairs={{8,0},{16,8},{24,16},{32,24},{40,32},{48,40},{56,48},{64,56},{72,6... | collective-permute-start | bytes 9224 | tf_op jit(solution)/shard_map/ppermute | solution.py:50
  38.5 1.9 collective-permute-start.2
  40.5 5.8 %collective-permute-start.1 = (bf16[2,4,192]{2,1,0:T(4,128)(2,1)S(1)}, bf16[2,4,192]{2,1,0:T(4,128)(2,1)S(1)}, u32[]{:S(2)}, u32[]{:S(2)}) collective-permute-start(bf16[2,4,192]{2,1,0:T(4,128)(2,1)S(1)} %get-tuple-element.63), channel_id=1, source_target_pairs={{8,0},{16,8},{24,16},{32,24},{40,32},{48,40},{56,48},{64,56},{72,6... | collective-permute-start | bytes 9224 | tf_op jit(solution)/shard_map/ppermute | solution.py:50
  46.2 1.9 collective-permute-start
  48.5 4.8 %collective-permute-done = bf16[2,4,192]{2,1,0:T(4,128)(2,1)S(1)} collective-permute-done((bf16[2,4,192]{2,1,0:T(4,128)(2,1)S(1)}, bf16[2,4,192]{2,1,0:T(4,128)(2,1)S(1)}, u32[]{:S(2)}, u32[]{:S(2)}) %collective-permute-start) | collective-permute-done | bytes 3104 | tf_op jit(solution)/shard_map/ppermute | solution.py:49
  53.4 1.1 broadcast_in_dim.39
  54.5 9.7 %all-to-all-start = ((bf16[8,4,72,192]{3,2,1,0:T(8,128)(2,1)}), bf16[8,4,72,192]{3,2,1,0:T(8,128)(2,1)S(1)}, u32[]{:S(2)}, u32[]{:S(2)}) async-start(bf16[8,4,72,192]{3,2,1,0:T(8,128)(2,1)} %broadcast_in_dim.39), calls=%async_computation | async-start | bytes 2359296 | tf_op jit(solution)/shard_map/all_to_all | solution.py:38
  64.3 1.9 collective-permute-start.6
  66.3 2.4 %collective-permute-start.5 = (bf16[2,4,96]{2,1,0:T(4,128)(2,1)S(1)}, bf16[2,4,96]{2,1,0:T(4,128)(2,1)S(1)}, u32[]{:S(2)}, u32[]{:S(2)}) collective-permute-start(bf16[2,4,96]{2,1,0:T(4,128)(2,1)S(1)} %get-tuple-element.60), channel_id=1, source_target_pairs={{0,8},{8,16},{16,24},{24,32},{32,40},{40,48},{48,56},{56,64},{64,7... | collective-permute-start | bytes 4616 | tf_op jit(solution)/shard_map/ppermute | solution.py:49
  68.7 4.6 %collective-permute-done.5 = bf16[2,4,96]{2,1,0:T(4,128)(2,1)S(1)} collective-permute-done((bf16[2,4,96]{2,1,0:T(4,128)(2,1)S(1)}, bf16[2,4,96]{2,1,0:T(4,128)(2,1)S(1)}, u32[]{:S(2)}, u32[]{:S(2)}) %collective-permute-start.5) | collective-permute-done | bytes 1568 | tf_op jit(solution)/shard_map/ppermute | solution.py:49
  73.3 0.7 maximum_convert_fusion
  74.0 30.7 %all_gather.14 = bf16[2,768,192]{2,1,0:T(8,128)(2,1)S(1)} all-gather(bf16[2,24,192]{2,1,0:T(8,128)(2,1)S(1)} %slice.235), channel_id=1, replica_groups={{0,8,16,24,32,40,48,56,64,72,80,88,96,104,112,120,128,136,144,152,160,1..., dimensions={1}, use_global_device_ids=true | all-gather | bytes 608256 | tf_op jit(solution)/shard_map/all_gather | solution.py:246
  105.1 0.8 broadcast_in_dim.75
  105.9 8.0 %all-to-all-start.1 = ((bf16[8,2,72,192]{3,2,1,0:T(8,128)(2,1)}), bf16[8,2,72,192]{3,2,1,0:T(8,128)(2,1)S(1)}, u32[]{:S(2)}, u32[]{:S(2)}) async-start(bf16[8,2,72,192]{3,2,1,0:T(8,128)(2,1)} %broadcast_in_dim.75), calls=%async_computation.1 | async-start | bytes 1179648 | tf_op jit(solution)/shard_map/all_to_all | solution.py:38
  114.3 2.4 %fusion.61 = (bf16[8,1,2,68,96]{4,1,3,2,0:T(2,128)(2,1)S(1)}, bf16[8,1,2,68,96]{4,1,3,2,0:T(2,128)(2,1)S(1)}, bf16[8,1,2,68,96]{4,1,3,2,0:T(2,128)(2,1)S(1)}, bf...) fusion(bf16[8,2,2,72,96]{4,1,3,2,0:T(2,128)(2,1)S(1)} %bitcast.115), kind=kLoop, calls=%fused_computation.120 | loop fusion | bytes 2506752 | tf_op jit(solution)/shard_map/slice | solution.py:241
  117.4 3.0 %concatenate.51 = bf16[8,2,68,480]{3,0,2,1:T(8,128)(2,1)} concatenate(bf16[8,2,68,96]{3,0,2,1:T(8,128)(2,1)S(1)} %get-tuple-element.72, bf16[8,2,68,96]{3,0,2,1:T(8,128)(2,1)S(1)} %get-tuple-element.77, bf16[8,2,68,96]{3,0,2,1:T(8,128)(2,1)S(1)} %get-tuple-element.76, bf16[8,2,68,96]{3,0,2,1:T(8,128)(2,1)S(1)} %get-tuple-element.75, bf16[8,2,68,96]{3,0,2,1:T(8,128)(2,1)S(1)} %get-tuple-element.74), dimensions={3} | concatenate | bytes 2088960 | tf_op jit(solution)/shard_map/concatenate | solution.py:244
  120.3 3.0 %concatenate.50 = bf16[8,2,68,480]{3,0,2,1:T(8,128)(2,1)} concatenate(bf16[8,2,68,96]{3,0,2,1:T(8,128)(2,1)S(1)} %get-tuple-element.77, bf16[8,2,68,96]{3,0,2,1:T(8,128)(2,1)S(1)} %get-tuple-element.76, bf16[8,2,68,96]{3,0,2,1:T(8,128)(2,1)S(1)} %get-tuple-element.75, bf16[8,2,68,96]{3,0,2,1:T(8,128)(2,1)S(1)} %get-tuple-element.74, bf16[8,2,68,96]{3,0,2,1:T(8,128)(2,1)S(1)} %get-tuple-element.73), dimensions={3} | concatenate | bytes 2088960 | tf_op jit(solution)/shard_map/concatenate | solution.py:244
  123.3 2.4 %all-to-all-done.1 = bf16[8,2,72,192]{3,2,1,0:T(8,128)(2,1)S(1)} async-done(((bf16[8,2,72,192]{3,2,1,0:T(8,128)(2,1)}), bf16[8,2,72,192]{3,2,1,0:T(8,128)(2,1)S(1)}, u32[]{:S(2)}, u32[]{:S(2)}) %all-to-all-start.1) | async-done | bytes 442400 | tf_op jit(solution)/shard_map/all_to_all | solution.py:38
  125.9 0.7 copy.477
  126.6 1.3 reshape.182
  128.2 3.0 %fusion = f32[2,72,960]{2,1,0:T(8,128)S(1)} fusion(bf16[1536,2176]{1,0:T(8,128)(2,1)} %bitcast.110, f32[2,72,1536]{2,1,0:T(8,128)} %reshape.182, f32[1536]{0:T(1024)S(1)} %copy-done.13, f32[2,72]{1,0:T(2,128)S(1)} %get-tuple-element.71), kind=kOutput, calls=%fused_computation.1 | convolution fusion | flops 427106304 | bytes 4590144 | tf_op jit(solution)/shard_map/dot_general | solution.py:23
  131.5 1.1 broadcast_in_dim.76
  132.6 4.8 %all-to-all-start.2 = ((bf16[8,2,68,192]{3,1,2,0:T(2,128)(2,1)}), bf16[8,2,68,192]{3,1,2,0:T(2,128)(2,1)S(1)}, u32[]{:S(2)}, u32[]{:S(2)}) async-start(bf16[8,2,68,192]{3,1,2,0:T(2,128)(2,1)} %broadcast_in_dim.76), calls=%async_computation.2 | async-start | bytes 1114112 | tf_op jit(solution)/shard_map/all_to_all | solution.py:38
  137.7 2.2 copy.495.stacked_ref
  139.8 3.3 %fusion.60 = (bf16[2,768,240]{2,1,0:T(8,128)(2,1)}, bf16[2,768,240]{2,1,0:T(8,128)(2,1)S(1)}) fusion(bf16[2,768,2176]{2,1,0:T(8,128)(2,1)} %all-gather.3.cloned.1.call-done), kind=kLoop, calls=%fused_computation.119 | loop fusion | bytes 2949120 | tf_op jit(solution)/shard_map/slice | solution.py:206
  143.4 0.7 copy.494
  144.1 1.3 reshape.175.weight_ref
  145.4 3.2 %fine_back.1 = bf16[272,96]{1,0:T(8,128)(2,1)} custom-call(bf16[8,272,480]{2,1,0:T(8,128)(2,1)} %copy.495.stacked_ref, bf16[8,96,480]{2,1,0:T(8,128)(2,1)} %reshape.175.weight_ref), custom_call_target="tpu_custom_call" | custom-call | tf_op jit(solution)/shard_map/fine_back/pallas_call | solution.py:148
  148.5 0.9 copy.496
  150.1 1.5 fusion.21
  152.1 1.1 broadcast_in_dim.79
  153.2 7.3 %all-to-all-start.3 = ((bf16[8,4,136,96]{3,2,1,0:T(8,128)(2,1)}), bf16[8,4,136,96]{3,2,1,0:T(8,128)(2,1)S(1)}, u32[]{:S(2)}, u32[]{:S(2)}) async-start(bf16[8,4,136,96]{3,2,1,0:T(8,128)(2,1)} %broadcast_in_dim.79), calls=%async_computation.3 | async-start | bytes 2228224 | tf_op jit(solution)/shard_map/all_to_all | solution.py:38
  161.5 1.7 slice.271
  163.2 0.8 copy.500
  164.0 1.5 copy.501
  165.5 3.2 %reshape.177 = bf16[768,480]{1,0:T(8,128)(2,1)} reshape(bf16[2,32,12,2,240]{4,3,2,1,0:T(2,128)(2,1)} %copy.501) | data formatting | bytes 1474560 | tf_op jit(solution)/shard_map/reshape | solution.py:209
  168.7 1.3 reshape.194
  170.0 1.3 copy.539
  171.6 0.8 copy.486
  172.3 4.0 %all-to-all-done.3.shared_ref = bf16[8,4,136,96]{3,2,1,0:T(8,128)(2,1)S(1)} async-done(((bf16[8,4,136,96]{3,2,1,0:T(8,128)(2,1)}), bf16[8,4,136,96]{3,2,1,0:T(8,128)(2,1)S(1)}, u32[]{:S(2)}, u32[]{:S(2)}) %all-to-all-start.3) | async-done | bytes 835616 | tf_op jit(solution)/shard_map/all_to_all | solution.py:38
  176.8 0.6 multiply_reduce_fusion
  177.9 2.9 %copy-done = bf16[2,768,2176]{2,1,0:T(8,128)(2,1)S(1)} copy-done((bf16[2,768,2176]{2,1,0:T(8,128)(2,1)S(1)}, bf16[2,768,2176]{2,1,0:T(8,128)(2,1)}, u32[]{:S(2)}) %copy-start) | copy-done | bytes 6684696
  180.8 4.0 %fine_adjoint.1 = (bf16[8,2,64,192]{3,2,1,0:T(8,128)(2,1)}, bf16[8,2,136,96]{3,2,1,0:T(8,128)(2,1)S(1)}, bf16[2,64,192]{2,1,0:T(8,128)(2,1)S(1)}) custom-call(bf16[8,4,136,96]{3,2,1,0:T(8,128)(2,1)S(1)} %all-to-all-done.3.shared_ref, bf16[8,2,136,96]{3,2,1,0:T(8,128)(2,1)S(1)} %copy.506.cot_ref, f32[8,1,96]{2,1,0:T(1,128)S(1)} %reshape.179.gain_ref, ...), custom_call_target="tpu_custom_call" | custom-call | tf_op jit(solution)/shard_map/fine_adjoint/pallas_call | solution.py:119
  184.8 4.3 %all-to-all-start.4 = ((bf16[8,2,64,192]{3,2,1,0:T(8,128)(2,1)}), bf16[8,2,64,192]{3,2,1,0:T(8,128)(2,1)S(1)}, u32[]{:S(2)}, u32[]{:S(2)}) async-start(bf16[8,2,64,192]{3,2,1,0:T(8,128)(2,1)} %get-tuple-element.8), calls=%async_computation.4 | async-start | bytes 1048576 | tf_op jit(solution)/shard_map/all_to_all | solution.py:38
  189.1 1.8 fusion.10
  191.4 8.1 %all-to-all-done.4 = bf16[8,2,64,192]{3,2,1,0:T(8,128)(2,1)S(1)} async-done(((bf16[8,2,64,192]{3,2,1,0:T(8,128)(2,1)}), bf16[8,2,64,192]{3,2,1,0:T(8,128)(2,1)S(1)}, u32[]{:S(2)}, u32[]{:S(2)}) %all-to-all-start.4) | async-done | bytes 393248 | tf_op jit(solution)/shard_map/all_to_all | solution.py:38
  200.4 0.8 broadcast_in_dim.84
  201.2 3.5 %all-to-all-start.5 = ((bf16[8,2,64,256]{3,2,1,0:T(8,128)(2,1)}), bf16[8,2,64,256]{3,2,1,0:T(8,128)(2,1)S(1)}, u32[]{:S(2)}, u32[]{:S(2)}) async-start(bf16[8,2,64,256]{3,2,1,0:T(8,128)(2,1)} %broadcast_in_dim.84), calls=%async_computation.5 | async-start | bytes 1048576 | tf_op jit(solution)/shard_map/all_to_all | solution.py:38
  205.8 0.7 copy.513
  206.6 0.7 copy.514
  207.4 7.7 %all-to-all-done.5 = bf16[8,2,64,256]{3,2,1,0:T(8,128)(2,1)S(1)} async-done(((bf16[8,2,64,256]{3,2,1,0:T(8,128)(2,1)}), bf16[8,2,64,256]{3,2,1,0:T(8,128)(2,1)S(1)}, u32[]{:S(2)}, u32[]{:S(2)}) %all-to-all-start.5) | async-done | bytes 524320 | tf_op jit(solution)/shard_map/all_to_all | solution.py:38
  215.2 0.6 copy.511
  215.8 1.2 reshape.184
  217.4 2.3 %convolution_convert_fusion = bf16[2,64,192]{2,1,0:T(8,128)(2,1)} fusion(bf16[1536,2176]{1,0:T(8,128)(2,1)} %bitcast.113, f32[2,64,1536]{2,1,0:T(8,128)} %reshape.184, f32[2,72,1536]{2,1,0:T(8,128)S(1)} %copy-done.6, f32[2,64]{1,0:T(2,128)S(1)} %fusion.52), kind=kOutput, calls=%fused_computation.10 | convolution fusion | flops 76111872 | bytes 2409472 | tf_op jit(solution)/shard_map/dot_general | solution.py:23
  (113 shorter events, 9.7 us)
Async XLA Ops:
  7.2 18.0 %copy-start.9 = (bf16[2,128,96]{1,2,0:T(8,128)(2,1)S(1)}, bf16[2,128,96]{1,2,0:T(8,128)(2,1)}, u32[]{:S(2)}) copy-start(bf16[2,128,96]{1,2,0:T(8,128)(2,1)} %param.17) | copy-start | bytes 147460
  7.2 33.3 %copy-start.10 = (bf16[2,64,192]{2,1,0:T(8,128)(2,1)S(1)}, bf16[2,64,192]{2,1,0:T(8,128)(2,1)}, u32[]{:S(2)}) copy-start(bf16[2,64,192]{2,1,0:T(8,128)(2,1)} %param.9) | copy-start | bytes 147460
  7.2 121.0 %all-gather.3.cloned.1.call-start = ((), (), s32[]{:S(2)}) async-start(), calls=%async_computation.6 | async-start | bytes 6893568 | tf_op jit(solution)/shard_map/all_gather | solution.py:196
  9.7 8.2 %collective-permute-start.4 = (bf16[24,624]{1,0:T(8,128)(2,1)S(1)}, bf16[24,624]{1,0:T(8,128)(2,1)S(1)}, u32[]{:S(2)}, u32[]{:S(2)}) collective-permute-start(bf16[24,624]{1,0:T(8,128)(2,1)S(1)} %maximum_maximum_fusion.1), channel_id=1, source_target_pairs={{0,0},{1,64},{2,128},{3,192},{4,256},{5,320},{6,384},{7,448},{8,8}... | collective-permute-start | bytes 89864 | tf_op jit(solution)/shard_map/ppermute | solution.py:173
  25.3 22.9 %collective-permute-start.3 = (bf16[2,8,96]{1,2,0:T(8,128)(2,1)S(1)}, bf16[2,8,96]{1,2,0:T(8,128)(2,1)S(1)}, u32[]{:S(2)}, u32[]{:S(2)}) collective-permute-start(bf16[2,8,96]{1,2,0:T(8,128)(2,1)S(1)} %get-tuple-element.65), channel_id=1, source_target_pairs={{8,0},{16,8},{24,16},{32,24},{40,32},{48,40},{56,48},{64,56},{72,6... | collective-permute-start | bytes 9224 | tf_op jit(solution)/shard_map/ppermute | solution.py:50
  38.5 9.7 %collective-permute-start.2 = (bf16[2,8,96]{1,2,0:T(8,128)(2,1)S(1)}, bf16[2,8,96]{1,2,0:T(8,128)(2,1)S(1)}, u32[]{:S(2)}, u32[]{:S(2)}) collective-permute-start(bf16[2,8,96]{1,2,0:T(8,128)(2,1)S(1)} %get-tuple-element.64), channel_id=1, source_target_pairs={{0,8},{8,16},{16,24},{24,32},{32,40},{40,48},{48,56},{56,64},{64,7... | collective-permute-start | bytes 9224 | tf_op jit(solution)/shard_map/ppermute | solution.py:49
  40.5 8.1 %collective-permute-start.1 = (bf16[2,4,192]{2,1,0:T(4,128)(2,1)S(1)}, bf16[2,4,192]{2,1,0:T(4,128)(2,1)S(1)}, u32[]{:S(2)}, u32[]{:S(2)}) collective-permute-start(bf16[2,4,192]{2,1,0:T(4,128)(2,1)S(1)} %get-tuple-element.63), channel_id=1, source_target_pairs={{8,0},{16,8},{24,16},{32,24},{40,32},{48,40},{56,48},{64,56},{72,6... | collective-permute-start | bytes 9224 | tf_op jit(solution)/shard_map/ppermute | solution.py:50
  46.2 7.1 %collective-permute-start = (bf16[2,4,192]{2,1,0:T(4,128)(2,1)S(1)}, bf16[2,4,192]{2,1,0:T(4,128)(2,1)S(1)}, u32[]{:S(2)}, u32[]{:S(2)}) collective-permute-start(bf16[2,4,192]{2,1,0:T(4,128)(2,1)S(1)} %get-tuple-element.62), channel_id=1, source_target_pairs={{0,8},{8,16},{16,24},{24,32},{32,40},{40,48},{48,56},{56,64},{64,7... | collective-permute-start | bytes 9224 | tf_op jit(solution)/shard_map/ppermute | solution.py:49
  54.5 9.7 %copy-start.11 = (bf16[2,128,96]{1,2,0:T(8,128)(2,1)S(1)}, bf16[2,128,96]{1,2,0:T(8,128)(2,1)}, u32[]{:S(2)}) copy-start(bf16[2,128,96]{1,2,0:T(8,128)(2,1)} %param.14) | copy-start | bytes 147460
  54.5 50.1 %all-to-all-start = ((bf16[8,4,72,192]{3,2,1,0:T(8,128)(2,1)}), bf16[8,4,72,192]{3,2,1,0:T(8,128)(2,1)S(1)}, u32[]{:S(2)}, u32[]{:S(2)}) async-start(bf16[8,4,72,192]{3,2,1,0:T(8,128)(2,1)} %broadcast_in_dim.39), calls=%async_computation | async-start | bytes 2359296 | tf_op jit(solution)/shard_map/all_to_all | solution.py:38
  64.3 4.4 %collective-permute-start.6 = (bf16[2,4,96]{2,1,0:T(4,128)(2,1)S(1)}, bf16[2,4,96]{2,1,0:T(4,128)(2,1)S(1)}, u32[]{:S(2)}, u32[]{:S(2)}) collective-permute-start(bf16[2,4,96]{2,1,0:T(4,128)(2,1)S(1)} %get-tuple-element.61), channel_id=1, source_target_pairs={{8,0},{16,8},{24,16},{32,24},{40,32},{48,40},{56,48},{64,56},{72,6... | collective-permute-start | bytes 4616 | tf_op jit(solution)/shard_map/ppermute | solution.py:50
  66.3 7.0 %collective-permute-start.5 = (bf16[2,4,96]{2,1,0:T(4,128)(2,1)S(1)}, bf16[2,4,96]{2,1,0:T(4,128)(2,1)S(1)}, u32[]{:S(2)}, u32[]{:S(2)}) collective-permute-start(bf16[2,4,96]{2,1,0:T(4,128)(2,1)S(1)} %get-tuple-element.60), channel_id=1, source_target_pairs={{0,8},{8,16},{16,24},{24,32},{32,40},{40,48},{48,56},{56,64},{64,7... | collective-permute-start | bytes 4616 | tf_op jit(solution)/shard_map/ppermute | solution.py:49
  105.9 19.8 %all-to-all-start.1 = ((bf16[8,2,72,192]{3,2,1,0:T(8,128)(2,1)}), bf16[8,2,72,192]{3,2,1,0:T(8,128)(2,1)S(1)}, u32[]{:S(2)}, u32[]{:S(2)}) async-start(bf16[8,2,72,192]{3,2,1,0:T(8,128)(2,1)} %broadcast_in_dim.75), calls=%async_computation.1 | async-start | bytes 1179648 | tf_op jit(solution)/shard_map/all_to_all | solution.py:38
  126.6 1.6 copy-start.13
  131.3 6.0 %copy-start.3 = (bf16[8,2,68,480]{3,0,2,1:T(8,128)(2,1)S(1)}, bf16[8,2,68,480]{3,0,2,1:T(8,128)(2,1)}, u32[]{:S(2)}) copy-start(bf16[8,2,68,480]{3,0,2,1:T(8,128)(2,1)} %concatenate.50) | copy-start | bytes 3133444
  131.4 6.0 %copy-start.2 = (bf16[8,2,68,480]{3,0,2,1:T(8,128)(2,1)S(1)}, bf16[8,2,68,480]{3,0,2,1:T(8,128)(2,1)}, u32[]{:S(2)}) copy-start(bf16[8,2,68,480]{3,0,2,1:T(8,128)(2,1)} %concatenate.51) | copy-start | bytes 3133444
  132.6 16.9 %all-to-all-start.2 = ((bf16[8,2,68,192]{3,1,2,0:T(2,128)(2,1)}), bf16[8,2,68,192]{3,1,2,0:T(2,128)(2,1)S(1)}, u32[]{:S(2)}, u32[]{:S(2)}) async-start(bf16[8,2,68,192]{3,1,2,0:T(2,128)(2,1)} %broadcast_in_dim.76), calls=%async_computation.2 | async-start | bytes 1114112 | tf_op jit(solution)/shard_map/all_to_all | solution.py:38
  150.1 1.6 copy-start.7
  153.2 7.3 %copy-start.12 = (f32[768]{0:T(1024)S(1)}, f32[768]{0:T(1024)}, u32[]{:S(2)}) copy-start(f32[768]{0:T(1024)} %param.15) | copy-start | bytes 9220
  153.2 23.1 %all-to-all-start.3 = ((bf16[8,4,136,96]{3,2,1,0:T(8,128)(2,1)}), bf16[8,4,136,96]{3,2,1,0:T(8,128)(2,1)S(1)}, u32[]{:S(2)}, u32[]{:S(2)}) async-start(bf16[8,4,136,96]{3,2,1,0:T(8,128)(2,1)} %broadcast_in_dim.79), calls=%async_computation.3 | async-start | bytes 2228224 | tf_op jit(solution)/shard_map/all_to_all | solution.py:38
  161.3 1.8 copy-start.5
  176.8 1.0 copy-start.1
  177.9 2.9 %copy-start = (bf16[2,768,2176]{2,1,0:T(8,128)(2,1)S(1)}, bf16[2,768,2176]{2,1,0:T(8,128)(2,1)}, u32[]{:S(2)}) copy-start(bf16[2,768,2176]{2,1,0:T(8,128)(2,1)} %all-gather.3.cloned.1.call-done) | copy-start | bytes 20054020
  184.8 14.7 %all-to-all-start.4 = ((bf16[8,2,64,192]{3,2,1,0:T(8,128)(2,1)}), bf16[8,2,64,192]{3,2,1,0:T(8,128)(2,1)S(1)}, u32[]{:S(2)}, u32[]{:S(2)}) async-start(bf16[8,2,64,192]{3,2,1,0:T(8,128)(2,1)} %get-tuple-element.8), calls=%async_computation.4 | async-start | bytes 1048576 | tf_op jit(solution)/shard_map/all_to_all | solution.py:38
  199.9 4.8 %copy-start.4 = (bf16[768,480]{1,0:T(8,128)(2,1)S(1)}, bf16[768,480]{1,0:T(8,128)(2,1)}, u32[]{:S(2)}) copy-start(bf16[768,480]{1,0:T(8,128)(2,1)} %reshape.177) | copy-start | bytes 2211844
  201.2 13.9 %all-to-all-start.5 = ((bf16[8,2,64,256]{3,2,1,0:T(8,128)(2,1)}), bf16[8,2,64,256]{3,2,1,0:T(8,128)(2,1)S(1)}, u32[]{:S(2)}, u32[]{:S(2)}) async-start(bf16[8,2,64,256]{3,2,1,0:T(8,128)(2,1)} %broadcast_in_dim.84), calls=%async_computation.5 | async-start | bytes 1048576 | tf_op jit(solution)/shard_map/all_to_all | solution.py:38
  204.7 0.9 copy-start.8
  215.8 1.5 copy-start.6
Sparse Core Ops, SparseCore 0:
  25.3 88.6 all-gather.2

commit v5 on v4

--- a/solution.py
+++ b/solution.py
@@ -42,13 +42,23 @@
     return exchange(jnp.broadcast_to(piece[None], (NT,) + piece.shape))
 
 
-def neighbours(shard, width):
-    size, length = lax.axis_size("seq"), shard.shape[1]
+def neighbours(trunk, cotangent, skip):
+    size = lax.axis_size("seq")
     up = [(i, i + 1) for i in range(size - 1)]
     down = [(j, i) for i, j in up]
-    before = lax.ppermute(shard[:, length - width :], "seq", up)
-    after = lax.ppermute(shard[:, :width], "seq", down)
-    return jnp.concatenate([before, shard, after], axis=1)
+
+    def edge(coarse, fine):
+        both = jnp.concatenate([cotangent[:, fine], skip[:, fine]], axis=2)
+        return jnp.concatenate([trunk[:, coarse], both], axis=1)
+
+    before = lax.ppermute(edge(slice(-4, None), slice(-8, None)), "seq", up)
+    after = lax.ppermute(edge(slice(0, 4), slice(0, 8)), "seq", down)
+    part = cotangent.shape[2]
+    return (
+        jnp.concatenate([before[:, :4], trunk, after[:, :4]], axis=1),
+        jnp.concatenate([before[:, 4:, :part], cotangent, after[:, 4:, :part]], axis=1),
+        jnp.concatenate([before[:, 8:, part:], skip, after[:, 4:8, part:]], axis=1),
+    )
 
 
 def lanes(blocks):
@@ -56,8 +66,10 @@
     return moved.reshape(moved.shape[:2] + (-1,))
 
 
-def fine_adjoint(shared_ref, cot_ref, gain_ref, inside_ref, up_ref, conv_ref, back_ref, grad_ref, lifted_ref, norm_ref, rows_ref, taps_ref):
+def fine_adjoint(shared_ref, cot_ref, gain_ref, inside_ref, up_ref, conv_ref, back_ref, grad_ref, lifted_ref, norm_ref, rows_ref, taps_ref, held_ref, fetched):
     slab, rows = back_ref.shape[2], rows_ref.shape[1]
+    fetch = pltpu.make_async_copy(conv_ref.at[:, pl.ds(0, 1024)], held_ref, fetched)
+    fetch.start()
     for p in range(2):
         square = jnp.zeros(shared_ref.shape[2:], F32)
         for t in range(NT):
@@ -98,8 +110,9 @@
             if k < 4:
                 tail = tail + pltpu.roll(rows_ref[s, 3 - k : 3 - k + slab, 128:256], 64, 1)
             taps_ref[s * slab : (s + 1) * slab, 640 + k * 64 : 768 + k * 64] = tail.astype(BF16)
+    fetch.wait()
     for t in range(NT):
-        back = dot_t(taps_ref[...], conv_ref[192 * t : 192 * (t + 1), :]).astype(BF16)
+        back = dot_t(taps_ref[...], held_ref[192 * t : 192 * (t + 1), :]).astype(BF16)
         for s in range(2):
             back_ref[t, s] = back[s * slab : (s + 1) * slab]
 
@@ -118,8 +131,7 @@
     rows = shared.shape[2] // 2
     return pl.pallas_call(
         fine_adjoint,
-        grid=(1,),
-        in_specs=[whole] * 5 + [pl.BlockSpec((C_COARSE, 1024), lambda i: (0, 0))],
+        in_specs=[whole] * 5 + [pl.BlockSpec(memory_space=pltpu.HBM)],
         out_specs=[whole] * 3,
         out_shape=[
             jax.ShapeDtypeStruct((NT, 2, slab, 192), BF16),
@@ -130,6 +142,8 @@
             pltpu.VMEM((NT,) + shared.shape[2:], F32),
             pltpu.VMEM((2, rows, 256), F32),
             pltpu.VMEM((2 * slab, 1024), BF16),
+            pltpu.VMEM((C_COARSE, 1024), BF16),
+            pltpu.SemaphoreType.DMA,
         ],
         compiler_params=pltpu.CompilerParams(vmem_limit_bytes=40 * 2**20),
         name="fine_adjoint",
@@ -216,9 +230,7 @@
         .reshape(NT, part_fine, 480)
     )
 
-    trunk_ext = neighbours(trunk, 4)
-    skip_ext = neighbours(skip, 4)
-    cot_ext = neighbours(cotangent, 8)
+    trunk_ext, cot_ext, skip_ext = neighbours(trunk, cotangent, skip)
     fine_rows = 2 * slab + 8
     index = place * slab - 2 + lax.broadcasted_iota(jnp.int32, (1, slab + 4, 1), 1)
     inside = (index >= 0) & (index < slab * lax.axis_size("seq"))

time: 228 us -> 216 us (0.947)
  the two profiles are of different devices: /device:TPU:8 before, /device:TPU:32 now
where the time goes in v5:
time: 216 us; the launch traced here: 215 us
  local copies, waits for them, and re-layouts  51.3 us (24%)
  blocking collectives  51 us (24%)
  starting transfers between devices  48.2 us (22%)
  waiting for transfers between devices  28 us (13%)
  between operations  14.7 us (7%)
  Pallas kernels  7.84 us (4%)
  matrix products  7.33 us (3%)
  other arithmetic  6.41 us (3%)
    all_to_all x6, starting transfers between devices, exchange(): return lax.all_to_all(blocks, 'tensor', 0, 0)  43.2 us
    all_gather x1, blocking collectives, per_device(): lax.all_gather(paired[:, :, :192], 'seq', axis=1, tiled=True, axis_index_...  40.1 us
    all_to_all x6, waiting for transfers between devices, exchange(): return lax.all_to_all(blocks, 'tensor', 0, 0)  23 us
    all_gather x1, blocking collectives, per_device(): paired = lax.all_gather(packed, 'seq', axis=0, axis_index_groups=Y_PAIRS)  10.9 us
    dot_general x4, matrix products, dot(): lax.dot_general(left, right, (((left.ndim - 1,), (0,)), ((), ())), prefer...  6.93 us
    concatenate x2, local copies, waits for them, and re-layouts, per_device(): jnp.concatenate([tap(p, k) for k in range(5)], axis=-1)  5.96 us
    unnamed x35, local copies, waits for them, and re-layouts  5.58 us
    broadcast_in_dim x6, local copies, waits for them, and re-layouts, share(): return exchange(jnp.broadcast_to(piece[None], (NT,) + piece.shape))  5.05 us
  transfers between devices with their start and end apart: 10, of which 6 were waited for; matrix products, arithmetic and copies ran while one was open for 19% of the time, Pallas kernels for 1%

profile of v5, /device:TPU:32, one launch (start us, length us, event | category | flops | bytes accessed | tf_op | source)
XLA Modules:
  0.0 214.8 jit_solution(9999859972584578822)
XLA Ops:
  7.2 0.8 copy.528
  8.2 0.8 reshape.165
  9.0 0.8 maximum_maximum_fusion.1
  9.8 0.7 collective-permute-start.2
  10.4 0.8 copy_bitcast_fusion.7
  11.2 0.8 slice.262
  12.2 0.8 concatenate.62
  13.0 10.9 %all-gather = bf16[48,2368]{1,0:T(8,128)(2,1)S(1)} all-gather(bf16[24,2368]{1,0:T(8,128)(2,1)S(1)} %concatenate.62), channel_id=2, replica_groups={{0,256},{8,264},{16,272},{24,280},{32,288},{40,296},{48,304},{56,312},{..., dimensions={0}, use_global_device_ids=true | all-gather | bytes 340992 | tf_op jit(solution)/shard_map/all_gather | solution.py:209
  23.9 0.8 slice.267
  25.1 1.9 collective-permute-start.1
  27.2 2.4 %collective-permute-start = (bf16[2,12,192]{2,1,0:T(8,128)(2,1)S(1)}, bf16[2,12,192]{2,1,0:T(8,128)(2,1)S(1)}, u32[]{:S(2)}, u32[]{:S(2)}) collective-permute-start(bf16[2,12,192]{2,1,0:T(8,128)(2,1)S(1)} %maximum_maximum_fusion.2), channel_id=1, source_target_pairs={{0,8},{8,16},{16,24},{24,32},{32,40},{40,48},{48,56},{56,64},{64,7... | collective-permute-start | bytes 27656 | tf_op jit(solution)/shard_map/ppermute | solution.py:54
  29.8 2.5 %collective-permute-done = bf16[2,12,192]{2,1,0:T(8,128)(2,1)S(1)} collective-permute-done((bf16[2,12,192]{2,1,0:T(8,128)(2,1)S(1)}, bf16[2,12,192]{2,1,0:T(8,128)(2,1)S(1)}, u32[]{:S(2)}, u32[]{:S(2)}) %collective-permute-start) | collective-permute-done | bytes 9248 | tf_op jit(solution)/shard_map/ppermute | solution.py:54
  32.8 1.1 broadcast_in_dim.39
  33.9 13.9 %all-to-all-start = ((bf16[8,4,72,192]{3,2,1,0:T(8,128)(2,1)}), bf16[8,4,72,192]{3,2,1,0:T(8,128)(2,1)S(1)}, u32[]{:S(2)}, u32[]{:S(2)}) async-start(bf16[8,4,72,192]{3,2,1,0:T(8,128)(2,1)} %broadcast_in_dim.39), calls=%async_computation | async-start | bytes 2359296 | tf_op jit(solution)/shard_map/all_to_all | solution.py:38
  48.0 0.7 maximum_convert_fusion
  48.7 40.1 %all_gather.14 = bf16[2,768,192]{2,1,0:T(8,128)(2,1)S(1)} all-gather(bf16[2,24,192]{2,1,0:T(8,128)(2,1)S(1)} %slice.265), channel_id=1, replica_groups={{0,8,16,24,32,40,48,56,64,72,80,88,96,104,112,120,128,136,144,152,160,1..., dimensions={1}, use_global_device_ids=true | all-gather | bytes 608256 | tf_op jit(solution)/shard_map/all_gather | solution.py:258
  88.8 0.4 fusion.2
  89.2 0.8 broadcast_in_dim.75
  90.1 6.9 %all-to-all-start.1 = ((bf16[8,2,72,192]{3,2,1,0:T(8,128)(2,1)}), bf16[8,2,72,192]{3,2,1,0:T(8,128)(2,1)S(1)}, u32[]{:S(2)}, u32[]{:S(2)}) async-start(bf16[8,2,72,192]{3,2,1,0:T(8,128)(2,1)} %broadcast_in_dim.75), calls=%async_computation.1 | async-start | bytes 1179648 | tf_op jit(solution)/shard_map/all_to_all | solution.py:38
  97.4 2.4 %fusion.61 = (bf16[8,1,2,68,96]{4,1,3,2,0:T(2,128)(2,1)S(1)}, bf16[8,1,2,68,96]{4,1,3,2,0:T(2,128)(2,1)S(1)}, bf16[8,1,2,68,96]{4,1,3,2,0:T(2,128)(2,1)S(1)}, bf...) fusion(bf16[8,2,2,72,96]{4,1,3,2,0:T(2,128)(2,1)S(1)} %bitcast.115), kind=kLoop, calls=%fused_computation.122 | loop fusion | bytes 2506752 | tf_op jit(solution)/shard_map/slice | solution.py:253
  100.4 3.0 %concatenate.67 = bf16[8,2,68,480]{3,0,2,1:T(8,128)(2,1)} concatenate(bf16[8,2,68,96]{3,0,2,1:T(8,128)(2,1)S(1)} %get-tuple-element.74, bf16[8,2,68,96]{3,0,2,1:T(8,128)(2,1)S(1)} %get-tuple-element.79, bf16[8,2,68,96]{3,0,2,1:T(8,128)(2,1)S(1)} %get-tuple-element.78, bf16[8,2,68,96]{3,0,2,1:T(8,128)(2,1)S(1)} %get-tuple-element.77, bf16[8,2,68,96]{3,0,2,1:T(8,128)(2,1)S(1)} %get-tuple-element.76), dimensions={3} | concatenate | bytes 2088960 | tf_op jit(solution)/shard_map/concatenate | solution.py:256
  103.4 3.0 %concatenate.66 = bf16[8,2,68,480]{3,0,2,1:T(8,128)(2,1)} concatenate(bf16[8,2,68,96]{3,0,2,1:T(8,128)(2,1)S(1)} %get-tuple-element.79, bf16[8,2,68,96]{3,0,2,1:T(8,128)(2,1)S(1)} %get-tuple-element.78, bf16[8,2,68,96]{3,0,2,1:T(8,128)(2,1)S(1)} %get-tuple-element.77, bf16[8,2,68,96]{3,0,2,1:T(8,128)(2,1)S(1)} %get-tuple-element.76, bf16[8,2,68,96]{3,0,2,1:T(8,128)(2,1)S(1)} %get-tuple-element.75), dimensions={3} | concatenate | bytes 2088960 | tf_op jit(solution)/shard_map/concatenate | solution.py:256
  106.4 2.4 %all-to-all-done.1 = bf16[8,2,72,192]{3,2,1,0:T(8,128)(2,1)S(1)} async-done(((bf16[8,2,72,192]{3,2,1,0:T(8,128)(2,1)}), bf16[8,2,72,192]{3,2,1,0:T(8,128)(2,1)S(1)}, u32[]{:S(2)}, u32[]{:S(2)}) %all-to-all-start.1) | async-done | bytes 442400 | tf_op jit(solution)/shard_map/all_to_all | solution.py:38
  108.9 0.7 copy.531
  109.6 0.4 reshape.182
  110.3 2.5 %all-gather.3.cloned.1.call-done = bf16[2,768,2176]{2,1,0:T(8,128)(2,1)} async-done(((bf16[2,24,2176]{2,1,0:T(8,128)(2,1)}), bf16[2,768,2176]{2,1,0:T(8,128)(2,1)}) %all-gather.3.cloned.1.call-update) | async-done | bytes 6684688 | tf_op jit(solution)/shard_map/all_gather | solution.py:210
  112.8 2.8 %fusion = f32[2,72,960]{2,1,0:T(8,128)S(1)} fusion(bf16[1536,2176]{1,0:T(8,128)(2,1)} %bitcast.110, f32[2,72,1536]{2,1,0:T(8,128)S(1)} %reshape.182, f32[1536]{0:T(1024)S(1)} %copy-done.14, f32[2,72]{1,0:T(2,128)S(1)} %get-tuple-element.71), kind=kOutput, calls=%fused_computation.1 | convolution fusion | flops 427106304 | bytes 4590144 | tf_op jit(solution)/shard_map/dot_general | solution.py:23
  115.8 1.1 broadcast_in_dim.76
  116.9 7.6 %all-to-all-start.2 = ((bf16[8,2,68,192]{3,1,2,0:T(2,128)(2,1)}), bf16[8,2,68,192]{3,1,2,0:T(2,128)(2,1)S(1)}, u32[]{:S(2)}, u32[]{:S(2)}) async-start(bf16[8,2,68,192]{3,1,2,0:T(2,128)(2,1)} %broadcast_in_dim.76), calls=%async_computation.2 | async-start | bytes 1114112 | tf_op jit(solution)/shard_map/all_to_all | solution.py:38
  124.8 2.2 %copy.547.stacked_ref = bf16[8,272,480]{2,1,0:T(8,128)(2,1)} copy(bf16[8,272,480]{2,0,1:T(8,128)(2,1)S(1)} %bitcast.119) | data formatting | bytes 4177920 | tf_op jit(solution)/shard_map/reshape | solution.py:257
  126.9 3.4 %fusion.60 = (bf16[2,768,240]{2,1,0:T(8,128)(2,1)}, bf16[2,768,240]{2,1,0:T(8,128)(2,1)S(1)}) fusion(bf16[2,768,2176]{2,1,0:T(8,128)(2,1)} %all-gather.3.cloned.1.call-done), kind=kLoop, calls=%fused_computation.121 | loop fusion | bytes 2949120 | tf_op jit(solution)/shard_map/slice | solution.py:220
  130.6 0.7 copy.546
  131.2 1.3 reshape.175.weight_ref
  132.5 3.2 %fine_back.1 = bf16[272,96]{1,0:T(8,128)(2,1)} custom-call(bf16[8,272,480]{2,1,0:T(8,128)(2,1)} %copy.547.stacked_ref, bf16[8,96,480]{2,1,0:T(8,128)(2,1)} %reshape.175.weight_ref), custom_call_target="tpu_custom_call" | custom-call | tf_op jit(solution)/shard_map/fine_back/pallas_call | solution.py:162
  135.7 0.9 copy.548
  136.8 0.5 reshape.171
  137.3 1.5 fusion.21
  139.2 1.2 broadcast_in_dim.79
  140.4 7.3 %all-to-all-start.3 = ((bf16[8,4,136,96]{3,2,1,0:T(8,128)(2,1)}), bf16[8,4,136,96]{3,2,1,0:T(8,128)(2,1)S(1)}, u32[]{:S(2)}, u32[]{:S(2)}) async-start(bf16[8,4,136,96]{3,2,1,0:T(8,128)(2,1)} %broadcast_in_dim.79), calls=%async_computation.3 | async-start | bytes 2228224 | tf_op jit(solution)/shard_map/all_to_all | solution.py:38
  148.7 1.7 slice.301
  150.3 0.8 copy.552
  151.2 1.5 copy.553
  152.7 3.2 %reshape.177 = bf16[768,480]{1,0:T(8,128)(2,1)} reshape(bf16[2,32,12,2,240]{4,3,2,1,0:T(2,128)(2,1)} %copy.553) | data formatting | bytes 1474560 | tf_op jit(solution)/shard_map/reshape | solution.py:223
  155.9 1.3 reshape.194
  157.2 1.3 copy.593
  158.8 0.8 copy.538
  159.5 4.8 %all-to-all-done.3.shared_ref = bf16[8,4,136,96]{3,2,1,0:T(8,128)(2,1)S(1)} async-done(((bf16[8,4,136,96]{3,2,1,0:T(8,128)(2,1)}), bf16[8,4,136,96]{3,2,1,0:T(8,128)(2,1)S(1)}, u32[]{:S(2)}, u32[]{:S(2)}) %all-to-all-start.3) | async-done | bytes 835616 | tf_op jit(solution)/shard_map/all_to_all | solution.py:38
  164.7 0.6 multiply_reduce_fusion
  165.3 0.4 copy-done.1
  165.8 2.9 %copy-done = bf16[2,768,2176]{2,1,0:T(8,128)(2,1)S(1)} copy-done((bf16[2,768,2176]{2,1,0:T(8,128)(2,1)S(1)}, bf16[2,768,2176]{2,1,0:T(8,128)(2,1)}, u32[]{:S(2)}) %copy-start) | copy-done | bytes 6684696
  168.7 4.7 %fine_adjoint.1 = (bf16[8,2,64,192]{3,2,1,0:T(8,128)(2,1)}, bf16[8,2,136,96]{3,2,1,0:T(8,128)(2,1)S(1)}, bf16[2,64,192]{2,1,0:T(8,128)(2,1)S(1)}) custom-call(bf16[8,4,136,96]{3,2,1,0:T(8,128)(2,1)S(1)} %all-to-all-done.3.shared_ref, bf16[8,2,136,96]{3,2,1,0:T(8,128)(2,1)S(1)} %copy.558.cot_ref, f32[8,1,96]{2,1,0:T(1,128)S(1)} %reshape.179.gain_ref, ...), custom_call_target="tpu_custom_call" | custom-call | tf_op jit(solution)/shard_map/fine_adjoint/pallas_call | solution.py:132
  173.4 3.9 %all-to-all-start.4 = ((bf16[8,2,64,192]{3,2,1,0:T(8,128)(2,1)}), bf16[8,2,64,192]{3,2,1,0:T(8,128)(2,1)S(1)}, u32[]{:S(2)}, u32[]{:S(2)}) async-start(bf16[8,2,64,192]{3,2,1,0:T(8,128)(2,1)} %get-tuple-element.8), calls=%async_computation.4 | async-start | bytes 1048576 | tf_op jit(solution)/shard_map/all_to_all | solution.py:38
  177.4 1.8 fusion.10
  179.2 0.4 convert_element_type.161
  179.7 8.1 %all-to-all-done.4 = bf16[8,2,64,192]{3,2,1,0:T(8,128)(2,1)S(1)} async-done(((bf16[8,2,64,192]{3,2,1,0:T(8,128)(2,1)}), bf16[8,2,64,192]{3,2,1,0:T(8,128)(2,1)S(1)}, u32[]{:S(2)}, u32[]{:S(2)}) %all-to-all-start.4) | async-done | bytes 393248 | tf_op jit(solution)/shard_map/all_to_all | solution.py:38
  188.7 0.8 broadcast_in_dim.84
  189.5 3.5 %all-to-all-start.5 = ((bf16[8,2,64,256]{3,2,1,0:T(8,128)(2,1)}), bf16[8,2,64,256]{3,2,1,0:T(8,128)(2,1)S(1)}, u32[]{:S(2)}, u32[]{:S(2)}) async-start(bf16[8,2,64,256]{3,2,1,0:T(8,128)(2,1)} %broadcast_in_dim.84), calls=%async_computation.5 | async-start | bytes 1048576 | tf_op jit(solution)/shard_map/all_to_all | solution.py:38
  193.4 0.5 copy-done.9
  194.1 0.7 copy.565
  195.0 0.7 copy.566
  195.7 7.7 %all-to-all-done.5 = bf16[8,2,64,256]{3,2,1,0:T(8,128)(2,1)S(1)} async-done(((bf16[8,2,64,256]{3,2,1,0:T(8,128)(2,1)}), bf16[8,2,64,256]{3,2,1,0:T(8,128)(2,1)S(1)}, u32[]{:S(2)}, u32[]{:S(2)}) %all-to-all-start.5) | async-done | bytes 524320 | tf_op jit(solution)/shard_map/all_to_all | solution.py:38
  203.5 0.6 copy.563
  204.1 1.2 reshape.184
  205.7 2.3 %convolution_convert_fusion = bf16[2,64,192]{2,1,0:T(8,128)(2,1)} fusion(bf16[1536,2176]{1,0:T(8,128)(2,1)} %bitcast.113, f32[2,64,1536]{2,1,0:T(8,128)} %reshape.184, f32[2,72,1536]{2,1,0:T(8,128)S(1)} %copy-done.7, f32[2,64]{1,0:T(2,128)S(1)} %fusion.52), kind=kOutput, calls=%fused_computation.10 | convolution fusion | flops 76111872 | bytes 2409472 | tf_op jit(solution)/shard_map/dot_general | solution.py:23
  (118 shorter events, 8.1 us)
Async XLA Ops:
  7.2 17.6 %copy-start.12 = (bf16[2,128,96]{1,2,0:T(8,128)(2,1)S(1)}, bf16[2,128,96]{1,2,0:T(8,128)(2,1)}, u32[]{:S(2)}) copy-start(bf16[2,128,96]{1,2,0:T(8,128)(2,1)} %param.14) | copy-start | bytes 147460
  7.2 17.7 %copy-start.10 = (bf16[2,128,96]{1,2,0:T(8,128)(2,1)S(1)}, bf16[2,128,96]{1,2,0:T(8,128)(2,1)}, u32[]{:S(2)}) copy-start(bf16[2,128,96]{1,2,0:T(8,128)(2,1)} %param.17) | copy-start | bytes 147460
  7.2 105.6 %all-gather.3.cloned.1.call-start = ((), (), s32[]{:S(2)}) async-start(), calls=%async_computation.6 | async-start | bytes 6893568 | tf_op jit(solution)/shard_map/all_gather | solution.py:210
  7.2 17.8 %copy-start.11 = (bf16[2,64,192]{2,1,0:T(8,128)(2,1)S(1)}, bf16[2,64,192]{2,1,0:T(8,128)(2,1)}, u32[]{:S(2)}) copy-start(bf16[2,64,192]{2,1,0:T(8,128)(2,1)} %param.9) | copy-start | bytes 147460
  9.8 2.3 %collective-permute-start.2 = (bf16[24,624]{1,0:T(8,128)(2,1)S(1)}, bf16[24,624]{1,0:T(8,128)(2,1)S(1)}, u32[]{:S(2)}, u32[]{:S(2)}) collective-permute-start(bf16[24,624]{1,0:T(8,128)(2,1)S(1)} %maximum_maximum_fusion.1), channel_id=1, source_target_pairs={{0,0},{1,64},{2,128},{3,192},{4,256},{5,320},{6,384},{7,448},{8,8}... | collective-permute-start | bytes 89864 | tf_op jit(solution)/shard_map/ppermute | solution.py:187
  25.1 4.5 %collective-permute-start.1 = (bf16[2,12,192]{2,1,0:T(8,128)(2,1)S(1)}, bf16[2,12,192]{2,1,0:T(8,128)(2,1)S(1)}, u32[]{:S(2)}, u32[]{:S(2)}) collective-permute-start(bf16[2,12,192]{2,1,0:T(8,128)(2,1)S(1)} %maximum_maximum_fusion.3), channel_id=1, source_target_pairs={{8,0},{16,8},{24,16},{32,24},{40,32},{48,40},{56,48},{64,56},{72,6... | collective-permute-start | bytes 27656 | tf_op jit(solution)/shard_map/ppermute | solution.py:55
  27.2 5.1 %collective-permute-start = (bf16[2,12,192]{2,1,0:T(8,128)(2,1)S(1)}, bf16[2,12,192]{2,1,0:T(8,128)(2,1)S(1)}, u32[]{:S(2)}, u32[]{:S(2)}) collective-permute-start(bf16[2,12,192]{2,1,0:T(8,128)(2,1)S(1)} %maximum_maximum_fusion.2), channel_id=1, source_target_pairs={{0,8},{8,16},{16,24},{24,32},{32,40},{40,48},{48,56},{56,64},{64,7... | collective-permute-start | bytes 27656 | tf_op jit(solution)/shard_map/ppermute | solution.py:54
  33.9 54.9 %all-to-all-start = ((bf16[8,4,72,192]{3,2,1,0:T(8,128)(2,1)}), bf16[8,4,72,192]{3,2,1,0:T(8,128)(2,1)S(1)}, u32[]{:S(2)}, u32[]{:S(2)}) async-start(bf16[8,4,72,192]{3,2,1,0:T(8,128)(2,1)} %broadcast_in_dim.39), calls=%async_computation | async-start | bytes 2359296 | tf_op jit(solution)/shard_map/all_to_all | solution.py:38
  90.1 18.7 %all-to-all-start.1 = ((bf16[8,2,72,192]{3,2,1,0:T(8,128)(2,1)}), bf16[8,2,72,192]{3,2,1,0:T(8,128)(2,1)S(1)}, u32[]{:S(2)}, u32[]{:S(2)}) async-start(bf16[8,2,72,192]{3,2,1,0:T(8,128)(2,1)} %broadcast_in_dim.75), calls=%async_computation.1 | async-start | bytes 1179648 | tf_op jit(solution)/shard_map/all_to_all | solution.py:38
  109.6 3.1 %copy-start.14 = (f32[1536]{0:T(1024)S(1)}, f32[1536]{0:T(1024)}, u32[]{:S(2)}) copy-start(f32[1536]{0:T(1024)} %param.11) | copy-start | bytes 18436
  110.0 5.5 %copy-start.6 = (f32[2,72,1536]{2,1,0:T(8,128)}, f32[2,72,1536]{2,1,0:T(8,128)S(1)}, u32[]{:S(2)}) copy-start(f32[2,72,1536]{2,1,0:T(8,128)S(1)} %reshape.182) | copy-start | bytes 2654212
  115.7 8.8 %copy-start.3 = (bf16[8,2,68,480]{3,0,2,1:T(8,128)(2,1)S(1)}, bf16[8,2,68,480]{3,0,2,1:T(8,128)(2,1)}, u32[]{:S(2)}) copy-start(bf16[8,2,68,480]{3,0,2,1:T(8,128)(2,1)} %concatenate.66) | copy-start | bytes 3133444
  115.7 8.8 %copy-start.2 = (bf16[8,2,68,480]{3,0,2,1:T(8,128)(2,1)S(1)}, bf16[8,2,68,480]{3,0,2,1:T(8,128)(2,1)}, u32[]{:S(2)}) copy-start(bf16[8,2,68,480]{3,0,2,1:T(8,128)(2,1)} %concatenate.67) | copy-start | bytes 3133444
  116.9 19.7 %all-to-all-start.2 = ((bf16[8,2,68,192]{3,1,2,0:T(2,128)(2,1)}), bf16[8,2,68,192]{3,1,2,0:T(2,128)(2,1)S(1)}, u32[]{:S(2)}, u32[]{:S(2)}) async-start(bf16[8,2,68,192]{3,1,2,0:T(2,128)(2,1)} %broadcast_in_dim.76), calls=%async_computation.2 | async-start | bytes 1114112 | tf_op jit(solution)/shard_map/all_to_all | solution.py:38
  137.3 1.6 copy-start.8
  140.4 7.3 %copy-start.13 = (f32[768]{0:T(1024)S(1)}, f32[768]{0:T(1024)}, u32[]{:S(2)}) copy-start(f32[768]{0:T(1024)} %param.15) | copy-start | bytes 9220
  140.4 23.9 %all-to-all-start.3 = ((bf16[8,4,136,96]{3,2,1,0:T(8,128)(2,1)}), bf16[8,4,136,96]{3,2,1,0:T(8,128)(2,1)S(1)}, u32[]{:S(2)}, u32[]{:S(2)}) async-start(bf16[8,4,136,96]{3,2,1,0:T(8,128)(2,1)} %broadcast_in_dim.79), calls=%async_computation.3 | async-start | bytes 2228224 | tf_op jit(solution)/shard_map/all_to_all | solution.py:38
  148.5 1.8 copy-start.5
  164.7 1.0 copy-start.1
  165.8 2.9 %copy-start = (bf16[2,768,2176]{2,1,0:T(8,128)(2,1)S(1)}, bf16[2,768,2176]{2,1,0:T(8,128)(2,1)}, u32[]{:S(2)}) copy-start(bf16[2,768,2176]{2,1,0:T(8,128)(2,1)} %all-gather.3.cloned.1.call-done) | copy-start | bytes 20054020
  173.4 14.4 %all-to-all-start.4 = ((bf16[8,2,64,192]{3,2,1,0:T(8,128)(2,1)}), bf16[8,2,64,192]{3,2,1,0:T(8,128)(2,1)S(1)}, u32[]{:S(2)}, u32[]{:S(2)}) async-start(bf16[8,2,64,192]{3,2,1,0:T(8,128)(2,1)} %get-tuple-element.8), calls=%async_computation.4 | async-start | bytes 1048576 | tf_op jit(solution)/shard_map/all_to_all | solution.py:38
  188.2 4.8 %copy-start.4 = (bf16[768,480]{1,0:T(8,128)(2,1)S(1)}, bf16[768,480]{1,0:T(8,128)(2,1)}, u32[]{:S(2)}) copy-start(bf16[768,480]{1,0:T(8,128)(2,1)} %reshape.177) | copy-start | bytes 2211844
  189.5 13.9 %all-to-all-start.5 = ((bf16[8,2,64,256]{3,2,1,0:T(8,128)(2,1)}), bf16[8,2,64,256]{3,2,1,0:T(8,128)(2,1)S(1)}, u32[]{:S(2)}, u32[]{:S(2)}) async-start(bf16[8,2,64,256]{3,2,1,0:T(8,128)(2,1)} %broadcast_in_dim.84), calls=%async_computation.5 | async-start | bytes 1048576 | tf_op jit(solution)/shard_map/all_to_all | solution.py:38
  193.0 0.9 copy-start.9
  204.1 1.5 copy-start.7
Sparse Core Ops, SparseCore 0:
  24.9 87.8 all-gather.2

commit v6 on v5

--- a/solution.py
+++ b/solution.py
@@ -66,10 +66,8 @@
     return moved.reshape(moved.shape[:2] + (-1,))
 
 
-def fine_adjoint(shared_ref, cot_ref, gain_ref, inside_ref, up_ref, conv_ref, back_ref, grad_ref, lifted_ref, norm_ref, rows_ref, taps_ref, held_ref, fetched):
+def fine_adjoint(shared_ref, cot_ref, gain_ref, inside_ref, up_ref, conv_ref, back_ref, grad_ref, lifted_ref, norm_ref, rows_ref, taps_ref):
     slab, rows = back_ref.shape[2], rows_ref.shape[1]
-    fetch = pltpu.make_async_copy(conv_ref.at[:, pl.ds(0, 1024)], held_ref, fetched)
-    fetch.start()
     for p in range(2):
         square = jnp.zeros(shared_ref.shape[2:], F32)
         for t in range(NT):
@@ -110,9 +108,8 @@
             if k < 4:
                 tail = tail + pltpu.roll(rows_ref[s, 3 - k : 3 - k + slab, 128:256], 64, 1)
             taps_ref[s * slab : (s + 1) * slab, 640 + k * 64 : 768 + k * 64] = tail.astype(BF16)
-    fetch.wait()
     for t in range(NT):
-        back = dot_t(taps_ref[...], held_ref[192 * t : 192 * (t + 1), :]).astype(BF16)
+        back = dot_t(taps_ref[...], conv_ref[192 * t : 192 * (t + 1), :]).astype(BF16)
         for s in range(2):
             back_ref[t, s] = back[s * slab : (s + 1) * slab]
 
@@ -131,7 +128,7 @@
     rows = shared.shape[2] // 2
     return pl.pallas_call(
         fine_adjoint,
-        in_specs=[whole] * 5 + [pl.BlockSpec(memory_space=pltpu.HBM)],
+        in_specs=[whole] * 6,
         out_specs=[whole] * 3,
         out_shape=[
             jax.ShapeDtypeStruct((NT, 2, slab, 192), BF16),
@@ -142,10 +139,8 @@
             pltpu.VMEM((NT,) + shared.shape[2:], F32),
             pltpu.VMEM((2, rows, 256), F32),
             pltpu.VMEM((2 * slab, 1024), BF16),
-            pltpu.VMEM((C_COARSE, 1024), BF16),
-            pltpu.SemaphoreType.DMA,
         ],
-        compiler_params=pltpu.CompilerParams(vmem_limit_bytes=40 * 2**20),
+        compiler_params=pltpu.CompilerParams(vmem_limit_bytes=18 * 2**20),
         name="fine_adjoint",
     )(shared, cot, gain, inside, up_phases, flat)
 
@@ -194,7 +189,6 @@
     )
     packed = jnp.concatenate(
         [
-            both_turned[:, :192],
             conv1_shard,
             jnp.zeros((24, 64), BF16),
             up_shard,
@@ -202,13 +196,14 @@
             out_shard,
             conv2_shard,
             both_turned[:, 384:],
-            jnp.zeros((24, 96), BF16),
+            both_turned[:, :192],
+            jnp.zeros((24, 32), BF16),
         ],
         axis=1,
     )
     paired = lax.all_gather(packed, "seq", axis=0, axis_index_groups=Y_PAIRS)
     gathered = lax.all_gather(
-        paired[:, :, 192:], "seq", axis=1, tiled=True, axis_index_groups=Z_CORES
+        paired, "seq", axis=1, tiled=True, axis_index_groups=Z_CORES
     )
     gathered = with_layout_constraint(gathered, Layout(major_to_minor=(0, 1, 2)))
     flat = gathered.reshape(C_COARSE, -1)
@@ -256,7 +251,7 @@
         [jnp.concatenate([tap(p, k) for k in range(5)], axis=-1) for p in range(2)], axis=1
     ).reshape(NT, 2 * seqs * rows, 5 * part_fine)
     out_turned = lax.all_gather(
-        paired[:, :, :192], "seq", axis=1, tiled=True, axis_index_groups=Z_CORES
+        paired[:, :, 2080:2272], "seq", axis=1, tiled=True, axis_index_groups=Z_CORES
     ).reshape(NT, part_coarse, 192)
     projected = lax.dot_general(
         trunk_blocks, out_turned, (((0, 3), (0, 2)), ((), ())), preferred_element_type=F32
@@ -292,9 +287,10 @@
         gain_fine.reshape(NT, 1, part_fine),
         inside_rows.reshape(2, seqs * rows, 1),
         up_phases,
-        flat,
+        flat[:, :1024],
         slab,
     )
+    late, back_blocks = lax.optimization_barrier((second[:, :2], back_blocks))
     third = exchange(back_blocks)
     back_coarse = jnp.sum(third.astype(F32), axis=0)
 
@@ -318,8 +314,7 @@
     trunk_grad = dot(projected_grad, out_t).astype(BF16)
 
     merged_full = (
-        second[:, :2]
-        .reshape(NT, 2, seqs, rows, part_fine)
+        late.reshape(NT, 2, seqs, rows, part_fine)
         .transpose(2, 3, 1, 0, 4)
         .reshape(seqs, fine_rows, C_FINE)
         .astype(F32)

time: 216 us -> 223 us (1.032)
  local copies, waits for them, and re-layouts: 51.3 us -> 64.5 us
  waiting for transfers between devices: 28 us -> 18.1 us
  starting transfers between devices: 48.2 us -> 53.1 us
    all_to_all x6, waiting for transfers between devices: 23 us -> 16.4 us  [exchange(): return lax.all_to_all(blocks, 'tensor', 0, 0)]
    slice x3 -> x4, local copies, waits for them, and re-layouts: 0.89 us -> 5.1 us  [the longest x1 2.19 us: per_device(): flat[:, :1024]]
    all_to_all x6, starting transfers between devices: 43.2 us -> 46.9 us  [exchange(): return lax.all_to_all(blocks, 'tensor', 0, 0)]
    ppermute x1, waiting for transfers between devices: 2.5 us -> 0.01 us  [neighbours(): before = lax.ppermute(edge(slice(-4, None), slice(-8, None)), 'seq', up)]
    unnamed x35 -> x37, local copies, waits for them, and re-layouts: 5.58 us -> 5.78 us
  transfers between devices with their start and end apart: 10 -> 10, of which waited for: 6 -> 5; matrix products, arithmetic and copies ran while one was open for 19% -> 24% of each run, Pallas kernels for 1% -> 1%
where the time goes in v6:
time: 223 us; the launch traced here: 221 us
  local copies, waits for them, and re-layouts  64.5 us (29%)
  starting transfers between devices  53.1 us (24%)
  blocking collectives  50.6 us (23%)
  waiting for transfers between devices  18.1 us (8%)
  between operations  14.6 us (7%)
  Pallas kernels  7.56 us (3%)
  matrix products  7.37 us (3%)
  other arithmetic  5.63 us (3%)
    all_to_all x6, starting transfers between devices, exchange(): return lax.all_to_all(blocks, 'tensor', 0, 0)  46.9 us
    all_gather x1, blocking collectives, per_device(): lax.all_gather(paired[:, :, 2080:2272], 'seq', axis=1, tiled=True, axis_i...  39.6 us
    all_to_all x6, waiting for transfers between devices, exchange(): return lax.all_to_all(blocks, 'tensor', 0, 0)  16.4 us
    all_gather x1, blocking collectives, per_device(): paired = lax.all_gather(packed, 'seq', axis=0, axis_index_groups=Y_PAIRS)  10.9 us
    dot_general x4, matrix products, dot(): lax.dot_general(left, right, (((left.ndim - 1,), (0,)), ((), ())), prefer...  6.97 us
    concatenate x2, local copies, waits for them, and re-layouts, per_device(): jnp.concatenate([tap(p, k) for k in range(5)], axis=-1)  6.78 us
    unnamed x37, local copies, waits for them, and re-layouts  5.78 us
    broadcast_in_dim x6, local copies, waits for them, and re-layouts, share(): return exchange(jnp.broadcast_to(piece[None], (NT,) + piece.shape))  5.39 us
  transfers between devices with their start and end apart: 10, of which 5 were waited for; matrix products, arithmetic and copies ran while one was open for 24% of the time, Pallas kernels for 1%

profile of v6, /device:TPU:32, one launch (start us, length us, event | category | flops | bytes accessed | tf_op | source)
XLA Modules:
  0.0 221.4 jit_solution(2782401090588089966)
XLA Ops:
  7.2 0.8 copy.530
  8.2 0.8 reshape.167
  9.0 0.8 maximum_maximum_fusion.1
  9.8 0.7 collective-permute-start.2
  10.4 0.8 copy_bitcast_fusion.7
  11.2 0.8 slice.259
  12.2 0.8 concatenate.62
  13.0 10.9 %all-gather = bf16[48,2304]{1,0:T(8,128)(2,1)} all-gather(bf16[24,2304]{1,0:T(8,128)(2,1)S(1)} %concatenate.62), channel_id=2, replica_groups={{0,256},{8,264},{16,272},{24,280},{32,288},{40,296},{48,304},{56,312},{..., dimensions={0}, use_global_device_ids=true | all-gather | bytes 331776 | tf_op jit(solution)/shard_map/all_gather | solution.py:204
  24.4 1.9 collective-permute-start
  26.4 3.6 %collective-permute-start.1 = (bf16[2,12,192]{2,1,0:T(8,128)(2,1)S(1)}, bf16[2,12,192]{2,1,0:T(8,128)(2,1)S(1)}, u32[]{:S(2)}, u32[]{:S(2)}) collective-permute-start(bf16[2,12,192]{2,1,0:T(8,128)(2,1)S(1)} %maximum_maximum_fusion.3), channel_id=1, source_target_pairs={{8,0},{16,8},{24,16},{32,24},{40,32},{48,40},{56,48},{64,56},{72,6... | collective-permute-start | bytes 27656 | tf_op jit(solution)/shard_map/ppermute | solution.py:55
  30.2 1.3 collective-permute-done.1
  32.0 1.2 broadcast_in_dim.39
  33.2 13.9 %all-to-all-start = ((bf16[8,4,72,192]{3,2,1,0:T(8,128)(2,1)}), bf16[8,4,72,192]{3,2,1,0:T(8,128)(2,1)S(1)}, u32[]{:S(2)}, u32[]{:S(2)}) async-start(bf16[8,4,72,192]{3,2,1,0:T(8,128)(2,1)} %broadcast_in_dim.39), calls=%async_computation | async-start | bytes 2359296 | tf_op jit(solution)/shard_map/all_to_all | solution.py:38
  47.8 0.7 maximum_convert_fusion
  48.5 0.8 slice.265
  49.3 39.6 %all_gather.14 = bf16[2,768,192]{2,1,0:T(8,128)(2,1)S(1)} all-gather(bf16[2,24,192]{2,1,0:T(8,128)(2,1)S(1)} %slice.265), channel_id=1, replica_groups={{0,8,16,24,32,40,48,56,64,72,80,88,96,104,112,120,128,136,144,152,160,1..., dimensions={1}, use_global_device_ids=true | all-gather | bytes 608256 | tf_op jit(solution)/shard_map/all_gather | solution.py:253
  89.8 0.9 broadcast_in_dim.75
  90.7 7.5 %all-to-all-start.1 = ((bf16[8,2,72,192]{3,2,1,0:T(8,128)(2,1)}), bf16[8,2,72,192]{3,2,1,0:T(8,128)(2,1)S(1)}, u32[]{:S(2)}, u32[]{:S(2)}) async-start(bf16[8,2,72,192]{3,2,1,0:T(8,128)(2,1)} %broadcast_in_dim.75), calls=%async_computation.1 | async-start | bytes 1179648 | tf_op jit(solution)/shard_map/all_to_all | solution.py:38
  98.2 2.4 %fusion.61 = (bf16[8,1,2,68,96]{4,1,3,2,0:T(2,128)(2,1)S(1)}, bf16[8,1,2,68,96]{4,1,3,2,0:T(2,128)(2,1)S(1)}, bf16[8,1,2,68,96]{4,1,3,2,0:T(2,128)(2,1)S(1)}, bf...) fusion(bf16[8,2,2,72,96]{4,1,3,2,0:T(2,128)(2,1)S(1)} %bitcast.110), kind=kLoop, calls=%fused_computation.121 | loop fusion | bytes 2506752 | tf_op jit(solution)/shard_map/slice | solution.py:248
  101.0 1.0 copy_bitcast_fusion.1
  102.0 3.5 %concatenate.66 = bf16[8,2,68,480]{3,0,2,1:T(8,128)(2,1)S(1)} concatenate(bf16[8,2,68,96]{3,0,2,1:T(8,128)(2,1)S(1)} %get-tuple-element.83, bf16[8,2,68,96]{3,0,2,1:T(8,128)(2,1)S(1)} %get-tuple-element.82, bf16[8,2,68,96]{3,0,2,1:T(8,128)(2,1)S(1)} %get-tuple-element.81, bf16[8,2,68,96]{3,0,2,1:T(8,128)(2,1)S(1)} %get-tuple-element.80, bf16[8,2,68,96]{3,0,2,1:T(8,128)(2,1)} %get-tuple-element.79), dimensions={3} | concatenate | bytes 2088960 | tf_op jit(solution)/shard_map/concatenate | solution.py:251
  105.5 3.3 %concatenate.67 = bf16[8,2,68,480]{3,0,2,1:T(8,128)(2,1)} concatenate(bf16[8,2,68,96]{3,0,2,1:T(8,128)(2,1)} %get-tuple-element.78, bf16[8,2,68,96]{3,0,2,1:T(8,128)(2,1)S(1)} %get-tuple-element.83, bf16[8,2,68,96]{3,0,2,1:T(8,128)(2,1)S(1)} %get-tuple-element.82, bf16[8,2,68,96]{3,0,2,1:T(8,128)(2,1)S(1)} %get-tuple-element.81, bf16[8,2,68,96]{3,0,2,1:T(8,128)(2,1)S(1)} %get-tuple-element.80), dimensions={3} | concatenate | bytes 2088960 | tf_op jit(solution)/shard_map/concatenate | solution.py:251
  108.8 1.2 all-to-all-done.1
  110.1 0.7 copy.531
  110.8 1.3 reshape.182
  112.7 3.1 %fusion = f32[2,72,960]{2,1,0:T(8,128)S(1)} fusion(bf16[1536,2304]{1,0:T(8,128)(2,1)} %bitcast.117, f32[2,72,1536]{2,1,0:T(8,128)} %reshape.182, f32[1536]{0:T(1024)} %param.11, f32[2,72]{1,0:T(2,128)S(1)} %get-tuple-element.75), kind=kOutput, calls=%fused_computation.1 | convolution fusion | flops 427106304 | bytes 4592192 | tf_op jit(solution)/shard_map/dot_general | solution.py:23
  116.1 1.1 broadcast_in_dim.76
  117.2 7.3 %all-to-all-start.2 = ((bf16[8,2,68,192]{3,1,2,0:T(2,128)(2,1)}), bf16[8,2,68,192]{3,1,2,0:T(2,128)(2,1)}, u32[]{:S(2)}, u32[]{:S(2)}) async-start(bf16[8,2,68,192]{3,1,2,0:T(2,128)(2,1)} %broadcast_in_dim.76), calls=%async_computation.2 | async-start | bytes 1114112 | tf_op jit(solution)/shard_map/all_to_all | solution.py:38
  124.8 2.2 copy.547.stacked_ref
  127.0 3.3 %fusion.60 = (bf16[2,768,240]{2,1,0:T(8,128)(2,1)}, bf16[2,768,240]{2,1,0:T(8,128)(2,1)S(1)}) fusion(bf16[2,768,2304]{2,1,0:T(8,128)(2,1)} %all-gather.3.cloned.1.call-done), kind=kLoop, calls=%fused_computation.120 | loop fusion | bytes 2949120 | tf_op jit(solution)/shard_map/slice | solution.py:215
  130.5 0.7 copy.546
  131.2 1.3 reshape.175.weight_ref
  132.5 3.2 %fine_back.1 = bf16[272,96]{1,0:T(8,128)(2,1)} custom-call(bf16[8,272,480]{2,1,0:T(8,128)(2,1)} %copy.547.stacked_ref, bf16[8,96,480]{2,1,0:T(8,128)(2,1)} %reshape.175.weight_ref), custom_call_target="tpu_custom_call" | custom-call | tf_op jit(solution)/shard_map/fine_back/pallas_call | solution.py:157
  135.6 0.9 copy.548
  136.6 1.2 copy.534
  138.3 1.5 fusion.21
  140.2 1.2 broadcast_in_dim.79
  141.4 7.3 %all-to-all-start.3 = ((bf16[8,4,136,96]{3,2,1,0:T(8,128)(2,1)}), bf16[8,4,136,96]{3,2,1,0:T(8,128)(2,1)}, u32[]{:S(2)}, u32[]{:S(2)}) async-start(bf16[8,4,136,96]{3,2,1,0:T(8,128)(2,1)} %broadcast_in_dim.79), calls=%async_computation.3 | async-start | bytes 2228224 | tf_op jit(solution)/shard_map/all_to_all | solution.py:38
  149.0 0.8 dynamic_slice.8
  150.3 0.9 copy.553.cot_ref
  151.2 2.5 %slice.294 = bf16[1536,192]{1,0:T(8,128)(2,1)} slice(bf16[1536,2304]{1,0:T(8,128)(2,1)} %bitcast.119), slice={[0:1536], [1216:1408]} | slice | bytes 1179648 | tf_op jit(solution)/shard_map/slice | solution.py:212
  153.7 2.2 slice.295.conv_ref
  155.9 3.1 %reshape.194 = bf16[8,192,2,96]{3,2,1,0:T(2,128)(2,1)} reshape(bf16[1536,192]{1,0:T(8,128)(2,1)} %slice.294) | data formatting | bytes 1179648 | tf_op jit(solution)/shard_map/reshape;reshape | solution.py:281
  159.0 1.3 copy.593
  160.3 1.2 pad.4.up_ref
  161.6 0.8 copy.556
  162.4 1.5 copy.557
  163.9 3.2 %reshape.179 = bf16[768,480]{1,0:T(8,128)(2,1)} reshape(bf16[2,32,12,2,240]{4,3,2,1,0:T(2,128)(2,1)} %copy.557) | data formatting | bytes 1474560 | tf_op jit(solution)/shard_map/reshape | solution.py:218
  167.1 0.7 copy.538
  167.9 2.0 slice.292
  170.0 1.0 copy-done.1
  171.1 4.4 %fine_adjoint.1 = (bf16[8,2,64,192]{3,2,1,0:T(8,128)(2,1)S(1)}, bf16[8,2,136,96]{3,2,1,0:T(8,128)(2,1)S(1)}, bf16[2,64,192]{2,1,0:T(8,128)(2,1)S(1)}) custom-call(bf16[8,4,136,96]{3,2,1,0:T(8,128)(2,1)} %all-to-all-done.3.shared_ref, bf16[8,2,136,96]{3,2,1,0:T(8,128)(2,1)S(1)} %copy-done.1, f32[8,1,96]{2,1,0:T(1,128)S(1)} %reshape.177.gain_ref, ...), custom_call_target="tpu_custom_call" | custom-call | tf_op jit(solution)/shard_map/fine_adjoint/pallas_call | solution.py:129
  175.5 0.8 copy-done.2
  176.3 0.8 copy-done.3
  177.1 7.3 %all-to-all-start.4 = ((bf16[8,2,64,192]{3,2,1,0:T(8,128)(2,1)}), bf16[8,2,64,192]{3,2,1,0:T(8,128)(2,1)S(1)}, u32[]{:S(2)}, u32[]{:S(2)}) async-start(bf16[8,2,64,192]{3,2,1,0:T(8,128)(2,1)} %copy-done.2), calls=%async_computation.4 | async-start | bytes 1048576 | tf_op jit(solution)/shard_map/all_to_all | solution.py:38
  186.3 8.4 %all-to-all-done.4 = bf16[8,2,64,192]{3,2,1,0:T(8,128)(2,1)S(1)} async-done(((bf16[8,2,64,192]{3,2,1,0:T(8,128)(2,1)}), bf16[8,2,64,192]{3,2,1,0:T(8,128)(2,1)S(1)}, u32[]{:S(2)}, u32[]{:S(2)}) %all-to-all-start.4) | async-done | bytes 393248 | tf_op jit(solution)/shard_map/all_to_all | solution.py:38
  195.6 0.9 broadcast_in_dim.84
  196.4 3.5 %all-to-all-start.5 = ((bf16[8,2,64,256]{3,2,1,0:T(8,128)(2,1)}), bf16[8,2,64,256]{3,2,1,0:T(8,128)(2,1)S(1)}, u32[]{:S(2)}, u32[]{:S(2)}) async-start(bf16[8,2,64,256]{3,2,1,0:T(8,128)(2,1)} %broadcast_in_dim.84), calls=%async_computation.5 | async-start | bytes 1048576 | tf_op jit(solution)/shard_map/all_to_all | solution.py:38
  201.0 0.7 copy.565
  201.8 0.9 constant_dynamic-slice_fusion
  202.8 0.7 copy.566
  203.5 6.8 %all-to-all-done.5 = bf16[8,2,64,256]{3,2,1,0:T(8,128)(2,1)S(1)} async-done(((bf16[8,2,64,256]{3,2,1,0:T(8,128)(2,1)}), bf16[8,2,64,256]{3,2,1,0:T(8,128)(2,1)S(1)}, u32[]{:S(2)}, u32[]{:S(2)}) %all-to-all-start.5) | async-done | bytes 524320 | tf_op jit(solution)/shard_map/all_to_all | solution.py:38
  211.7 0.8 copy-done.8
  212.5 2.1 convolution_convert_fusion
  (120 shorter events, 11.9 us)
Async XLA Ops:
  7.2 16.8 %copy-start.13 = (bf16[2,128,96]{1,2,0:T(8,128)(2,1)S(1)}, bf16[2,128,96]{1,2,0:T(8,128)(2,1)}, u32[]{:S(2)}) copy-start(bf16[2,128,96]{1,2,0:T(8,128)(2,1)} %param.14) | copy-start | bytes 147460
  7.2 16.9 %copy-start.11 = (bf16[2,128,96]{1,2,0:T(8,128)(2,1)S(1)}, bf16[2,128,96]{1,2,0:T(8,128)(2,1)}, u32[]{:S(2)}) copy-start(bf16[2,128,96]{1,2,0:T(8,128)(2,1)} %param.17) | copy-start | bytes 147460
  7.2 17.1 %copy-start.12 = (bf16[2,64,192]{2,1,0:T(8,128)(2,1)S(1)}, bf16[2,64,192]{2,1,0:T(8,128)(2,1)}, u32[]{:S(2)}) copy-start(bf16[2,64,192]{2,1,0:T(8,128)(2,1)} %param.9) | copy-start | bytes 147460
  7.2 105.5 %all-gather.3.cloned.1.call-start = ((), (), s32[]{:S(2)}) async-start(), calls=%async_computation.6 | async-start | bytes 7299072 | tf_op jit(solution)/shard_map/all_gather | solution.py:205
  9.8 2.3 %collective-permute-start.2 = (bf16[24,624]{1,0:T(8,128)(2,1)S(1)}, bf16[24,624]{1,0:T(8,128)(2,1)S(1)}, u32[]{:S(2)}, u32[]{:S(2)}) collective-permute-start(bf16[24,624]{1,0:T(8,128)(2,1)S(1)} %maximum_maximum_fusion.1), channel_id=1, source_target_pairs={{0,0},{1,64},{2,128},{3,192},{4,256},{5,320},{6,384},{7,448},{8,8}... | collective-permute-start | bytes 89864 | tf_op jit(solution)/shard_map/ppermute | solution.py:182
  24.4 5.7 %collective-permute-start = (bf16[2,12,192]{2,1,0:T(8,128)(2,1)S(1)}, bf16[2,12,192]{2,1,0:T(8,128)(2,1)S(1)}, u32[]{:S(2)}, u32[]{:S(2)}) collective-permute-start(bf16[2,12,192]{2,1,0:T(8,128)(2,1)S(1)} %maximum_maximum_fusion.2), channel_id=1, source_target_pairs={{0,8},{8,16},{16,24},{24,32},{32,40},{40,48},{48,56},{56,64},{64,7... | collective-permute-start | bytes 27656 | tf_op jit(solution)/shard_map/ppermute | solution.py:54
  26.4 5.1 %collective-permute-start.1 = (bf16[2,12,192]{2,1,0:T(8,128)(2,1)S(1)}, bf16[2,12,192]{2,1,0:T(8,128)(2,1)S(1)}, u32[]{:S(2)}, u32[]{:S(2)}) collective-permute-start(bf16[2,12,192]{2,1,0:T(8,128)(2,1)S(1)} %maximum_maximum_fusion.3), channel_id=1, source_target_pairs={{8,0},{16,8},{24,16},{32,24},{40,32},{48,40},{56,48},{64,56},{72,6... | collective-permute-start | bytes 27656 | tf_op jit(solution)/shard_map/ppermute | solution.py:55
  33.2 55.8 %all-to-all-start = ((bf16[8,4,72,192]{3,2,1,0:T(8,128)(2,1)}), bf16[8,4,72,192]{3,2,1,0:T(8,128)(2,1)S(1)}, u32[]{:S(2)}, u32[]{:S(2)}) async-start(bf16[8,4,72,192]{3,2,1,0:T(8,128)(2,1)} %broadcast_in_dim.39), calls=%async_computation | async-start | bytes 2359296 | tf_op jit(solution)/shard_map/all_to_all | solution.py:38
  90.7 19.3 %all-to-all-start.1 = ((bf16[8,2,72,192]{3,2,1,0:T(8,128)(2,1)}), bf16[8,2,72,192]{3,2,1,0:T(8,128)(2,1)S(1)}, u32[]{:S(2)}, u32[]{:S(2)}) async-start(bf16[8,2,72,192]{3,2,1,0:T(8,128)(2,1)} %broadcast_in_dim.75), calls=%async_computation.1 | async-start | bytes 1179648 | tf_op jit(solution)/shard_map/all_to_all | solution.py:38
  115.9 8.6 %copy-start.4 = (bf16[8,2,68,480]{3,0,2,1:T(8,128)(2,1)S(1)}, bf16[8,2,68,480]{3,0,2,1:T(8,128)(2,1)}, u32[]{:S(2)}) copy-start(bf16[8,2,68,480]{3,0,2,1:T(8,128)(2,1)} %concatenate.67) | copy-start | bytes 3133444
  117.2 19.4 %all-to-all-start.2 = ((bf16[8,2,68,192]{3,1,2,0:T(2,128)(2,1)}), bf16[8,2,68,192]{3,1,2,0:T(2,128)(2,1)}, u32[]{:S(2)}, u32[]{:S(2)}) async-start(bf16[8,2,68,192]{3,1,2,0:T(2,128)(2,1)} %broadcast_in_dim.76), calls=%async_computation.2 | async-start | bytes 1114112 | tf_op jit(solution)/shard_map/all_to_all | solution.py:38
  138.3 1.6 copy-start.9
  141.4 7.3 %copy-start.14 = (f32[768]{0:T(1024)S(1)}, f32[768]{0:T(1024)}, u32[]{:S(2)}) copy-start(f32[768]{0:T(1024)} %param.15) | copy-start | bytes 9220
  141.4 7.5 %copy-start.15 = (f32[68]{0:T(128)S(1)}, f32[68]{0:T(128)}, u32[]{:S(2)}) copy-start(f32[68]{0:T(128)} %get-tuple-element.77) | copy-start | bytes 820
  141.4 26.5 %all-to-all-start.3 = ((bf16[8,4,136,96]{3,2,1,0:T(8,128)(2,1)}), bf16[8,4,136,96]{3,2,1,0:T(8,128)(2,1)}, u32[]{:S(2)}, u32[]{:S(2)}) async-start(bf16[8,4,136,96]{3,2,1,0:T(8,128)(2,1)} %broadcast_in_dim.79), calls=%async_computation.3 | async-start | bytes 2228224 | tf_op jit(solution)/shard_map/all_to_all | solution.py:38
  160.3 1.2 copy-start.6
  167.9 2.1 copy-start
  170.0 1.1 copy-start.1
  175.5 0.8 copy-start.2
  176.3 0.8 copy-start.3
  177.1 7.3 %copy-start.7 = (bf16[8,2,136,96]{3,2,1,0:T(8,128)(2,1)S(1)}, bf16[8,2,136,96]{3,2,1,0:T(8,128)(2,1)}, u32[]{:S(2)}) copy-start(bf16[8,2,136,96]{3,2,1,0:T(8,128)(2,1)} %slice.292) | copy-start | bytes 1253380
  177.1 17.5 %all-to-all-start.4 = ((bf16[8,2,64,192]{3,2,1,0:T(8,128)(2,1)}), bf16[8,2,64,192]{3,2,1,0:T(8,128)(2,1)S(1)}, u32[]{:S(2)}, u32[]{:S(2)}) async-start(bf16[8,2,64,192]{3,2,1,0:T(8,128)(2,1)} %copy-done.2), calls=%async_computation.4 | async-start | bytes 1048576 | tf_op jit(solution)/shard_map/all_to_all | solution.py:38
  195.1 4.9 %copy-start.5 = (bf16[768,480]{1,0:T(8,128)(2,1)S(1)}, bf16[768,480]{1,0:T(8,128)(2,1)}, u32[]{:S(2)}) copy-start(bf16[768,480]{1,0:T(8,128)(2,1)} %reshape.179) | copy-start | bytes 2211844
  196.4 13.9 %all-to-all-start.5 = ((bf16[8,2,64,256]{3,2,1,0:T(8,128)(2,1)}), bf16[8,2,64,256]{3,2,1,0:T(8,128)(2,1)S(1)}, u32[]{:S(2)}, u32[]{:S(2)}) async-start(bf16[8,2,64,256]{3,2,1,0:T(8,128)(2,1)} %broadcast_in_dim.84), calls=%async_computation.5 | async-start | bytes 1048576 | tf_op jit(solution)/shard_map/all_to_all | solution.py:38
  199.9 0.9 copy-start.10
  211.3 1.2 copy-start.8
Sparse Core Ops, SparseCore 0:
  24.1 88.6 all-gather.2
